TPU v7x, 32 devices: a whole 2x2x4 slice. The times are simulated.
32 devices in a mesh: wide: 16 (over z, y, core), narrow: 2 (over x).
Axes of the slice: x: 2, y: 2, z: 4, core: 2. Of those that a mesh axis runs over, the one named last changes fastest.
Arguments:
- tokens: bfloat16 [32768, 768], P(('wide', 'narrow')), may hold values from -6 to 6
- init_memory: bfloat16 [64, 10, 768], P(('wide', 'narrow')), may hold values from -6 to 6
- w_query: bfloat16 [589824], P(('wide', 'narrow')), may hold values from -0.21875 to 0.21875
- w_key: bfloat16 [589824], P(('wide', 'narrow')), may hold values from -0.21875 to 0.21875
- w_value: bfloat16 [589824], P(('wide', 'narrow')), may hold values from -0.21875 to 0.21875
- w_output: bfloat16 [589824], P(('wide', 'narrow')), may hold values from -3 to 3
- w_inner: bfloat16 [2359296], P(('wide', 'narrow')), may hold values from -0.21875 to 0.21875
- w_outer: bfloat16 [2359296], P(('wide', 'narrow')), may hold values from -0.109375 to 0.109375
- vectors: bfloat16 [9216], P(('wide', 'narrow'))
- chain_start: int32 [64], P(('wide', 'narrow')), may hold values from 0 to 1, as said below
- true_count: int32 [64], P(('wide', 'narrow')), may hold values from 128 to 512, as said below
- cotangent: bfloat16 [32768, 768], P(('wide', 'narrow')), may hold values from -6 to 6
Outputs:
- mixed: bfloat16 [32768, 768], P(('wide', 'narrow'))
- grad_tokens: float32 [32768, 768], P(('wide', 'narrow'))
- grad_memory: float32 [64, 10, 768], P(('wide', 'narrow'))
- grad_query: float32 [589824], P(('wide', 'narrow'))
- grad_key: float32 [589824], P(('wide', 'narrow'))
- grad_value: float32 [589824], P(('wide', 'narrow'))
- grad_output: float32 [589824], P(('wide', 'narrow'))
- grad_inner: float32 [2359296], P(('wide', 'narrow'))
- grad_outer: float32 [2359296], P(('wide', 'narrow'))
- grad_vectors: float32 [9216], P(('wide', 'narrow'))
Inputs may be any that keep to these rules, and one draw needn't show every extreme that they name: `chain_start`: the first segment of each aligned block of 2 segments begins a chain, so no chain crosses such a block; a later segment of a block may begin a new chain or continue the chain before; segment 1 continues segment 0. `true_count`: every segment that is followed by a continuation of its chain is full; the last segment of a chain may be partly padded, and segment 64 - 1 holds exactly 128 true tokens.
All inputs are finite; a program needn't handle non-finite values.
Results may differ from a plain program's by a relative error of at most 0.014.
Values may be sent and summed in bfloat16 or wider, within the bound.
No kernel may reach another device: no remote copies, remote signals or barrier semaphores. Data moves between devices by JAX's collectives and lax.ppermute only.
A program may use at most 256 MiB of HBM per device.

v0:
```python
import math

import jax
import jax.numpy as jnp
from jax import lax
from jax.sharding import PartitionSpec as P

D = 768
HEADS = 12
HEAD_DIM = 64
FF = 3072
SEG = 512
MEM = 10


EPS = 1e-06


def shortened(value):

    def short(part):
        return part.astype(jnp.bfloat16) if part.dtype == jnp.float32 else part

    return jax.tree.map(short, value)


def layer_norm(hidden_in, gain, shift):
    average = jnp.mean(hidden_in, axis=-1, keepdims=True)
    centred = hidden_in - average
    variance = jnp.mean(centred * centred, axis=-1, keepdims=True)
    return centred * lax.rsqrt(variance + EPS) * gain + shift


def gelu_exact(pre_act):
    return jax.nn.gelu(pre_act, approximate=False)


def fetch_weights(shards):
    return jax.tree.map(
        lambda part, own: part.astype(own.dtype),
        lax.all_gather(shortened(shards), ("wide", "narrow"), axis=0, tiled=True),
        shards,
    )


def reduce_grads(grad_flat):
    return lax.psum_scatter(grad_flat, ("wide", "narrow"), scatter_dimension=0, tiled=True)


def unpack(gathered):
    matrices = (
        gathered[0].reshape(D, D),
        gathered[1].reshape(D, D),
        gathered[2].reshape(D, D),
        gathered[3].reshape(D, D),
        gathered[4].reshape(D, FF),
        gathered[5].reshape(FF, D),
    )
    vector_all = gathered[6].astype(jnp.float32)
    vector_parts = tuple((vector_all[index * D : (index + 1) * D] for index in range(8))) + (
        vector_all[8 * D :],
    )
    return (matrices, vector_parts)


def project(hidden_in, matrices, vector_parts):
    low_hidden = hidden_in.astype(jnp.bfloat16)
    queries = (
        jnp.dot(low_hidden, matrices[0], preferred_element_type=jnp.float32) + vector_parts[0]
    ).astype(jnp.bfloat16)
    key_rows = jnp.dot(low_hidden, matrices[1], preferred_element_type=jnp.float32).astype(
        jnp.bfloat16
    )
    value_rows = (
        jnp.dot(low_hidden, matrices[2], preferred_element_type=jnp.float32) + vector_parts[1]
    ).astype(jnp.bfloat16)
    row_count = hidden_in.shape[0]
    return (
        low_hidden,
        queries.reshape(row_count, HEADS, HEAD_DIM),
        key_rows.reshape(row_count, HEADS, HEAD_DIM),
        value_rows.reshape(row_count, HEADS, HEAD_DIM),
    )


def logits(head_queries, head_keys, key_ok):
    scaling = 1.0 / math.sqrt(HEAD_DIM)
    raw_scores = jnp.einsum(
        "qhd,khd->hqk", head_queries, head_keys, preferred_element_type=jnp.float32
    )
    return jnp.where(key_ok[None, None, :], raw_scores * scaling, -1e30)


def finish(hidden_in, probabilities, head_values, matrices, vector_parts):
    row_count = hidden_in.shape[0]
    attended = (
        jnp.einsum(
            "hqk,khd->qhd",
            probabilities.astype(jnp.bfloat16),
            head_values,
            preferred_element_type=jnp.float32,
        )
        .reshape(row_count, D)
        .astype(jnp.bfloat16)
    )
    branch_one = (
        jnp.dot(attended, matrices[3], preferred_element_type=jnp.float32) + vector_parts[2]
    )
    resid_one = hidden_in + branch_one
    hidden_one = layer_norm(resid_one, vector_parts[3], vector_parts[4])
    low_one = hidden_one.astype(jnp.bfloat16)
    pre_act = jnp.dot(low_one, matrices[4], preferred_element_type=jnp.float32) + vector_parts[8]
    activated = gelu_exact(pre_act).astype(jnp.bfloat16)
    branch_two = (
        jnp.dot(activated, matrices[5], preferred_element_type=jnp.float32) + vector_parts[5]
    )
    resid_two = hidden_one + branch_two
    result = layer_norm(resid_two, vector_parts[6], vector_parts[7])
    return (attended, resid_one, low_one, pre_act, activated, resid_two, result)


def backward_segment(hidden_in, key_ok, log_total, grad_result, matrices, vector_parts):
    scaling = 1.0 / math.sqrt(HEAD_DIM)
    row_count = hidden_in.shape[0]
    low_hidden, head_queries, head_keys, head_values = project(hidden_in, matrices, vector_parts)
    probabilities = jnp.exp(logits(head_queries, head_keys, key_ok) - log_total)
    attended, resid_one, low_one, pre_act, activated, resid_two, result = finish(
        hidden_in, probabilities, head_values, matrices, vector_parts
    )
    unused, norm_two_pull = jax.vjp(layer_norm, resid_two, vector_parts[6], vector_parts[7])
    grad_resid_two, grad_gain_two, grad_shift_two = norm_two_pull(grad_result)
    grad_branch_two = grad_resid_two.astype(jnp.bfloat16)
    grad_bias_outer = jnp.sum(grad_branch_two.astype(jnp.float32), axis=0)
    grad_w_outer = jnp.einsum(
        "rf,rd->fd", activated, grad_branch_two, preferred_element_type=jnp.float32
    )
    grad_activated = jnp.einsum(
        "rd,fd->rf", grad_branch_two, matrices[5], preferred_element_type=jnp.float32
    )
    unused_act, gelu_pull = jax.vjp(gelu_exact, pre_act)
    grad_pre = gelu_pull(grad_activated)[0].astype(jnp.bfloat16)
    grad_bias_inner = jnp.sum(grad_pre.astype(jnp.float32), axis=0)
    grad_w_inner = jnp.einsum("rd,rf->df", low_one, grad_pre, preferred_element_type=jnp.float32)
    grad_hidden_one = grad_resid_two + jnp.einsum(
        "rf,df->rd", grad_pre, matrices[4], preferred_element_type=jnp.float32
    )
    unused_one, norm_one_pull = jax.vjp(layer_norm, resid_one, vector_parts[3], vector_parts[4])
    grad_resid_one, grad_gain_one, grad_shift_one = norm_one_pull(grad_hidden_one)
    grad_branch_one = grad_resid_one.astype(jnp.bfloat16)
    grad_bias_output = jnp.sum(grad_branch_one.astype(jnp.float32), axis=0)
    grad_w_output = jnp.einsum(
        "rd,re->de", attended, grad_branch_one, preferred_element_type=jnp.float32
    )
    grad_attended = jnp.einsum(
        "re,de->rd", grad_branch_one, matrices[3], preferred_element_type=jnp.float32
    )
    grad_attended = grad_attended.astype(jnp.bfloat16).reshape(row_count, HEADS, HEAD_DIM)
    grad_values = (
        jnp.einsum(
            "hqk,qhd->khd",
            probabilities.astype(jnp.bfloat16),
            grad_attended,
            preferred_element_type=jnp.float32,
        )
        .astype(jnp.bfloat16)
        .reshape(row_count, D)
    )
    grad_probs = jnp.einsum(
        "qhd,khd->hqk", grad_attended, head_values, preferred_element_type=jnp.float32
    )
    grad_scores = probabilities * (
        grad_probs - jnp.sum(grad_probs * probabilities, axis=-1, keepdims=True)
    )
    grad_raw = (grad_scores * scaling).astype(jnp.bfloat16)
    grad_queries = (
        jnp.einsum("hqk,khd->qhd", grad_raw, head_keys, preferred_element_type=jnp.float32)
        .astype(jnp.bfloat16)
        .reshape(row_count, D)
    )
    grad_keys = (
        jnp.einsum("hqk,qhd->khd", grad_raw, head_queries, preferred_element_type=jnp.float32)
        .astype(jnp.bfloat16)
        .reshape(row_count, D)
    )
    grad_w_query = jnp.einsum(
        "rd,re->de", low_hidden, grad_queries, preferred_element_type=jnp.float32
    )
    grad_w_key = jnp.einsum("rd,re->de", low_hidden, grad_keys, preferred_element_type=jnp.float32)
    grad_w_value = jnp.einsum(
        "rd,re->de", low_hidden, grad_values, preferred_element_type=jnp.float32
    )
    grad_bias_query = jnp.sum(grad_queries.astype(jnp.float32), axis=0)
    grad_bias_value = jnp.sum(grad_values.astype(jnp.float32), axis=0)
    grad_hidden = grad_resid_one
    grad_hidden = grad_hidden + jnp.einsum(
        "re,de->rd", grad_queries, matrices[0], preferred_element_type=jnp.float32
    )
    grad_hidden = grad_hidden + jnp.einsum(
        "re,de->rd", grad_keys, matrices[1], preferred_element_type=jnp.float32
    )
    grad_hidden = grad_hidden + jnp.einsum(
        "re,de->rd", grad_values, matrices[2], preferred_element_type=jnp.float32
    )
    grad_vector = jnp.concatenate(
        [
            grad_bias_query,
            grad_bias_value,
            grad_bias_output,
            grad_gain_one,
            grad_shift_one,
            grad_bias_outer,
            grad_gain_two,
            grad_shift_two,
            grad_bias_inner,
        ]
    )
    return (
        grad_hidden,
        (
            grad_w_query,
            grad_w_key,
            grad_w_value,
            grad_w_output,
            grad_w_inner,
            grad_w_outer,
            grad_vector,
        ),
    )


def per_device(
    tokens,
    init_memory,
    w_query,
    w_key,
    w_value,
    w_output,
    w_inner,
    w_outer,
    vectors,
    chain_start,
    true_count,
    cotangent,
):
    shards = (w_query, w_key, w_value, w_output, w_inner, w_outer, vectors)
    matrices, vector_parts = unpack(fetch_weights(shards))
    slot_count = chain_start.shape[0]
    positions = jnp.arange(SEG, dtype=jnp.int32)
    present = (positions[None, :] < true_count[:, None]).astype(jnp.float32)
    seg_tokens = tokens.reshape(slot_count, SEG, D).astype(jnp.float32) * present[:, :, None]
    live_memory = jnp.ones((MEM,), jnp.bool_)

    def forward_step(carry, item):
        tok_rows, seg_memory, starting, valid = item
        memory = jnp.where(starting > 0, seg_memory.astype(jnp.float32), carry)
        rows_in = jnp.concatenate([memory, tok_rows, memory], axis=0)
        key_ok = jnp.concatenate([live_memory, valid > 0, live_memory])
        unused, head_queries, head_keys, head_values = project(rows_in, matrices, vector_parts)
        scores = logits(head_queries, head_keys, key_ok)
        row_max = jnp.max(scores, axis=-1, keepdims=True)
        log_total = row_max + jnp.log(jnp.sum(jnp.exp(scores - row_max), axis=-1, keepdims=True))
        probabilities = jnp.exp(scores - log_total)
        result = finish(rows_in, probabilities, head_values, matrices, vector_parts)[-1]
        return (result[MEM + SEG :], (result[MEM : MEM + SEG] * valid[:, None], memory, log_total))

    start_mem = jnp.zeros((MEM, D), jnp.float32)
    unused_carry, (token_out, memories, log_totals) = lax.scan(
        forward_step, start_mem, (seg_tokens, init_memory, chain_start, present)
    )
    mixed = token_out.reshape(slot_count * SEG, D).astype(jnp.bfloat16)
    matrices, vector_parts = unpack(fetch_weights(shards))
    seg_cotangent = cotangent.reshape(slot_count, SEG, D).astype(jnp.float32)
    zero_sums = (
        jnp.zeros((D, D), jnp.float32),
        jnp.zeros((D, D), jnp.float32),
        jnp.zeros((D, D), jnp.float32),
        jnp.zeros((D, D), jnp.float32),
        jnp.zeros((D, FF), jnp.float32),
        jnp.zeros((FF, D), jnp.float32),
        jnp.zeros((8 * D + FF,), jnp.float32),
    )

    def backward_step(carry, item):
        grad_write, sums = carry
        tok_rows, memory, starting, valid, log_total, seg_cot = item
        rows_in = jnp.concatenate([memory, tok_rows, memory], axis=0)
        key_ok = jnp.concatenate([live_memory, valid > 0, live_memory])
        grad_result = jnp.concatenate(
            [jnp.zeros((MEM, D), jnp.float32), seg_cot * valid[:, None], grad_write], axis=0
        )
        grad_hidden, seg_grads = backward_segment(
            rows_in, key_ok, log_total, grad_result, matrices, vector_parts
        )
        sums = tuple((total + piece for total, piece in zip(sums, seg_grads)))
        grad_mem = grad_hidden[:MEM] + grad_hidden[MEM + SEG :]
        grad_tok = grad_hidden[MEM : MEM + SEG] * valid[:, None]
        grad_init = jnp.where(starting > 0, grad_mem, jnp.zeros_like(grad_mem))
        passed = jnp.where(starting > 0, jnp.zeros_like(grad_mem), grad_mem)
        return ((passed, sums), (grad_tok, grad_init))

    (unused_pass, sums), (grad_toks, grad_inits) = lax.scan(
        backward_step,
        (start_mem, zero_sums),
        (seg_tokens, memories, chain_start, present, log_totals, seg_cotangent),
        reverse=True,
    )
    flat_sums = tuple((total.reshape(-1) for total in sums))
    owned = reduce_grads(flat_sums)
    return (
        mixed,
        grad_toks.reshape(slot_count * SEG, D),
        grad_inits,
        owned[0],
        owned[1],
        owned[2],
        owned[3],
        owned[4],
        owned[5],
        owned[6],
    )


def solution(mesh):
    return jax.shard_map(
        per_device,
        mesh=mesh,
        in_specs=(
            P(("wide", "narrow"), None),
            P(("wide", "narrow"), None, None),
            P(("wide", "narrow")),
            P(("wide", "narrow")),
            P(("wide", "narrow")),
            P(("wide", "narrow")),
            P(("wide", "narrow")),
            P(("wide", "narrow")),
            P(("wide", "narrow")),
            P(("wide", "narrow")),
            P(("wide", "narrow")),
            P(("wide", "narrow"), None),
        ),
        out_specs=(
            P(("wide", "narrow"), None),
            P(("wide", "narrow"), None),
            P(("wide", "narrow"), None, None),
            P(("wide", "narrow")),
            P(("wide", "narrow")),
            P(("wide", "narrow")),
            P(("wide", "narrow")),
            P(("wide", "narrow")),
            P(("wide", "narrow")),
            P(("wide", "narrow")),
        ),
        check_vma=False,
    )
```

profile of v0, /device:TPU:0, one launch (start us, length us, event | category | flops | bytes accessed | tf_op | source)
XLA Modules:
  0.0 1421.1 jit_solution(1484383626377044185)
XLA Ops:
  12.2 42.2 %all-reduce = bf16[9216]{0:T(1024)(128)(2,1)S(1)} all-reduce(bf16[9216]{0:T(1024)(128)(2,1)S(1)} %dynamic-update-slice), channel_id=1, replica_groups=mesh['wide'=16,'narrow'=2] {'wide','narrow'}, use_global_device_ids=true, to_apply=%add | all-reduce | flops 9216 | bytes 36864
  71.2 52.7 %all-gather.11.cloned.1.call-done = bf16[589824]{0:T(1024)(128)(2,1)} async-done(((bf16[18432]{0:T(1024)(128)(2,1)}), bf16[589824]{0:T(1024)(128)(2,1)}) %all-gather.11.cloned.1.call-update) | async-done | bytes 1179664 | tf_op jit(solution)/shard_map/all_gather | solution.py:41
  127.2 52.7 %all-gather.7.cloned.1.call-done = bf16[589824]{0:T(1024)(128)(2,1)} async-done(((bf16[18432]{0:T(1024)(128)(2,1)}), bf16[589824]{0:T(1024)(128)(2,1)}) %all-gather.7.cloned.1.call-update) | async-done | bytes 1179664 | tf_op jit(solution)/shard_map/all_gather | solution.py:41
  182.5 53.3 %all-gather.13.cloned.1.call-done = bf16[589824]{0:T(1024)(128)(2,1)} async-done(((bf16[18432]{0:T(1024)(128)(2,1)}), bf16[589824]{0:T(1024)(128)(2,1)}) %all-gather.13.cloned.1.call-update) | async-done | bytes 1179664 | tf_op jit(solution)/shard_map/all_gather | solution.py:41
  239.1 62.0 %all-gather.15.cloned.1.call-done = bf16[2359296]{0:T(1024)(128)(2,1)} async-done(((bf16[73728]{0:T(1024)(128)(2,1)}), bf16[2359296]{0:T(1024)(128)(2,1)}) %all-gather.15.cloned.1.call-update) | async-done | bytes 4718608 | tf_op jit(solution)/shard_map/all_gather | solution.py:41
  309.4 57.0 %all-gather.17.cloned.1.call-done = bf16[2359296]{0:T(1024)(128)(2,1)} async-done(((bf16[73728]{0:T(1024)(128)(2,1)}), bf16[2359296]{0:T(1024)(128)(2,1)}) %all-gather.17.cloned.1.call-update) | async-done | bytes 4718608 | tf_op jit(solution)/shard_map/all_gather | solution.py:41
  375.7 164.3 %while.49 = (s32[]{:T(128)}, f32[10,768]{1,0:T(8,128)S(1)}, bf16[2,512,768]{2,1,0:T(8,128)(2,1)}, f32[2,10,768]{2,1,0:T(8,128)S(1)}, f32[2,12,532,1]{2,1,3,0:T(8...) while((s32[]{:T(128)}, f32[10,768]{1,0:T(8,128)S(1)}, ...), condition=%wide.region_7.8_spmd, body=%wide.region_0.7_spmd.sunk | while | flops 8566788096 | bytes 135446352 | solution.py:267
  430.9 9.7 fusion.273
  442.9 23.1 %fusion.275 = (f32[532]{0:T(1024)S(1)}, f32[532,768]{1,0:T(8,128)S(1)}) fusion(f32[768]{0:T(1024)S(1)} %get-tuple-element.1610, bf16[3072,768]{1,0:T(8,128)(2,1)} %get-tuple-element.1609, bf16[768,3072]{1,0:T(8,128)(2,1)} %get-tuple-element.1607, f32[3072]{0:T(1024)S(1)} %get-tuple-element.1608, f32[532,768]{1,0:T(8,128)} %copy-done.23, ...), kind=kOutput, calls=%fused_computation.202.clone.1 | convolution fusion | flops 5133348352 | bytes 12733680 | tf_op jit(solution)/shard_map/while/body/eval_jaxpr/dot_general | solution.py:115
  502.1 9.7 fusion.273
  514.1 23.1 %fusion.275 = (f32[532]{0:T(1024)S(1)}, f32[532,768]{1,0:T(8,128)S(1)}) fusion(f32[768]{0:T(1024)S(1)} %get-tuple-element.1610, bf16[3072,768]{1,0:T(8,128)(2,1)} %get-tuple-element.1609, bf16[768,3072]{1,0:T(8,128)(2,1)} %get-tuple-element.1607, f32[3072]{0:T(1024)S(1)} %get-tuple-element.1608, f32[532,768]{1,0:T(8,128)} %copy-done.23, ...), kind=kOutput, calls=%fused_computation.202.clone.1 | convolution fusion | flops 5133348352 | bytes 12733680 | tf_op jit(solution)/shard_map/while/body/eval_jaxpr/dot_general | solution.py:115
  542.5 396.9 %while.50 = (s32[]{:T(128)}, f32[10,768]{1,0:T(8,128)S(1)}, f32[768,768]{1,0:T(8,128)}, f32[768,768]{1,0:T(8,128)}, f32[768,768]{1,0:T(8,128)}, /*index=5*/f32[7...) while((s32[]{:T(128)}, f32[10,768]{1,0:T(8,128)S(1)}, ...), condition=%wide.region_28.29_spmd.clone, body=%wide.region_8.28_spmd.clone.sunk | while | flops 25441777664 | bytes 574569472 | solution.py:301
  585.2 19.3 %multiply_convert_fusion.3 = (bf16[532,3072]{1,0:T(8,128)(2,1)S(1)}, f32[532,3072]{1,0:T(8,128)}, f32[532,3072]{1,0:T(8,128)}) fusion(f32[3072]{0:T(1024)S(1)} %get-tuple-element.1716, bf16[768,3072]{1,0:T(8,128)(2,1)S(1)} %bitcast.297, f32[532,768]{1,0:T(8,128)S(1)} %get-tuple-element.1502, f32[768]{0:T(1024)S(1)} %get-tuple-element.1714, ...), kind=kOutput, calls=%fused_computation.101.clone.1 | convolution fusion | flops 2620197888 | bytes 22718624 | tf_op jit(solution)/shard_map/while/body/eval_jaxpr/dot_general | solution.py:112
  610.5 10.4 convert_reduce_fusion.11
  669.4 25.4 %fusion.334 = bf16[12,64,532]{2,1,0:T(8,128)(2,1)} fusion(bf16[532,12,64]{0,2,1:T(8,128)(2,1)} %bitcast.288, f32[12,532,532]{1,2,0:T(8,128)} %copy-done, f32[12,532,532]{1,2,0:T(8,128)} %fusion.333), kind=kOutput, calls=%fused_computation.156.clone.1 | convolution fusion | flops 452121792 | bytes 28804608 | tf_op jit(solution)/shard_map/while/body/eval_jaxpr/hqk,qhd->khd/dot_general | solution.py:181
  694.8 24.2 %convert_reduce_fusion.13 = (f32[12,64]{1,0:T(8,128)}, bf16[12,64,532]{2,1,0:T(8,128)(2,1)}) fusion(bf16[532,12,64]{0,2,1:T(8,128)(2,1)} %bitcast.286, f32[12,532,532]{1,2,0:T(8,128)} %copy-done, f32[12,532,532]{1,2,0:T(8,128)} %fusion.333), kind=kOutput, calls=%fused_computation.128.clone.1 | convolution fusion | flops 452938176 | bytes 28807680 | tf_op jit(solution)/shard_map/while/body/eval_jaxpr/hqk,khd->qhd/dot_general | solution.py:176
  775.0 19.5 %multiply_convert_fusion.3 = (bf16[532,3072]{1,0:T(8,128)(2,1)S(1)}, f32[532,3072]{1,0:T(8,128)}, f32[532,3072]{1,0:T(8,128)}) fusion(f32[3072]{0:T(1024)S(1)} %get-tuple-element.1716, bf16[768,3072]{1,0:T(8,128)(2,1)S(1)} %bitcast.297, f32[532,768]{1,0:T(8,128)S(1)} %get-tuple-element.1502, f32[768]{0:T(1024)S(1)} %get-tuple-element.1714, ...), kind=kOutput, calls=%fused_computation.101.clone.1 | convolution fusion | flops 2620197888 | bytes 22718624 | tf_op jit(solution)/shard_map/while/body/eval_jaxpr/dot_general | solution.py:112
  800.6 10.2 convert_reduce_fusion.11
  865.3 25.4 %fusion.334 = bf16[12,64,532]{2,1,0:T(8,128)(2,1)} fusion(bf16[532,12,64]{0,2,1:T(8,128)(2,1)} %bitcast.288, f32[12,532,532]{1,2,0:T(8,128)} %copy-done, f32[12,532,532]{1,2,0:T(8,128)} %fusion.333), kind=kOutput, calls=%fused_computation.156.clone.1 | convolution fusion | flops 452121792 | bytes 28804608 | tf_op jit(solution)/shard_map/while/body/eval_jaxpr/hqk,qhd->khd/dot_general | solution.py:181
  890.8 24.3 %convert_reduce_fusion.13 = (f32[12,64]{1,0:T(8,128)}, bf16[12,64,532]{2,1,0:T(8,128)(2,1)}) fusion(bf16[532,12,64]{0,2,1:T(8,128)(2,1)} %bitcast.286, f32[12,532,532]{1,2,0:T(8,128)} %copy-done, f32[12,532,532]{1,2,0:T(8,128)} %fusion.333), kind=kOutput, calls=%fused_computation.128.clone.1 | convolution fusion | flops 452938176 | bytes 28807680 | tf_op jit(solution)/shard_map/while/body/eval_jaxpr/hqk,khd->qhd/dot_general | solution.py:176
  949.3 9.5 copy.75
  958.8 10.7 reshape.349
  970.3 42.0 %all-reduce.7 = f32[9216]{0:T(1024)S(1)} all-reduce(f32[9216]{0:T(1024)S(1)} %copy-done.36), channel_id=8, replica_groups=mesh['wide'=16,'narrow'=2] {'wide','narrow'}, use_global_device_ids=true, to_apply=%region_35.36.clone | all-reduce | flops 9216 | bytes 73728
  1012.9 391.7 %all-reduce.11.cloned.1.call-done = (f32[589824]{0:T(1024)}, f32[589824]{0:T(1024)}, f32[589824]{0:T(1024)}, f32[589824]{0:T(1024)}, f32[2359296]{0:T(1024)}, /*index=5*/f32[2359296]{0:T(1024)}) async-done(((f32[589824]{0:T(1024)}, f32[589824]{0:T(1024)}, f32[589824]{0:T(1024)}, f32[589824]{0:T(1024)}, f32[2359296]{0:T(1024)}, /*index=5*/f32[2359296]{0:T(1024)}), (f32[589824]{0:T(1024)}, f32[589824]{0:T(1024)}, ...) | async-done | bytes 28311568
  (544 shorter events, 370.3 us)
Async XLA Ops:
  7.2 60.7 %all-gather.9.cloned.1.call-start = ((), (), s32[]{:S(2)}) async-start(), calls=%async_computation.1 | async-start | bytes 1216512 | tf_op jit(solution)/shard_map/all_gather | solution.py:41
  7.9 116.0 %all-gather.11.cloned.1.call-start = ((), (), s32[]{:S(2)}) async-start(), calls=%async_computation.2 | async-start | bytes 1216512 | tf_op jit(solution)/shard_map/all_gather | solution.py:41
  8.7 171.3 %all-gather.7.cloned.1.call-start = ((), (), s32[]{:S(2)}) async-start(), calls=%async_computation | async-start | bytes 1216512 | tf_op jit(solution)/shard_map/all_gather | solution.py:41
  9.4 226.4 %all-gather.13.cloned.1.call-start = ((), (), s32[]{:S(2)}) async-start(), calls=%async_computation.3 | async-start | bytes 1216512 | tf_op jit(solution)/shard_map/all_gather | solution.py:41
  10.0 291.2 %all-gather.15.cloned.1.call-start = ((), (), s32[]{:S(2)}) async-start(), calls=%async_computation.4 | async-start | bytes 4866048 | tf_op jit(solution)/shard_map/all_gather | solution.py:41
  10.6 355.9 %all-gather.17.cloned.1.call-start = ((), (), s32[]{:S(2)}) async-start(), calls=%async_computation.5 | async-start | bytes 4866048 | tf_op jit(solution)/shard_map/all_gather | solution.py:41
  11.1 1393.5 %all-reduce.11.cloned.1.call-start = ((), (), s32[]{:S(2)}) async-start(), calls=%async_computation.6 | async-start | bytes 56623104
  309.4 66.3 %copy-start.70 = (s32[2]{0:T(128)S(1)}, s32[2]{0:T(128)}, u32[]{:S(2)}) copy-start(s32[2]{0:T(128)} %param.25) | copy-start | bytes 28
  550.1 31.9 %copy-start.63 = (f32[768]{0:T(1024)}, f32[768]{0:T(1024)S(1)}, u32[]{:S(2)}) copy-start(f32[768]{0:T(1024)S(1)} %get-tuple-element.1712) | copy-start | bytes 9220 | tf_op jit(solution)/shard_map/while
  550.1 35.0 %copy-start.57 = (f32[3072]{0:T(1024)}, f32[3072]{0:T(1024)S(1)}, u32[]{:S(2)}) copy-start(f32[3072]{0:T(1024)S(1)} %get-tuple-element.1716) | copy-start | bytes 36868 | tf_op jit(solution)/shard_map/while
  550.1 54.3 %copy-start.61 = (f32[768]{0:T(1024)}, f32[768]{0:T(1024)S(1)}, u32[]{:S(2)}) copy-start(f32[768]{0:T(1024)S(1)} %get-tuple-element.1714) | copy-start | bytes 9220 | tf_op jit(solution)/shard_map/while
  550.1 97.5 %copy-start.53 = (f32[768]{0:T(1024)}, f32[768]{0:T(1024)S(1)}, u32[]{:S(2)}) copy-start(f32[768]{0:T(1024)S(1)} %get-tuple-element.1713) | copy-start | bytes 9220 | tf_op jit(solution)/shard_map/while
  584.7 42.0 %copy-start.8 = (f32[532,768]{1,0:T(8,128)}, f32[532,768]{1,0:T(8,128)S(1)}, u32[]{:S(2)}) copy-start(f32[532,768]{1,0:T(8,128)S(1)} %get-tuple-element.1502) | copy-start | bytes 4902916 | tf_op jit(solution)/shard_map/while
  694.8 25.6 %copy-start.45 = (f32[9216]{0:T(1024)S(1)}, f32[9216]{0:T(1024)}, u32[]{:S(2)}) copy-start(f32[9216]{0:T(1024)} %custom-call.12) | copy-start | bytes 110596 | tf_op jit(solution)/shard_map/while
  694.8 28.0 %copy-start.50 = (f32[768]{0:T(1024)S(1)}, f32[768]{0:T(1024)}, u32[]{:S(2)}) copy-start(f32[768]{0:T(1024)} %get-tuple-element.1532) | copy-start | bytes 9220 | tf_op jit(solution)/shard_map/while
  694.8 28.7 %copy-start.34 = (f32[9216]{0:T(1024)S(1)}, f32[9216]{0:T(1024)}, u32[]{:S(2)}) copy-start(f32[9216]{0:T(1024)} %get-tuple-element.1660) | copy-start | bytes 110596 | tf_op jit(solution)/shard_map/while
  739.9 31.9 %copy-start.63 = (f32[768]{0:T(1024)}, f32[768]{0:T(1024)S(1)}, u32[]{:S(2)}) copy-start(f32[768]{0:T(1024)S(1)} %get-tuple-element.1712) | copy-start | bytes 9220 | tf_op jit(solution)/shard_map/while
  739.9 35.0 %copy-start.57 = (f32[3072]{0:T(1024)}, f32[3072]{0:T(1024)S(1)}, u32[]{:S(2)}) copy-start(f32[3072]{0:T(1024)S(1)} %get-tuple-element.1716) | copy-start | bytes 36868 | tf_op jit(solution)/shard_map/while
  739.9 54.6 %copy-start.61 = (f32[768]{0:T(1024)}, f32[768]{0:T(1024)S(1)}, u32[]{:S(2)}) copy-start(f32[768]{0:T(1024)S(1)} %get-tuple-element.1714) | copy-start | bytes 9220 | tf_op jit(solution)/shard_map/while
  739.9 100.1 %copy-start.53 = (f32[768]{0:T(1024)}, f32[768]{0:T(1024)S(1)}, u32[]{:S(2)}) copy-start(f32[768]{0:T(1024)S(1)} %get-tuple-element.1713) | copy-start | bytes 9220 | tf_op jit(solution)/shard_map/while
  774.6 42.0 %copy-start.8 = (f32[532,768]{1,0:T(8,128)}, f32[532,768]{1,0:T(8,128)S(1)}, u32[]{:S(2)}) copy-start(f32[532,768]{1,0:T(8,128)S(1)} %get-tuple-element.1502) | copy-start | bytes 4902916 | tf_op jit(solution)/shard_map/while
  890.8 25.6 %copy-start.45 = (f32[9216]{0:T(1024)S(1)}, f32[9216]{0:T(1024)}, u32[]{:S(2)}) copy-start(f32[9216]{0:T(1024)} %custom-call.12) | copy-start | bytes 110596 | tf_op jit(solution)/shard_map/while
  890.8 28.0 %copy-start.50 = (f32[768]{0:T(1024)S(1)}, f32[768]{0:T(1024)}, u32[]{:S(2)}) copy-start(f32[768]{0:T(1024)} %get-tuple-element.1532) | copy-start | bytes 9220 | tf_op jit(solution)/shard_map/while
  890.8 28.7 %copy-start.34 = (f32[9216]{0:T(1024)S(1)}, f32[9216]{0:T(1024)}, u32[]{:S(2)}) copy-start(f32[9216]{0:T(1024)} %get-tuple-element.1660) | copy-start | bytes 110596 | tf_op jit(solution)/shard_map/while
  (132 other events, 679.6 us)
Sparse Core Ops, SparseCore 0:
  10.9 56.8 all-gather.8
  70.8 53.0 all-gather.10
  126.8 53.0 all-gather.6
  182.7 53.0 all-gather.12
  238.6 62.5 all-gather.14
  303.9 62.4 all-gather.16
  969.7 434.9 all-reduce.10
where the time goes:
time: 1430 us; the launch traced here: 1420 us
  waiting for transfers between devices  679 us (47%)
  matrix products  414 us (29%)
  local copies, waits for them, and re-layouts  144 us (10%)
  blocking collectives  84.2 us (6%)
  other arithmetic  47.3 us (3%)
  loops' own time  38 us (3%)
  between operations  14.5 us (1%)
    unnamed x8, waiting for transfers between devices  395 us
    all_gather x6, waiting for transfers between devices, fetch_weights(): lax.all_gather(shortened(shards), ('wide', 'narrow'), axis=0, tiled=True)  284 us
    unnamed x2, blocking collectives  84.2 us
    dot_general x4, matrix products, finish(): jnp.dot(activated, matrices[5], preferred_element_type=jnp.float32)  53.7 us
    dot_general x2, matrix products, backward_segment(): jnp.einsum('hqk,qhd->khd', grad_raw, head_queries, preferred_element_type...  50.9 us
    dot_general x2, matrix products, backward_segment(): jnp.einsum('hqk,khd->qhd', grad_raw, head_keys, preferred_element_type=jn...  48.5 us
    dot_general x2, matrix products, finish(): jnp.dot(low_one, matrices[4], preferred_element_type=jnp.float32)  38.8 us
    while x298, local copies, waits for them, and re-layouts  28.6 us
  transfers between devices with their start and end apart: 7, of which 7 were waited for; matrix products, arithmetic and copies ran while one was open for 2% of the time, Pallas kernels for 0%

commit v1 on v0

v1 whole, which is shorter than its diff:
```python
import functools
import math

import jax
import jax.numpy as jnp
from jax import lax
from jax.experimental import pallas as pl
from jax.experimental.pallas import tpu as pltpu
from jax.sharding import PartitionSpec as P

D = 768
HEADS = 12
HEAD_DIM = 64
FF = 3072
SEG = 512
MEM = 10
EPS = 1e-06

MPAD = 16
R = SEG + MPAD
KEYS = 640
QUAD = 256
NQ = D // QUAD
BF = 512
NF = FF // BF
NEG = -1e30
EXP_SCALE = math.log2(math.e) / math.sqrt(HEAD_DIM)
F32 = jnp.float32
BF16 = jnp.bfloat16
VMEM_LIMIT = 60 * 1024 * 1024


def nt(a, b):
    return lax.dot_general(a, b, (((1,), (1,)), ((), ())), preferred_element_type=F32)


def tn(a, b):
    return lax.dot_general(a, b, (((0,), (0,)), ((), ())), preferred_element_type=F32)


def nn(a, b):
    return jnp.dot(a, b, preferred_element_type=F32)


def col_sum(v):
    return jnp.sum(v, axis=0, keepdims=True)


def row_mean(v):
    return jnp.mean(v, axis=-1, keepdims=True)


def row_ids(rows, cols):
    return lax.broadcasted_iota(jnp.int32, (rows, cols), 0)


def attn_fwd_kernel(
    count_ref, tok_ref, mem_ref, wq_ref, wk_ref, wv_ref, wo_ref, vq_ref, vec_ref,
    hb_ref, q_ref, k_ref, v_ref, o_ref, linv_ref, e_ref, xhat_ref, rstd_ref,
    h_s, k_s, v_s, acc_s,
):
    step = pl.program_id(0)
    count = count_ref[0]

    @pl.when(step == 0)
    def _():
        live = row_ids(SEG, D) < count
        h_s[0:SEG, :] = jnp.where(live, tok_ref[...].astype(F32), 0.0)
        h_s[SEG:R, :] = mem_ref[...]
        hb_ref[...] = h_s[...].astype(BF16)
        k_s[R:KEYS, :] = jnp.zeros((KEYS - R, QUAD), BF16)
        v_s[R:KEYS, :] = jnp.zeros((KEYS - R, QUAD), BF16)

    hb = hb_ref[...]
    q4 = (nn(hb, wq_ref[...]) + vq_ref[0:1, :]).astype(BF16)
    k4 = nn(hb, wk_ref[...]).astype(BF16)
    v4 = (nn(hb, wv_ref[...]) + vq_ref[1:2, :]).astype(BF16)
    q_ref[...] = q4
    k_ref[...] = k4
    v_ref[...] = v4
    k_s[0:R, :] = k4
    v_s[0:R, :] = v4
    key = lax.broadcasted_iota(jnp.int32, (1, KEYS), 1)
    bias = jnp.where(key < count, 0.0, NEG)
    twice = math.log(2.0) * math.sqrt(HEAD_DIM)
    bias = jnp.where((key >= SEG) & (key < SEG + MEM), twice, bias)
    first = lax.broadcasted_iota(jnp.int32, (1, 128), 1) < HEAD_DIM
    one = jnp.ones((KEYS, 128), BF16)
    for pair in range(2):
        lanes = slice(128 * pair, 128 * pair + 128)
        q2 = q4[:, lanes]
        k2 = k_s[:, lanes]
        vx = jnp.concatenate([v_s[:, lanes], one], axis=1)
        outs = []
        for half in range(2):
            mine = first if half == 0 else jnp.logical_not(first)
            qh = jnp.where(mine, q2, jnp.zeros_like(q2))
            s = nt(qh, k2) + bias
            top = jnp.max(s, axis=-1, keepdims=True)
            e = jnp.exp2((s - top) * EXP_SCALE).astype(BF16)
            e_ref[2 * pair + half] = e
            outs.append(nn(e, vx))
        num = jnp.where(first, outs[0][:, :128], outs[1][:, :128])
        den = jnp.where(first, outs[0][:, 128:], outs[1][:, 128:])
        inv = 1.0 / den
        linv_ref[:, lanes] = inv
        o_ref[:, lanes] = (num * inv).astype(BF16)
    part = nn(o_ref[...], wo_ref[...])

    @pl.when(step == 0)
    def _():
        acc_s[...] = part

    @pl.when(step > 0)
    def _():
        acc_s[...] = acc_s[...] + part

    @pl.when(step == NQ - 1)
    def _():
        r = h_s[...] + (acc_s[...] + vec_ref[2:3, :])
        c = r - row_mean(r)
        rstd = lax.rsqrt(row_mean(c * c) + EPS)
        xhat_ref[...] = c * rstd
        rstd_ref[...] = jnp.broadcast_to(rstd, (R, 128))


def const(shape):
    return pl.BlockSpec(shape, lambda j, *_: (0,) * len(shape))


def cols(rows, width):
    return pl.BlockSpec((rows, width), lambda j, *_: (0, j))


def rows(height, width):
    return pl.BlockSpec((height, width), lambda j, *_: (j, 0))


def sds(shape, dtype):
    return jax.ShapeDtypeStruct(shape, dtype)


def params():
    return pltpu.CompilerParams(
        dimension_semantics=("arbitrary",), vmem_limit_bytes=VMEM_LIMIT
    )


def attn_fwd(count, tok, mem, wq, wk, wv, wo, vecs):
    return pl.pallas_call(
        attn_fwd_kernel,
        grid_spec=pltpu.PrefetchScalarGridSpec(
            num_scalar_prefetch=1,
            grid=(NQ,),
            in_specs=[
                const((SEG, D)), const((MPAD, D)),
                cols(D, QUAD), cols(D, QUAD), cols(D, QUAD), rows(QUAD, D),
                cols(8, QUAD), const((8, D)),
            ],
            out_specs=[
                const((R, D)), cols(R, QUAD), cols(R, QUAD), cols(R, QUAD), cols(R, QUAD),
                cols(R, QUAD),
                pl.BlockSpec((4, R, KEYS), lambda j, *_: (j, 0, 0)),
                const((R, D)), const((R, 128)),
            ],
            scratch_shapes=[
                pltpu.VMEM((R, D), F32), pltpu.VMEM((KEYS, QUAD), BF16),
                pltpu.VMEM((KEYS, QUAD), BF16), pltpu.VMEM((R, D), F32),
            ],
        ),
        out_shape=[
            sds((R, D), BF16), sds((R, D), BF16), sds((R, D), BF16), sds((R, D), BF16),
            sds((R, D), BF16), sds((R, D), F32), sds((HEADS, R, KEYS), BF16),
            sds((R, D), F32), sds((R, 128), F32),
        ],
        compiler_params=params(),
        name="attn_fwd",
    )(count, tok, mem, wq, wk, wv, wo, vecs, vecs)


def ffn_fwd_kernel(
    count_ref, xhat_ref, wi_ref, bi_ref, wo_ref, vec_ref,
    h1b_ref, g_ref, gp_ref, mixed_ref, write_ref, xhat2_ref, rstd2_ref,
    acc_s,
):
    step = pl.program_id(0)

    @pl.when(step == 0)
    def _():
        h1b_ref[...] = (xhat_ref[...] * vec_ref[3:4, :] + vec_ref[4:5, :]).astype(BF16)

    f1 = nn(h1b_ref[...], wi_ref[...]) + bi_ref[...]
    cdf = 0.5 * (1.0 + lax.erf(f1 * math.sqrt(0.5)))
    pdf = jnp.exp(-0.5 * f1 * f1) * (1.0 / math.sqrt(2.0 * math.pi))
    g = (f1 * cdf).astype(BF16)
    g_ref[...] = g
    gp_ref[...] = (cdf + f1 * pdf).astype(BF16)
    part = nn(g, wo_ref[...])

    @pl.when(step == 0)
    def _():
        acc_s[...] = part

    @pl.when(step > 0)
    def _():
        acc_s[...] = acc_s[...] + part

    @pl.when(step == NF - 1)
    def _():
        h1 = xhat_ref[...] * vec_ref[3:4, :] + vec_ref[4:5, :]
        r = h1 + (acc_s[...] + vec_ref[5:6, :])
        c = r - row_mean(r)
        rstd = lax.rsqrt(row_mean(c * c) + EPS)
        xhat = c * rstd
        xhat2_ref[...] = xhat
        rstd2_ref[...] = jnp.broadcast_to(rstd, (R, 128))
        y = xhat * vec_ref[6:7, :] + vec_ref[7:8, :]
        live = row_ids(SEG, D) < count_ref[0]
        mixed_ref[...] = jnp.where(live, y[0:SEG, :], 0.0).astype(BF16)
        write_ref[...] = jnp.where(row_ids(MPAD, D) < MEM, y[SEG:R, :], 0.0)


def ffn_fwd(count, xhat, wi, bi, wo, vecs):
    return pl.pallas_call(
        ffn_fwd_kernel,
        grid_spec=pltpu.PrefetchScalarGridSpec(
            num_scalar_prefetch=1,
            grid=(NF,),
            in_specs=[const((R, D)), cols(D, BF), cols(1, BF), rows(BF, D), const((8, D))],
            out_specs=[
                const((R, D)), cols(R, BF), cols(R, BF), const((SEG, D)), const((MPAD, D)),
                const((R, D)), const((R, 128)),
            ],
            scratch_shapes=[pltpu.VMEM((R, D), F32)],
        ),
        out_shape=[
            sds((R, D), BF16), sds((R, FF), BF16), sds((R, FF), BF16), sds((SEG, D), BF16),
            sds((MPAD, D), F32), sds((R, D), F32), sds((R, 128), F32),
        ],
        compiler_params=params(),
        name="ffn_fwd",
    )(count, xhat, wi, bi, wo, vecs)


def norm_pull(grad, gain, xhat, rstd):
    gx = grad * gain
    return rstd * (gx - row_mean(gx) - xhat * row_mean(gx * xhat))


def ffn_bwd_kernel(
    count_ref, cot_ref, gw_ref, xhat2_ref, rstd2_ref, xhat_ref, rstd_ref, wi_ref, wo_ref,
    gp_ref, vec_ref,
    df2_ref, df1_ref, dr1_ref, dr1b_ref, dbi_ref, dvec_ref,
    acc_s,
):
    step = pl.program_id(0)

    @pl.when(step == 0)
    def _():
        live = row_ids(SEG, D) < count_ref[0]
        acc_s[0:SEG, :] = jnp.where(live, cot_ref[...].astype(F32), 0.0)
        acc_s[SEG:R, :] = gw_ref[...]
        dy = acc_s[...]
        xhat2 = xhat2_ref[...]
        dvec_ref[6:7, :] = col_sum(dy * xhat2)
        dvec_ref[7:8, :] = col_sum(dy)
        dr2 = norm_pull(dy, vec_ref[6:7, :], xhat2, rstd2_ref[:, 0:1])
        df2 = dr2.astype(BF16)
        df2_ref[...] = df2
        dvec_ref[5:6, :] = col_sum(df2.astype(F32))
        acc_s[...] = dr2

    df1 = (nt(df2_ref[...], wo_ref[...]) * gp_ref[...].astype(F32)).astype(BF16)
    df1_ref[...] = df1
    dbi_ref[...] = col_sum(df1.astype(F32))
    acc_s[...] = acc_s[...] + nt(df1, wi_ref[...])

    @pl.when(step == NF - 1)
    def _():
        dh1 = acc_s[...]
        xhat = xhat_ref[...]
        dvec_ref[3:4, :] = col_sum(dh1 * xhat)
        dvec_ref[4:5, :] = col_sum(dh1)
        dr1 = norm_pull(dh1, vec_ref[3:4, :], xhat, rstd_ref[:, 0:1])
        dr1_ref[...] = dr1
        dr1b = dr1.astype(BF16)
        dr1b_ref[...] = dr1b
        dvec_ref[2:3, :] = col_sum(dr1b.astype(F32))
        dvec_ref[0:2, :] = jnp.zeros((2, D), F32)


def ffn_bwd(count, cot, gw, xhat2, rstd2, xhat, rstd, wi, wo, gp, vecs):
    return pl.pallas_call(
        ffn_bwd_kernel,
        grid_spec=pltpu.PrefetchScalarGridSpec(
            num_scalar_prefetch=1,
            grid=(NF,),
            in_specs=[
                const((SEG, D)), const((MPAD, D)), const((R, D)), const((R, 128)),
                const((R, D)), const((R, 128)), cols(D, BF), rows(BF, D), cols(R, BF),
                const((8, D)),
            ],
            out_specs=[
                const((R, D)), cols(R, BF), const((R, D)), const((R, D)), cols(1, BF),
                const((8, D)),
            ],
            scratch_shapes=[pltpu.VMEM((R, D), F32)],
        ),
        out_shape=[
            sds((R, D), BF16), sds((R, FF), BF16), sds((R, D), F32), sds((R, D), BF16),
            sds((1, FF), F32), sds((8, D), F32),
        ],
        compiler_params=params(),
        name="ffn_bwd",
    )(count, cot, gw, xhat2, rstd2, xhat, rstd, wi, wo, gp, vecs)


def attn_bwd_kernel(
    count_ref, dr1_ref, dr1b_ref, wq_ref, wk_ref, wv_ref, wo_ref, q_ref, k_ref, v_ref, o_ref,
    linv_ref, e_ref,
    dq_ref, dk_ref, dv_ref, dqb_ref, dvb_ref, gtok_ref, gmem_ref,
    k_s, v_s, acc_s,
):
    step = pl.program_id(0)

    @pl.when(step == 0)
    def _():
        k_s[R:KEYS, :] = jnp.zeros((KEYS - R, QUAD), BF16)
        v_s[R:KEYS, :] = jnp.zeros((KEYS - R, QUAD), BF16)
        acc_s[...] = dr1_ref[...]

    k_s[0:R, :] = k_ref[...]
    v_s[0:R, :] = v_ref[...]
    grad_o = nt(dr1b_ref[...], wo_ref[...]).astype(BF16).astype(F32) * linv_ref[...]
    grad_ob = grad_o.astype(BF16)
    term = (-(grad_o * o_ref[...].astype(F32))).astype(BF16)
    first = lax.broadcasted_iota(jnp.int32, (1, 128), 1) < HEAD_DIM
    one = jnp.ones((KEYS, 128), BF16)
    scaling = 1.0 / math.sqrt(HEAD_DIM)
    for pair in range(2):
        lanes = slice(128 * pair, 128 * pair + 128)
        q2 = q_ref[:, lanes]
        k2 = k_s[:, lanes]
        do2 = grad_ob[:, lanes]
        tm2 = term[:, lanes]
        vx = jnp.concatenate([v_s[:, lanes], one], axis=1)
        dqs, dks, dvs = [], [], []
        for half in range(2):
            mine = first if half == 0 else jnp.logical_not(first)
            zero = jnp.zeros_like(do2)
            lhs = jnp.concatenate([jnp.where(mine, do2, zero), jnp.where(mine, tm2, zero)], axis=1)
            e = e_ref[2 * pair + half]
            ds = (nt(lhs, vx) * e.astype(F32)).astype(BF16)
            dqs.append(nn(ds, k2))
            dks.append(tn(ds, q2))
            dvs.append(tn(e, do2))
        dq_ref[:, lanes] = (jnp.where(first, dqs[0], dqs[1]) * scaling).astype(BF16)
        dk_ref[:, lanes] = (jnp.where(first, dks[0], dks[1])[0:R, :] * scaling).astype(BF16)
        dv_ref[:, lanes] = jnp.where(first, dvs[0], dvs[1])[0:R, :].astype(BF16)
    dq = dq_ref[...]
    dv = dv_ref[...]
    dqb_ref[...] = col_sum(dq.astype(F32))
    dvb_ref[...] = col_sum(dv.astype(F32))
    part = nt(dq, wq_ref[...]) + nt(dk_ref[...], wk_ref[...]) + nt(dv, wv_ref[...])
    acc_s[...] = acc_s[...] + part

    @pl.when(step == NQ - 1)
    def _():
        live = row_ids(SEG, D) < count_ref[0]
        gtok_ref[...] = jnp.where(live, acc_s[0:SEG, :], 0.0)
        gmem_ref[...] = jnp.where(row_ids(MPAD, D) < MEM, acc_s[SEG:R, :], 0.0)


def attn_bwd(count, dr1, dr1b, wq, wk, wv, wo, q, k, v, o, linv, e):
    return pl.pallas_call(
        attn_bwd_kernel,
        grid_spec=pltpu.PrefetchScalarGridSpec(
            num_scalar_prefetch=1,
            grid=(NQ,),
            in_specs=[
                const((R, D)), const((R, D)),
                cols(D, QUAD), cols(D, QUAD), cols(D, QUAD), rows(QUAD, D),
                cols(R, QUAD), cols(R, QUAD), cols(R, QUAD), cols(R, QUAD), cols(R, QUAD),
                pl.BlockSpec((4, R, KEYS), lambda j, *_: (j, 0, 0)),
            ],
            out_specs=[
                cols(R, QUAD), cols(R, QUAD), cols(R, QUAD), cols(1, QUAD), cols(1, QUAD),
                const((SEG, D)), const((MPAD, D)),
            ],
            scratch_shapes=[
                pltpu.VMEM((KEYS, QUAD), BF16), pltpu.VMEM((KEYS, QUAD), BF16),
                pltpu.VMEM((R, D), F32),
            ],
        ),
        out_shape=[
            sds((R, D), BF16), sds((R, D), BF16), sds((R, D), BF16), sds((1, D), F32),
            sds((1, D), F32), sds((SEG, D), F32), sds((MPAD, D), F32),
        ],
        compiler_params=params(),
        name="attn_bwd",
    )(count, dr1, dr1b, wq, wk, wv, wo, q, k, v, o, linv, e)


AXES = ("wide", "narrow")


def wgrad(left, grad):
    return tn(left, grad).astype(BF16)


def per_device(
    tokens, init_memory, w_query, w_key, w_value, w_output, w_inner, w_outer, vectors,
    chain_start, true_count, cotangent,
):
    slots = chain_start.shape[0]
    parts = D * D // w_query.shape[0]
    own = D // parts
    row = jnp.pad(vectors, (0, 8 * D - vectors.shape[0])).reshape(8, D)
    local_attn = jnp.concatenate(
        [w.reshape(own, D) for w in (w_query, w_key, w_value, w_output)] + [row], axis=0
    )
    attn_all = lax.all_gather(local_attn, AXES, axis=0, tiled=False)
    local_ffn = jnp.concatenate(
        [w_inner.reshape(own, FF)[:, D * i : D * i + D] for i in range(FF // D)]
        + [w_outer.reshape(4 * own, D)],
        axis=0,
    )
    ffn_all = lax.all_gather(local_ffn, AXES, axis=0, tiled=False)
    wq, wk, wv, wo = (
        attn_all[:, own * i : own * i + own].reshape(D, D) for i in range(4)
    )
    vec_all = attn_all[:, 4 * own].reshape(parts, D)[:, : vectors.shape[0]].reshape(-1)
    vec_all = vec_all.astype(F32)
    vecs = vec_all[: 8 * D].reshape(8, D)
    bi = vec_all[8 * D :].reshape(1, FF)
    wi = jnp.concatenate(
        [ffn_all[:, own * i : own * i + own].reshape(D, D) for i in range(FF // D)], axis=1
    )
    wu = ffn_all[:, 4 * own :].reshape(FF, D)

    tok = tokens.reshape(slots, SEG, D)
    cot = cotangent.reshape(slots, SEG, D)
    init = jnp.pad(init_memory.astype(F32), ((0, 0), (0, MPAD - MEM), (0, 0)))
    carry = jnp.zeros((MPAD, D), F32)
    saved, mixed = [], []
    for s in range(slots):
        count = true_count[s : s + 1]
        memory = jnp.where(chain_start[s] > 0, init[s], carry)
        a = attn_fwd(count, tok[s], memory, wq, wk, wv, wo, vecs)
        f = ffn_fwd(count, a[7], wi, bi, wu, vecs)
        carry = f[4]
        mixed.append(f[3])
        saved.append((a, f))
    back = jnp.zeros((MPAD, D), F32)
    done = [None] * slots
    for s in reversed(range(slots)):
        count = true_count[s : s + 1]
        hb, q, k, v, o, linv, e, xhat, rstd = saved[s][0]
        h1b, g, gp, _, _, xhat2, rstd2 = saved[s][1]
        df2, df1, dr1, dr1b, dbi, dvec = ffn_bwd(
            count, cot[s], back, xhat2, rstd2, xhat, rstd, wi, wu, gp, vecs
        )
        dq, dk, dv, dqb, dvb, gtok, gmem = attn_bwd(
            count, dr1, dr1b, wq, wk, wv, wo, q, k, v, o, linv, e
        )
        starts = chain_start[s] > 0
        ginit = jnp.where(starts, gmem, 0.0)[:MEM]
        back = jnp.where(starts, 0.0, gmem)
        vec = jnp.concatenate([dqb, dvb, dvec[2:8]], axis=0).reshape(-1)
        vec = jnp.concatenate([vec, dbi.reshape(-1)])
        done[s] = (hb, o, h1b, g, df2, df1, dr1b, dq, dk, dv, gtok, ginit, vec)

    def both(i):
        return jnp.concatenate([d[i] for d in done], axis=0)

    hb, o, h1b, g, df2, df1, dr1b, dq, dk, dv = (both(i) for i in range(10))
    vec = sum(d[12] for d in done)
    g_inner = wgrad(h1b, df1).reshape(parts, own, FF)
    g_outer = wgrad(g, df2).reshape(parts, 4 * own, D)
    flat_ffn = jnp.concatenate(
        [g_inner[:, :, D * i : D * i + D] for i in range(FF // D)] + [g_outer], axis=1
    )
    ffn_mine = lax.psum_scatter(flat_ffn, AXES, scatter_dimension=0, tiled=False)
    squares = [wgrad(hb, dq), wgrad(hb, dk), wgrad(hb, dv), wgrad(o, dr1b)]
    flat_attn = jnp.concatenate([w.reshape(parts, own, D) for w in squares], axis=1)
    attn_mine = lax.psum_scatter(flat_attn, AXES, scatter_dimension=0, tiled=False)
    vec_mine = lax.psum_scatter(vec, AXES, scatter_dimension=0, tiled=True)
    inner_mine = jnp.concatenate(
        [ffn_mine[own * i : own * i + own] for i in range(FF // D)], axis=1
    )
    return (
        jnp.concatenate(mixed, axis=0),
        both(10),
        jnp.stack([d[11] for d in done]),
        *(attn_mine[own * i : own * i + own].reshape(-1).astype(F32) for i in range(4)),
        inner_mine.reshape(-1).astype(F32),
        ffn_mine[4 * own :].reshape(-1).astype(F32),
        vec_mine,
    )


def solution(mesh):
    flat = P(AXES)
    return jax.shard_map(
        per_device,
        mesh=mesh,
        in_specs=(P(AXES, None), P(AXES, None, None)) + (flat,) * 9 + (P(AXES, None),),
        out_specs=(P(AXES, None), P(AXES, None), P(AXES, None, None)) + (flat,) * 7,
        check_vma=False,
    )
```

time: 1430 us -> 585 us (0.41)
  waiting for transfers between devices: 679 us -> 285 us
  matrix products: 414 us -> 24.8 us
  Pallas kernels: 0 us -> 142 us
  local copies, waits for them, and re-layouts: 144 us -> 49.7 us
  blocking collectives: 84.2 us -> 39.8 us
  loops' own time: 38 us -> 0 us
  other arithmetic: 47.3 us -> 16.1 us
    unnamed x8 -> x4, waiting for transfers between devices: 395 us -> 0.07 us
    dot_general x62 -> x6, matrix products: 414 us -> 24.8 us  [tn(): lax.dot_general(a, b, (((0,), (0,)), ((), ())), preferred_element_type=F32)]
    reduce_scatter x0 -> x2, waiting for transfers between devices: none -> 172 us  [the longest x1 138 us: per_device(): lax.psum_scatter(flat_ffn, AXES, scatter_dimension=0, tiled=False)]
    all_gather x6 -> x2, waiting for transfers between devices: 284 us -> 113 us  [the longest x1 58.5 us: per_device(): ffn_all = lax.all_gather(local_ffn, AXES, axis=0, tiled=False)]
    pallas_call x0 -> x8, Pallas kernels: none -> 142 us  [the longest x2 43.3 us: attn_bwd(): pl.pallas_call(attn_bwd_kernel, grid_spec=pltpu.PrefetchScalarGridSpec(nu...]
    reshape x11 -> x9, local copies, waits for them, and re-layouts: 50.7 us -> 5.52 us  [the longest x4 3.44 us: per_device(): w.reshape(own, D)]
    unnamed x2 -> x1, blocking collectives: 84.2 us -> 39.8 us
    another operation x2 -> x0, loops' own time: 38 us -> none  [the longest x1 23.4 us: per_device(): lax.scan(forward_step, start_mem, (seg_tokens, init_memory, chain_start,...]
  transfers between devices with their start and end apart: 7 -> 4, of which waited for: 7 -> 4; matrix products, arithmetic and copies ran while one was open for 2% -> 9% of each run, Pallas kernels for 0% -> 3%
where the time goes in v1:
time: 585 us; the launch traced here: 574 us
  waiting for transfers between devices  285 us (49%)
  Pallas kernels  142 us (24%)
  local copies, waits for them, and re-layouts  49.7 us (8%)
  blocking collectives  39.8 us (7%)
  matrix products  24.8 us (4%)
  other arithmetic  16.1 us (3%)
  between operations  15.8 us (3%)
    reduce_scatter x1, waiting for transfers between devices, per_device(): lax.psum_scatter(flat_ffn, AXES, scatter_dimension=0, tiled=False)  138 us
    all_gather x1, waiting for transfers between devices, per_device(): ffn_all = lax.all_gather(local_ffn, AXES, axis=0, tiled=False)  58.5 us
    all_gather x1, waiting for transfers between devices, per_device(): attn_all = lax.all_gather(local_attn, AXES, axis=0, tiled=False)  54.5 us
    pallas_call x2, Pallas kernels, attn_bwd(): pl.pallas_call(attn_bwd_kernel, grid_spec=pltpu.PrefetchScalarGridSpec(nu...  43.3 us
    unnamed x1, blocking collectives  39.8 us
    pallas_call x2, Pallas kernels, attn_fwd(): pl.pallas_call(attn_fwd_kernel, grid_spec=pltpu.PrefetchScalarGridSpec(nu...  35.4 us
    reduce_scatter x1, waiting for transfers between devices, per_device(): lax.psum_scatter(flat_attn, AXES, scatter_dimension=0, tiled=False)  33.8 us
    pallas_call x2, Pallas kernels, ffn_bwd(): pl.pallas_call(ffn_bwd_kernel, grid_spec=pltpu.PrefetchScalarGridSpec(num...  33.1 us
  transfers between devices with their start and end apart: 4, of which 4 were waited for; matrix products, arithmetic and copies ran while one was open for 9% of the time, Pallas kernels for 3%

profile of v1, /device:TPU:0, one launch (start us, length us, event | category | flops | bytes accessed | tf_op | source)
XLA Modules:
  0.0 573.5 jit_solution(6965501027019737193)
XLA Ops:
  25.4 54.5 %all-gather.5.cloned.1.call-done = bf16[3328,768]{1,0:T(8,128)(2,1)} async-done(((bf16[104,768]{1,0:T(8,128)(2,1)}), bf16[3328,768]{1,0:T(8,128)(2,1)}) %all-gather.5.cloned.1.call-update) | async-done | bytes 5111824 | tf_op jit(solution)/shard_map/all_gather | solution.py:422
  81.8 4.6 fusion.64
  86.4 17.6 %attn_fwd.2 = (bf16[528,768]{1,0:T(8,128)(2,1)}, bf16[528,768]{1,0:T(8,128)(2,1)}, bf16[528,768]{1,0:T(8,128)(2,1)}, bf16[528,768]{1,0:T(8,128)(2,1)}, bf16[528,...) custom-call(s32[1]{0:T(128)} %get-tuple-element.186.count_ref, ...), custom_call_target="tpu_custom_call" | custom-call | tf_op jit(solution)/shard_map/attn_fwd/pallas_call | solution.py:150
  105.9 58.5 %all-gather.7.cloned.1.call-done = bf16[6144,768]{1,0:T(8,128)(2,1)} async-done(((bf16[192,768]{1,0:T(8,128)(2,1)}), bf16[6144,768]{1,0:T(8,128)(2,1)}) %all-gather.7.cloned.1.call-update) | async-done | bytes 9437200 | tf_op jit(solution)/shard_map/all_gather | solution.py:428
  164.3 2.8 fusion.63
  169.4 2.6 slice.228
  172.1 2.5 pad_maximum_fusion.wi_ref
  174.5 15.2 %ffn_fwd.2 = (bf16[528,768]{1,0:T(8,128)(2,1)}, bf16[528,3072]{1,0:T(8,128)(2,1)}, bf16[528,3072]{1,0:T(8,128)(2,1)}, bf16[512,768]{1,0:T(8,128)(2,1)}, f32[16,7...) custom-call(s32[1]{0:T(128)} %get-tuple-element.186.count_ref, f32[528,768]{1,0:T(8,128)} %get-tuple-element.67.xhat_ref, ...), custom_call_target="tpu_custom_call" | custom-call | tf_op jit(solution)/shard_map/ffn_fwd/pallas_call | solution.py:224
  191.2 17.8 %attn_fwd.3 = (bf16[528,768]{1,0:T(8,128)(2,1)}, bf16[528,768]{1,0:T(8,128)(2,1)}, bf16[528,768]{1,0:T(8,128)(2,1)}, bf16[528,768]{1,0:T(8,128)(2,1)}, bf16[528,...) custom-call(s32[1]{0:T(128)} %get-tuple-element.187.count_ref, ...), custom_call_target="tpu_custom_call" | custom-call | tf_op jit(solution)/shard_map/attn_fwd/pallas_call | solution.py:150
  208.9 15.4 %ffn_fwd.3 = (bf16[528,768]{1,0:T(8,128)(2,1)}, bf16[528,3072]{1,0:T(8,128)(2,1)}, bf16[528,3072]{1,0:T(8,128)(2,1)}, bf16[512,768]{1,0:T(8,128)(2,1)}, f32[16,7...) custom-call(s32[1]{0:T(128)} %get-tuple-element.187.count_ref, f32[528,768]{1,0:T(8,128)} %get-tuple-element.70.xhat_ref, ...), custom_call_target="tpu_custom_call" | custom-call | tf_op jit(solution)/shard_map/ffn_fwd/pallas_call | solution.py:224
  224.9 16.3 %ffn_bwd.2 = (bf16[528,768]{1,0:T(8,128)(2,1)}, bf16[528,3072]{1,0:T(8,128)(2,1)}, f32[528,768]{1,0:T(8,128)}, bf16[528,768]{1,0:T(8,128)(2,1)}, f32[1,3072]{1,0:T(1,128)}, /*index=5*/f32[8,768]{1,0:T(8,128)}) custom-call(s32[1]{0:T(128)} %get-tuple-element.187.count_ref, bf16[512,768]{1,0:T(8,128)(2,1)} %get-tuple-element.173.cot_ref, ...), custom_call_target="tpu_custom_call" | custom-call | tf_op jit(solution)/shard_map/ffn_bwd/pallas_call | solution.py:293
  241.3 21.5 %attn_bwd.2 = (bf16[528,768]{1,0:T(8,128)(2,1)}, bf16[528,768]{1,0:T(8,128)(2,1)}, bf16[528,768]{1,0:T(8,128)(2,1)}, f32[1,768]{1,0:T(1,128)}, f32[1,768]{1,0:T(...) custom-call(s32[1]{0:T(128)} %get-tuple-element.187.count_ref, f32[528,768]{1,0:T(8,128)} %get-tuple-element.76.dr1_ref, ...), custom_call_target="tpu_custom_call" | custom-call | tf_op jit(solution)/shard_map/attn_bwd/pallas_call | solution.py:375
  265.5 16.8 %ffn_bwd.3 = (bf16[528,768]{1,0:T(8,128)(2,1)}, bf16[528,3072]{1,0:T(8,128)(2,1)}, f32[528,768]{1,0:T(8,128)}, bf16[528,768]{1,0:T(8,128)(2,1)}, f32[1,3072]{1,0:T(1,128)}, /*index=5*/f32[8,768]{1,0:T(8,128)}) custom-call(s32[1]{0:T(128)} %get-tuple-element.186.count_ref, bf16[512,768]{1,0:T(8,128)(2,1)} %get-tuple-element.172.cot_ref, ...), custom_call_target="tpu_custom_call" | custom-call | tf_op jit(solution)/shard_map/ffn_bwd/pallas_call | solution.py:293
  282.4 2.9 fusion.48
  285.3 21.8 %attn_bwd.3 = (bf16[528,768]{1,0:T(8,128)(2,1)}, bf16[528,768]{1,0:T(8,128)(2,1)}, bf16[528,768]{1,0:T(8,128)(2,1)}, f32[1,768]{1,0:T(1,128)}, f32[1,768]{1,0:T(...) custom-call(s32[1]{0:T(128)} %get-tuple-element.186.count_ref, f32[528,768]{1,0:T(8,128)} %get-tuple-element.89.dr1_ref, ...), custom_call_target="tpu_custom_call" | custom-call | tf_op jit(solution)/shard_map/attn_bwd/pallas_call | solution.py:375
  307.1 3.0 fusion.45
  313.8 2.5 pad_maximum_fusion.1
  318.2 8.5 %fusion.11 = bf16[768,3072]{1,0:T(8,128)(2,1)S(1)} fusion(bf16[528,3072]{1,0:T(8,128)(2,1)S(1)} %copy-done.24, bf16[528,3072]{1,0:T(8,128)(2,1)} %get-tuple-element.110, bf16[528,768]{1,0:T(8,128)(2,1)} %get-tuple-element.109, bf16[528,768]{1,0:T(8,128)(2,1)} %get-tuple-element.108), kind=kOutput, calls=%fused_computation.9 | convolution fusion | flops 5001412608 | bytes 12828672 | tf_op jit(solution)/shard_map/dot_general | solution.py:38
  332.3 6.9 %fusion.8 = bf16[3072,768]{1,0:T(8,128)(2,1)S(1)} fusion(bf16[528,3072]{1,0:T(8,128)(2,1)S(1)} %copy-done.23, bf16[528,3072]{1,0:T(8,128)(2,1)S(1)} %copy-done.22, bf16[528,768]{1,0:T(8,128)(2,1)S(1)} %copy-done.25, bf16[528,768]{1,0:T(8,128)(2,1)S(1)} %copy-done.26), kind=kOutput, calls=%fused_computation.8 | convolution fusion | flops 5001412608 | bytes 12828672 | tf_op jit(solution)/shard_map/dot_general | solution.py:38
  339.2 2.6 constant_dynamic-update-slice_fusion.8
  343.4 39.8 %all-reduce.2 = f32[9216]{0:T(1024)S(1)} all-reduce(f32[9216]{0:T(1024)S(1)} %maximum_add_fusion), channel_id=6, replica_groups=mesh['wide'=16,'narrow'=2] {'wide','narrow'}, use_global_device_ids=true, to_apply=%region_2.3.clone | all-reduce | flops 9216 | bytes 73728
  383.8 2.6 pad_maximum_fusion.3
  388.3 33.8 %reduce-scatter.3.cloned.1.call-done = bf16[1,96,768]{2,1,0:T(8,128)(2,1)} async-done(((bf16[32,96,768]{2,1,0:T(8,128)(2,1)}), bf16[1,96,768]{2,1,0:T(8,128)(2,1)}) %reduce-scatter.3.cloned.1.call-update) | async-done | bytes 147472 | tf_op jit(solution)/shard_map/reduce_scatter | solution.py:486
  425.5 137.9 %reduce-scatter.5.cloned.1.call-done = bf16[1,192,768]{2,1,0:T(8,128)(2,1)} async-done(((bf16[32,192,768]{2,1,0:T(8,128)(2,1)}), bf16[1,192,768]{2,1,0:T(8,128)(2,1)}) %reduce-scatter.5.cloned.1.call-update) | async-done | bytes 294928 | tf_op jit(solution)/shard_map/reduce_scatter | solution.py:483
  (137 shorter events, 49.3 us)
Async XLA Ops:
  7.2 15.7 %copy-start.1 = (bf16[1024,768]{1,0:T(8,128)(2,1)S(1)}, bf16[1024,768]{1,0:T(8,128)(2,1)}, u32[]{:S(2)}) copy-start(bf16[1024,768]{1,0:T(8,128)(2,1)} %param.12) | copy-start | bytes 4718596
  7.2 16.9 %copy-start.2 = (bf16[1024,768]{1,0:T(8,128)(2,1)S(1)}, bf16[1024,768]{1,0:T(8,128)(2,1)}, u32[]{:S(2)}) copy-start(bf16[1024,768]{1,0:T(8,128)(2,1)} %param.23) | copy-start | bytes 4718596
  7.2 72.7 %all-gather.5.cloned.1.call-start = ((), (), s32[]{:S(2)}) async-start(), calls=%async_computation.4 | async-start | bytes 5271552 | tf_op jit(solution)/shard_map/all_gather | solution.py:422
  12.2 152.2 %all-gather.7.cloned.1.call-start = ((), (), s32[]{:S(2)}) async-start(), calls=%async_computation.5 | async-start | bytes 9732096 | tf_op jit(solution)/shard_map/all_gather | solution.py:428
  17.4 404.7 %reduce-scatter.3.cloned.1.call-start = ((), (), s32[]{:S(2)}) async-start(), calls=%async_computation.2 | async-start | bytes 4866048 | tf_op jit(solution)/shard_map/reduce_scatter | solution.py:486
  164.3 5.1 copy-start
  241.3 23.0 %copy-start.5 = (bf16[528,768]{1,0:T(8,128)(2,1)S(1)}, bf16[528,768]{1,0:T(8,128)(2,1)}, u32[]{:S(2)}) copy-start(bf16[528,768]{1,0:T(8,128)(2,1)} %get-tuple-element.101) | copy-start | bytes 2433028
  265.5 16.8 %copy-start.6 = (bf16[528,768]{1,0:T(8,128)(2,1)S(1)}, bf16[528,768]{1,0:T(8,128)(2,1)}, u32[]{:S(2)}) copy-start(bf16[528,768]{1,0:T(8,128)(2,1)} %get-tuple-element.94.o_ref) | copy-start | bytes 2433028
  265.5 16.8 %copy-start.7 = (bf16[528,768]{1,0:T(8,128)(2,1)S(1)}, bf16[528,768]{1,0:T(8,128)(2,1)}, u32[]{:S(2)}) copy-start(bf16[528,768]{1,0:T(8,128)(2,1)} %get-tuple-element.81.o_ref) | copy-start | bytes 2433028
  265.5 16.9 %copy-start.8 = (bf16[528,768]{1,0:T(8,128)(2,1)S(1)}, bf16[528,768]{1,0:T(8,128)(2,1)}, u32[]{:S(2)}) copy-start(bf16[528,768]{1,0:T(8,128)(2,1)} %get-tuple-element.77.dr1b_ref) | copy-start | bytes 2433028
  285.3 21.8 %copy-start.10 = (bf16[1056,768]{1,0:T(8,128)(2,1)S(1)}, bf16[1056,768]{1,0:T(8,128)(2,1)}, u32[]{:S(2)}) copy-start(bf16[1056,768]{1,0:T(8,128)(2,1)} %copy-done.9) | copy-start | bytes 4866052
  285.3 21.8 %copy-start.29 = (bf16[528,768]{1,0:T(8,128)(2,1)S(1)}, bf16[528,768]{1,0:T(8,128)(2,1)}, u32[]{:S(2)}) copy-start(bf16[528,768]{1,0:T(8,128)(2,1)} %get-tuple-element.103) | copy-start | bytes 2433028
  307.1 3.0 copy-start.28
  307.1 3.0 copy-start.31
  310.2 1.8 copy-start.27
  310.2 1.8 copy-start.30
  316.3 1.9 copy-start.24
  316.3 247.2 %reduce-scatter.5.cloned.1.call-start = ((), (), s32[]{:S(2)}) async-start(), calls=%async_computation.3 | async-start | bytes 9732096 | tf_op jit(solution)/shard_map/reduce_scatter | solution.py:483
  326.7 4.7 copy-start.25
  326.7 4.7 copy-start.26
  327.9 3.5 copy-start.22
  327.9 4.4 copy-start.23
  341.9 44.6 %copy-start.3 = (f32[512,768]{1,0:T(8,128)S(1)}, f32[512,768]{1,0:T(8,128)}, u32[]{:S(2)}) copy-start(f32[512,768]{1,0:T(8,128)} %get-tuple-element.98) | copy-start | bytes 4718596
  341.9 44.6 %copy-start.4 = (f32[512,768]{1,0:T(8,128)S(1)}, f32[512,768]{1,0:T(8,128)}, u32[]{:S(2)}) copy-start(f32[512,768]{1,0:T(8,128)} %get-tuple-element.97) | copy-start | bytes 4718596
  (12 other events, 11.3 us)
Sparse Core Ops, SparseCore 0:
  12.3 67.5 all-gather.4
  83.4 80.8 all-gather.6
  316.4 105.6 reduce-scatter.2
  428.9 134.5 reduce-scatter.4

commit v2 on v1

--- a/solution.py
+++ b/solution.py
@@ -136,8 +136,31 @@
     return pl.BlockSpec((height, width), lambda j, *_: (j, 0))
 
 
+def slot_const(slot):
+    return pl.BlockSpec((R, D), lambda j, *_: (slot, 0))
+
+
+def slot_cols(slot, width):
+    return pl.BlockSpec((R, width), lambda j, *_: (slot, j))
+
+
+def any_spec():
+    return pl.BlockSpec(memory_space=pl.ANY)
+
+
 def sds(shape, dtype):
     return jax.ShapeDtypeStruct(shape, dtype)
+
+
+def kept(n, kernel):
+    def body(*refs):
+        return kernel(*refs[:1], *refs[1 + n :])
+
+    return body
+
+
+def cost(flops, moved):
+    return pl.CostEstimate(flops=flops, bytes_accessed=moved, transcendentals=0)
 
 
 def params():
@@ -146,19 +169,22 @@
     )
 
 
-def attn_fwd(count, tok, mem, wq, wk, wv, wo, vecs):
+def attn_fwd(slot, slots, prev, count, tok, mem, wqk, wvo, vecs):
+    n = len(prev)
     return pl.pallas_call(
-        attn_fwd_kernel,
+        kept(n, attn_fwd_kernel),
         grid_spec=pltpu.PrefetchScalarGridSpec(
             num_scalar_prefetch=1,
             grid=(NQ,),
-            in_specs=[
-                const((SEG, D)), const((MPAD, D)),
-                cols(D, QUAD), cols(D, QUAD), cols(D, QUAD), rows(QUAD, D),
+            in_specs=[any_spec()] * n + [
+                pl.BlockSpec((SEG, D), lambda j, *_: (slot, 0)), const((MPAD, D)),
+                cols(D, QUAD), pl.BlockSpec((D, QUAD), lambda j, *_: (0, NQ + j)),
+                cols(D, QUAD), pl.BlockSpec((QUAD, D), lambda j, *_: (j, 1)),
                 cols(8, QUAD), const((8, D)),
             ],
             out_specs=[
-                const((R, D)), cols(R, QUAD), cols(R, QUAD), cols(R, QUAD), cols(R, QUAD),
+                slot_const(slot), cols(R, QUAD), cols(R, QUAD), cols(R, QUAD),
+                slot_cols(slot, QUAD),
                 cols(R, QUAD),
                 pl.BlockSpec((4, R, KEYS), lambda j, *_: (j, 0, 0)),
                 const((R, D)), const((R, 128)),
@@ -169,13 +195,15 @@
             ],
         ),
         out_shape=[
-            sds((R, D), BF16), sds((R, D), BF16), sds((R, D), BF16), sds((R, D), BF16),
-            sds((R, D), BF16), sds((R, D), F32), sds((HEADS, R, KEYS), BF16),
+            sds((slots * R, D), BF16), sds((R, D), BF16), sds((R, D), BF16), sds((R, D), BF16),
+            sds((slots * R, D), BF16), sds((R, D), F32), sds((HEADS, R, KEYS), BF16),
             sds((R, D), F32), sds((R, 128), F32),
         ],
+        input_output_aliases={1: 0, 2: 4} if n else {},
         compiler_params=params(),
+        cost_estimate=cost(2 * R * (4 * D * D + 2 * KEYS * D * 4), 20_000_000),
         name="attn_fwd",
-    )(count, tok, mem, wq, wk, wv, wo, vecs, vecs)
+    )(count, *prev, tok, mem, wqk, wqk, wvo, wvo, vecs, vecs)
 
 
 def ffn_fwd_kernel(
@@ -220,26 +248,31 @@
         write_ref[...] = jnp.where(row_ids(MPAD, D) < MEM, y[SEG:R, :], 0.0)
 
 
-def ffn_fwd(count, xhat, wi, bi, wo, vecs):
+def ffn_fwd(slot, slots, prev, count, xhat, wi, bi, wo, vecs):
+    n = len(prev)
     return pl.pallas_call(
-        ffn_fwd_kernel,
+        kept(n, ffn_fwd_kernel),
         grid_spec=pltpu.PrefetchScalarGridSpec(
             num_scalar_prefetch=1,
             grid=(NF,),
-            in_specs=[const((R, D)), cols(D, BF), cols(1, BF), rows(BF, D), const((8, D))],
+            in_specs=[any_spec()] * n + [const((R, D)), cols(D, BF), cols(1, BF), rows(BF, D), const((8, D))],
             out_specs=[
-                const((R, D)), cols(R, BF), cols(R, BF), const((SEG, D)), const((MPAD, D)),
+                slot_const(slot), slot_cols(slot, BF), cols(R, BF),
+                pl.BlockSpec((SEG, D), lambda j, *_: (slot, 0)), const((MPAD, D)),
                 const((R, D)), const((R, 128)),
             ],
             scratch_shapes=[pltpu.VMEM((R, D), F32)],
         ),
         out_shape=[
-            sds((R, D), BF16), sds((R, FF), BF16), sds((R, FF), BF16), sds((SEG, D), BF16),
+            sds((slots * R, D), BF16), sds((slots * R, FF), BF16), sds((R, FF), BF16),
+            sds((slots * SEG, D), BF16),
             sds((MPAD, D), F32), sds((R, D), F32), sds((R, 128), F32),
         ],
+        input_output_aliases={1: 0, 2: 1, 3: 3} if n else {},
         compiler_params=params(),
+        cost_estimate=cost(2 * R * 2 * D * FF * 2, 20_000_000),
         name="ffn_fwd",
-    )(count, xhat, wi, bi, wo, vecs)
+    )(count, *prev, xhat, wi, bi, wo, vecs)
 
 
 def norm_pull(grad, gain, xhat, rstd):
@@ -289,30 +322,33 @@
         dvec_ref[0:2, :] = jnp.zeros((2, D), F32)
 
 
-def ffn_bwd(count, cot, gw, xhat2, rstd2, xhat, rstd, wi, wo, gp, vecs):
+def ffn_bwd(slot, slots, prev, count, cot, gw, xhat2, rstd2, xhat, rstd, wi, wo, gp, vecs):
+    n = len(prev)
     return pl.pallas_call(
-        ffn_bwd_kernel,
+        kept(n, ffn_bwd_kernel),
         grid_spec=pltpu.PrefetchScalarGridSpec(
             num_scalar_prefetch=1,
             grid=(NF,),
-            in_specs=[
-                const((SEG, D)), const((MPAD, D)), const((R, D)), const((R, 128)),
+            in_specs=[any_spec()] * n + [
+                pl.BlockSpec((SEG, D), lambda j, *_: (slot, 0)), const((MPAD, D)), const((R, D)), const((R, 128)),
                 const((R, D)), const((R, 128)), cols(D, BF), rows(BF, D), cols(R, BF),
                 const((8, D)),
             ],
             out_specs=[
-                const((R, D)), cols(R, BF), const((R, D)), const((R, D)), cols(1, BF),
-                const((8, D)),
+                slot_const(slot), slot_cols(slot, BF), const((R, D)), slot_const(slot),
+                cols(1, BF), const((8, D)),
             ],
             scratch_shapes=[pltpu.VMEM((R, D), F32)],
         ),
         out_shape=[
-            sds((R, D), BF16), sds((R, FF), BF16), sds((R, D), F32), sds((R, D), BF16),
-            sds((1, FF), F32), sds((8, D), F32),
+            sds((slots * R, D), BF16), sds((slots * R, FF), BF16), sds((R, D), F32),
+            sds((slots * R, D), BF16), sds((1, FF), F32), sds((8, D), F32),
         ],
+        input_output_aliases={1: 0, 2: 1, 3: 3} if n else {},
         compiler_params=params(),
+        cost_estimate=cost(2 * R * 2 * D * FF * 2, 20_000_000),
         name="ffn_bwd",
-    )(count, cot, gw, xhat2, rstd2, xhat, rstd, wi, wo, gp, vecs)
+    )(count, *prev, cot, gw, xhat2, rstd2, xhat, rstd, wi, wo, gp, vecs)
 
 
 def attn_bwd_kernel(
@@ -371,21 +407,25 @@
         gmem_ref[...] = jnp.where(row_ids(MPAD, D) < MEM, acc_s[SEG:R, :], 0.0)
 
 
-def attn_bwd(count, dr1, dr1b, wq, wk, wv, wo, q, k, v, o, linv, e):
+def attn_bwd(slot, slots, prev, count, dr1, dr1b, wqk, wvo, q, k, v, o, linv, e):
+    n = len(prev)
     return pl.pallas_call(
-        attn_bwd_kernel,
+        kept(n, attn_bwd_kernel),
         grid_spec=pltpu.PrefetchScalarGridSpec(
             num_scalar_prefetch=1,
             grid=(NQ,),
-            in_specs=[
-                const((R, D)), const((R, D)),
-                cols(D, QUAD), cols(D, QUAD), cols(D, QUAD), rows(QUAD, D),
-                cols(R, QUAD), cols(R, QUAD), cols(R, QUAD), cols(R, QUAD), cols(R, QUAD),
+            in_specs=[any_spec()] * n + [
+                const((R, D)), slot_const(slot),
+                cols(D, QUAD), pl.BlockSpec((D, QUAD), lambda j, *_: (0, NQ + j)),
+                cols(D, QUAD), pl.BlockSpec((QUAD, D), lambda j, *_: (j, 1)),
+                cols(R, QUAD), cols(R, QUAD), cols(R, QUAD), slot_cols(slot, QUAD),
+                cols(R, QUAD),
                 pl.BlockSpec((4, R, KEYS), lambda j, *_: (j, 0, 0)),
             ],
             out_specs=[
-                cols(R, QUAD), cols(R, QUAD), cols(R, QUAD), cols(1, QUAD), cols(1, QUAD),
-                const((SEG, D)), const((MPAD, D)),
+                slot_cols(slot, QUAD), slot_cols(slot, QUAD), slot_cols(slot, QUAD),
+                cols(1, QUAD), cols(1, QUAD),
+                pl.BlockSpec((SEG, D), lambda j, *_: (slot, 0)), const((MPAD, D)),
             ],
             scratch_shapes=[
                 pltpu.VMEM((KEYS, QUAD), BF16), pltpu.VMEM((KEYS, QUAD), BF16),
@@ -393,116 +433,308 @@
             ],
         ),
         out_shape=[
-            sds((R, D), BF16), sds((R, D), BF16), sds((R, D), BF16), sds((1, D), F32),
-            sds((1, D), F32), sds((SEG, D), F32), sds((MPAD, D), F32),
+            sds((slots * R, D), BF16), sds((slots * R, D), BF16), sds((slots * R, D), BF16),
+            sds((1, D), F32), sds((1, D), F32), sds((slots * SEG, D), F32), sds((MPAD, D), F32),
         ],
+        input_output_aliases={1: 0, 2: 1, 3: 2, 4: 5} if n else {},
         compiler_params=params(),
+        cost_estimate=cost(2 * R * (4 * D * D + 5 * KEYS * D * 4), 20_000_000),
         name="attn_bwd",
-    )(count, dr1, dr1b, wq, wk, wv, wo, q, k, v, o, linv, e)
-
-
-AXES = ("wide", "narrow")
-
-
-def wgrad(left, grad):
-    return tn(left, grad).astype(BF16)
+    )(count, *prev, dr1, dr1b, wqk, wqk, wvo, wvo, q, k, v, o, linv, e)
+
+
+def wgrad_inner_kernel(core_ref, h_ref, da_ref, db_ref, mine_ref, theirs_ref):
+    mine_ref[...] = tn(h_ref[...], da_ref[...]).astype(BF16)
+    theirs_ref[...] = tn(h_ref[...], db_ref[...]).astype(BF16)
+
+
+def wgrad_inner(core, h, d):
+    depth, n = h.shape[0], FF // D // 2
+    return pl.pallas_call(
+        wgrad_inner_kernel,
+        grid_spec=pltpu.PrefetchScalarGridSpec(
+            num_scalar_prefetch=1,
+            grid=(n,),
+            in_specs=[
+                const((depth, D)),
+                pl.BlockSpec((depth, D), lambda j, c: (0, c[0] * n + j)),
+                pl.BlockSpec((depth, D), lambda j, c: (0, (1 - c[0]) * n + j)),
+            ],
+            out_specs=[cols(D, D), cols(D, D)],
+        ),
+        out_shape=[sds((D, FF // 2), BF16)] * 2,
+        compiler_params=params(),
+        cost_estimate=cost(2 * depth * D * FF * 2, 15_000_000),
+        name="wgrad_inner",
+    )(core, h, d, d)
+
+
+def wgrad_outer_kernel(core_ref, g_ref, d_ref, mine_ref, theirs_ref):
+    full = tn(g_ref[...], d_ref[...]).astype(BF16)
+    low = core_ref[0] == 0
+    left, right = full[:, : D // 2], full[:, D // 2 :]
+    mine_ref[...] = jnp.where(low, left, right)
+    theirs_ref[...] = jnp.where(low, right, left)
+
+
+def wgrad_outer(core, g, d):
+    depth, n = g.shape[0], FF // D
+    return pl.pallas_call(
+        wgrad_outer_kernel,
+        grid_spec=pltpu.PrefetchScalarGridSpec(
+            num_scalar_prefetch=1,
+            grid=(n,),
+            in_specs=[cols(depth, D), const((depth, D))],
+            out_specs=[rows(D, D // 2), rows(D, D // 2)],
+        ),
+        out_shape=[sds((FF, D // 2), BF16)] * 2,
+        compiler_params=params(),
+        cost_estimate=cost(2 * depth * D * FF * 2, 15_000_000),
+        name="wgrad_outer",
+    )(core, g, d)
+
+
+def wgrad_attn_kernel(
+    core_ref, hb_ref, o_ref, dq_ref, dk_ref, dv_ref, da_ref, qv_ref, vq_ref, ko_ref, ok_ref
+):
+    low = core_ref[0] == 0
+
+    def put(mine_ref, theirs_ref, left, right):
+        mine_ref[...] = jnp.where(low, left, right)
+        theirs_ref[...] = jnp.where(low, right, left)
+
+    dq, dk = tn(hb_ref[...], dq_ref[...]), tn(hb_ref[...], dk_ref[...])
+    dv, do = tn(hb_ref[...], dv_ref[...]), tn(o_ref[...], da_ref[...])
+    put(qv_ref, vq_ref, dq.astype(BF16), dv.astype(BF16))
+    put(ko_ref, ok_ref, dk.astype(BF16), do.astype(BF16))
+
+
+def wgrad_attn(core, hb, o, dq, dk, dv, da):
+    depth, n = hb.shape[0], D // QUAD
+    return pl.pallas_call(
+        wgrad_attn_kernel,
+        grid_spec=pltpu.PrefetchScalarGridSpec(
+            num_scalar_prefetch=1,
+            grid=(n,),
+            in_specs=[const((depth, D))] * 2 + [cols(depth, QUAD)] * 4,
+            out_specs=[cols(D, QUAD)] * 4,
+        ),
+        out_shape=[sds((D, D), BF16)] * 4,
+        compiler_params=params(),
+        cost_estimate=cost(2 * depth * D * D * 4 * 2, 15_000_000),
+        name="wgrad_attn",
+    )(core, hb, o, dq, dk, dv, da)
+
+
+def strides(size):
+    return [1 << i for i in reversed(range(size.bit_length() - 1))]
+
+
+def after(value, *others):
+    return lax.optimization_barrier((value, others))[0]
+
+
+class Cube:
+    def __init__(self, wide, narrow):
+        self.size = {"wide": wide, "narrow": narrow}
+        self.dims = [("wide", s) for s in strides(wide)] + [("narrow", s) for s in strides(narrow)]
+        self.core, self.y, self.x = ("wide", 1), ("wide", 2), ("narrow", 1)
+        self.rest = [d for d in self.dims if d not in (self.core, self.y, self.x)]
+
+    def bit(self, dim):
+        return (lax.axis_index(dim[0]) // dim[1]) % 2
+
+    def swap(self, value, dim):
+        axis, stride = dim
+        return lax.ppermute(value, axis, [(i, i ^ stride) for i in range(self.size[axis])])
+
+    def open(self, value):
+        return value.reshape((1,) * len(self.dims) + value.shape)
+
+    def join(self, value, got, dim):
+        low = self.bit(dim) == 0
+        return jnp.concatenate(
+            [jnp.where(low, value, got), jnp.where(low, got, value)], axis=self.dims.index(dim)
+        )
+
+    def grow(self, value, *dims):
+        for dim in dims:
+            value = self.join(value, self.swap(value, dim), dim)
+        return value
+
+    def add(self, mine, got):
+        return (mine.astype(F32) + got.astype(F32)).astype(mine.dtype)
+
+    def split(self, value, dim):
+        axis, bit = self.dims.index(dim), self.bit(dim)
+        return (
+            lax.dynamic_index_in_dim(value, bit, axis),
+            lax.dynamic_index_in_dim(value, 1 - bit, axis),
+        )
+
+    def shrink(self, value, *dims):
+        for dim in dims:
+            mine, theirs = self.split(value, dim)
+            value = self.add(mine, self.swap(theirs, dim))
+        return value
+
+    def phase(self, *items):
+        parts = [self.split(value, dim) for value, dim in items]
+        sends = lax.optimization_barrier([p[1] for p in parts])
+        gots = [self.swap(send, dim) for send, (_, dim) in zip(sends, items)]
+        gots = lax.optimization_barrier(gots)
+        return [self.add(p[0], got) for p, got in zip(parts, gots)]
+
+    def spread(self, value):
+        return value.reshape((2,) * len(self.dims) + (-1, value.shape[-1]))
+
+    def halves(self, value):
+        mine, theirs = self.split(value, self.core)
+        got = self.swap(theirs, self.core)
+        low = self.bit(self.core) == 0
+        width = value.shape[-1]
+        return (
+            jnp.where(low, mine, got).reshape(-1, width),
+            jnp.where(low, got, mine).reshape(-1, width),
+        )
+
+
+def lanes_of(vec, own, groups):
+    n = vec.shape[-1]
+    height = -(-n // 128)
+    vec = jnp.pad(vec.reshape(groups, n), ((0, 0), (0, height * 128 - n)))
+    vec = vec.reshape(groups, height, 128)
+    return jnp.pad(vec, ((0, 0), (0, own - height), (0, 0))).reshape(groups * own, 128)
+
+
+def lanes_back(block, own, groups, n):
+    height = -(-n // 128)
+    return block.reshape(groups, own, 128)[:, :height].reshape(groups, height * 128)[:, :n]
 
 
 def per_device(
-    tokens, init_memory, w_query, w_key, w_value, w_output, w_inner, w_outer, vectors,
+    sizes, tokens, init_memory, w_query, w_key, w_value, w_output, w_inner, w_outer, vectors,
     chain_start, true_count, cotangent,
 ):
+    cube = Cube(*sizes)
+    core = cube.bit(cube.core).reshape(1)
     slots = chain_start.shape[0]
     parts = D * D // w_query.shape[0]
     own = D // parts
-    row = jnp.pad(vectors, (0, 8 * D - vectors.shape[0])).reshape(8, D)
-    local_attn = jnp.concatenate(
-        [w.reshape(own, D) for w in (w_query, w_key, w_value, w_output)] + [row], axis=0
-    )
-    attn_all = lax.all_gather(local_attn, AXES, axis=0, tiled=False)
-    local_ffn = jnp.concatenate(
-        [w_inner.reshape(own, FF)[:, D * i : D * i + D] for i in range(FF // D)]
-        + [w_outer.reshape(4 * own, D)],
-        axis=0,
-    )
-    ffn_all = lax.all_gather(local_ffn, AXES, axis=0, tiled=False)
-    wq, wk, wv, wo = (
-        attn_all[:, own * i : own * i + own].reshape(D, D) for i in range(4)
-    )
-    vec_all = attn_all[:, 4 * own].reshape(parts, D)[:, : vectors.shape[0]].reshape(-1)
-    vec_all = vec_all.astype(F32)
+    n_vec = vectors.shape[0]
+    square = [w.reshape(own, D) for w in (w_query, w_key, w_value, w_output)]
+    wqk = cube.open(jnp.concatenate(square[:2], axis=1))
+    wvo = cube.open(jnp.concatenate(square[2:] + [lanes_of(vectors, own, 1)], axis=1))
+    wi = cube.open(w_inner.reshape(own, FF))
+    wu = cube.open(w_outer.reshape(FF // parts, D))
+    wqk, wvo = cube.grow(wqk, *cube.rest), cube.grow(wvo, *cube.rest)
+    wi, wu = cube.grow(after(wi, wqk), *cube.rest), cube.grow(after(wu, wvo), *cube.rest)
+    wqk, wvo = cube.grow(wqk, cube.y, cube.x), cube.grow(wvo, cube.x, cube.y)
+    wi, wu = cube.grow(after(wi, wqk), cube.y), cube.grow(after(wu, wvo), cube.x)
+    wqk, wvo = cube.grow(wqk, cube.core), cube.grow(wvo, cube.core)
+    wqk, wvo = after(wqk, wi), after(wvo, wu)
+    wqk, wvo = wqk.reshape(D, -1), wvo.reshape(D, -1)
+    wi_got, wu_got = cube.swap(wi, cube.x), cube.swap(wu, cube.y)
+    vec_all = lanes_back(wvo[:, 2 * D :], own, parts, n_vec).reshape(-1).astype(F32)
     vecs = vec_all[: 8 * D].reshape(8, D)
     bi = vec_all[8 * D :].reshape(1, FF)
-    wi = jnp.concatenate(
-        [ffn_all[:, own * i : own * i + own].reshape(D, D) for i in range(FF // D)], axis=1
-    )
-    wu = ffn_all[:, 4 * own :].reshape(FF, D)
-
-    tok = tokens.reshape(slots, SEG, D)
-    cot = cotangent.reshape(slots, SEG, D)
+
     init = jnp.pad(init_memory.astype(F32), ((0, 0), (0, MPAD - MEM), (0, 0)))
     carry = jnp.zeros((MPAD, D), F32)
-    saved, mixed = [], []
+    saved = []
+    hb = o = h1b = g = mixed = None
     for s in range(slots):
         count = true_count[s : s + 1]
         memory = jnp.where(chain_start[s] > 0, init[s], carry)
-        a = attn_fwd(count, tok[s], memory, wq, wk, wv, wo, vecs)
-        f = ffn_fwd(count, a[7], wi, bi, wu, vecs)
-        carry = f[4]
-        mixed.append(f[3])
-        saved.append((a, f))
+        prev = [hb, o] if s else []
+        hb, q, k, v, o, linv, e, xhat, rstd = attn_fwd(
+            s, slots, prev, count, tokens, memory, wqk, wvo, vecs
+        )
+        if s == 0:
+            wi = cube.join(wi, after(wi_got, xhat), cube.x)
+            wu = cube.join(wu, after(wu_got, xhat), cube.y)
+            wi = cube.grow(wi, cube.core).reshape(D, FF)
+            wu = cube.grow(wu, cube.core).reshape(FF, D)
+        prev = [h1b, g, mixed] if s else []
+        h1b, g, gp, mixed, carry, xhat2, rstd2 = ffn_fwd(
+            s, slots, prev, count, xhat, wi, bi, wu, vecs
+        )
+        saved.append((q, k, v, linv, e, xhat, rstd, gp, xhat2, rstd2))
     back = jnp.zeros((MPAD, D), F32)
-    done = [None] * slots
+    df2 = df1 = da = dq = dk = dv = grad_tokens = None
+    grad_init, vec_parts = [None] * slots, []
     for s in reversed(range(slots)):
         count = true_count[s : s + 1]
-        hb, q, k, v, o, linv, e, xhat, rstd = saved[s][0]
-        h1b, g, gp, _, _, xhat2, rstd2 = saved[s][1]
-        df2, df1, dr1, dr1b, dbi, dvec = ffn_bwd(
-            count, cot[s], back, xhat2, rstd2, xhat, rstd, wi, wu, gp, vecs
+        q, k, v, linv, e, xhat, rstd, gp, xhat2, rstd2 = saved[s]
+        prev = [df2, df1, da] if df2 is not None else []
+        df2, df1, dr1, da, dbi, dvec = ffn_bwd(
+            s, slots, prev, count, cotangent, back, xhat2, rstd2, xhat, rstd, wi, wu, gp, vecs
         )
-        dq, dk, dv, dqb, dvb, gtok, gmem = attn_bwd(
-            count, dr1, dr1b, wq, wk, wv, wo, q, k, v, o, linv, e
+        if s == 0:
+            outer = wgrad_outer(core, g, df2)
+            inner = wgrad_inner(core, after(h1b, outer), df1)
+            outer = cube.spread(cube.add(outer[0], cube.swap(outer[1], cube.core)))
+            inner = cube.spread(cube.add(inner[0], cube.swap(inner[1], cube.core)))
+            inner, inner_send = cube.split(inner, cube.x)
+            outer, outer_send = cube.split(outer, cube.y)
+            dr1 = after(dr1, inner_send, outer_send)
+            inner_got = cube.swap(inner_send, cube.x)
+            outer_got = cube.swap(outer_send, cube.y)
+        prev = [dq, dk, dv, grad_tokens] if dq is not None else []
+        dq, dk, dv, dqb, dvb, grad_tokens, gmem = attn_bwd(
+            s, slots, prev, count, dr1, da, wqk, wvo, q, k, v, o, linv, e
         )
         starts = chain_start[s] > 0
-        ginit = jnp.where(starts, gmem, 0.0)[:MEM]
+        grad_init[s] = jnp.where(starts, gmem, 0.0)[:MEM]
         back = jnp.where(starts, 0.0, gmem)
-        vec = jnp.concatenate([dqb, dvb, dvec[2:8]], axis=0).reshape(-1)
-        vec = jnp.concatenate([vec, dbi.reshape(-1)])
-        done[s] = (hb, o, h1b, g, df2, df1, dr1b, dq, dk, dv, gtok, ginit, vec)
-
-    def both(i):
-        return jnp.concatenate([d[i] for d in done], axis=0)
-
-    hb, o, h1b, g, df2, df1, dr1b, dq, dk, dv = (both(i) for i in range(10))
-    vec = sum(d[12] for d in done)
-    g_inner = wgrad(h1b, df1).reshape(parts, own, FF)
-    g_outer = wgrad(g, df2).reshape(parts, 4 * own, D)
-    flat_ffn = jnp.concatenate(
-        [g_inner[:, :, D * i : D * i + D] for i in range(FF // D)] + [g_outer], axis=1
+        vec_parts.append(
+            jnp.concatenate([dqb, dvb, dvec[2:8].reshape(1, -1), dbi], axis=1)
+        )
+    inner = cube.add(inner, after(inner_got, dq))
+    outer = cube.add(outer, after(outer_got, dq))
+    inner, inner_send = cube.split(inner, cube.y)
+    outer, outer_send = cube.split(outer, cube.x)
+    attn = wgrad_attn(core, after(hb, inner_send, outer_send), o, dq, dk, dv, da)
+    inner_got = cube.swap(inner_send, cube.y)
+    outer_got = cube.swap(outer_send, cube.x)
+    inner = cube.add(inner, after(inner_got, attn))
+    outer = cube.add(outer, after(outer_got, attn))
+    first_got, second_got = cube.swap(attn[1], cube.core), cube.swap(attn[3], cube.core)
+    first = cube.spread(cube.add(attn[0], first_got))
+    second = cube.spread(cube.add(attn[2], second_got))
+    vec = sum(vec_parts).reshape((2,) * len(cube.dims) + (1, n_vec))
+    order = cube.rest[::-1]
+    first, second, inner, outer, vec = cube.phase(
+        (first, cube.x), (second, cube.y), (inner, order[0]), (outer, order[0]), (vec, cube.core)
     )
-    ffn_mine = lax.psum_scatter(flat_ffn, AXES, scatter_dimension=0, tiled=False)
-    squares = [wgrad(hb, dq), wgrad(hb, dk), wgrad(hb, dv), wgrad(o, dr1b)]
-    flat_attn = jnp.concatenate([w.reshape(parts, own, D) for w in squares], axis=1)
-    attn_mine = lax.psum_scatter(flat_attn, AXES, scatter_dimension=0, tiled=False)
-    vec_mine = lax.psum_scatter(vec, AXES, scatter_dimension=0, tiled=True)
-    inner_mine = jnp.concatenate(
-        [ffn_mine[own * i : own * i + own] for i in range(FF // D)], axis=1
+    first, second, vec = cube.phase((first, cube.y), (second, cube.x), (vec, cube.x))
+    inner, outer = cube.shrink(inner, *order[1:]), cube.shrink(outer, *order[1:])
+    first, second, vec = cube.phase((first, order[0]), (second, order[0]), (vec, cube.y))
+    first, second = cube.shrink(first, *order[1:]), cube.shrink(second, *order[1:])
+    vec = cube.shrink(vec, *order)
+    g_query, g_value = cube.halves(first)
+    g_key, g_output = cube.halves(second)
+    inner = jnp.concatenate(cube.halves(inner), axis=1)
+    outer = jnp.concatenate(cube.halves(outer), axis=1)
+    return (
+        mixed,
+        grad_tokens,
+        jnp.stack(grad_init),
+        *(
+            piece.astype(F32).reshape(-1)
+            for piece in (g_query, g_key, g_value, g_output, inner, outer, vec)
+        ),
     )
-    return (
-        jnp.concatenate(mixed, axis=0),
-        both(10),
-        jnp.stack([d[11] for d in done]),
-        *(attn_mine[own * i : own * i + own].reshape(-1).astype(F32) for i in range(4)),
-        inner_mine.reshape(-1).astype(F32),
-        ffn_mine[4 * own :].reshape(-1).astype(F32),
-        vec_mine,
-    )
+
+
+AXES = ("wide", "narrow")
 
 
 def solution(mesh):
     flat = P(AXES)
+    sizes = (mesh.shape["wide"], mesh.shape["narrow"])
     return jax.shard_map(
-        per_device,
+        functools.partial(per_device, sizes),
         mesh=mesh,
         in_specs=(P(AXES, None), P(AXES, None, None)) + (flat,) * 9 + (P(AXES, None),),
         out_specs=(P(AXES, None), P(AXES, None), P(AXES, None, None)) + (flat,) * 7,

time: 585 us -> 374 us (0.64)
  waiting for transfers between devices: 285 us -> 68 us
  starting transfers between devices: 0.16 us -> 48.9 us
  blocking collectives: 39.8 us -> 0 us
  Pallas kernels: 142 us -> 173 us
  other arithmetic: 16.1 us -> 45.7 us
  matrix products: 24.8 us -> 0 us
  local copies, waits for them, and re-layouts: 49.7 us -> 29.5 us
  between operations: 15.8 us -> 3.24 us
    reduce_scatter x2 -> x0, waiting for transfers between devices: 172 us -> none  [the longest x1 138 us: per_device(): lax.psum_scatter(flat_ffn, AXES, scatter_dimension=0, tiled=False)]
    all_gather x2 -> x0, waiting for transfers between devices: 113 us -> none  [the longest x1 58.5 us: per_device(): ffn_all = lax.all_gather(local_ffn, AXES, axis=0, tiled=False)]
    ppermute x0 -> x49, waiting for transfers between devices: none -> 68 us  [swap(): lax.ppermute(value, axis, [(i, i ^ stride) for i in range(self.size[axis])])]
    ppermute x0 -> x49, starting transfers between devices: none -> 48.9 us  [swap(): lax.ppermute(value, axis, [(i, i ^ stride) for i in range(self.size[axis])])]
    unnamed x1 -> x0, blocking collectives: 39.8 us -> none
    pallas_call x8 -> x11, Pallas kernels: 142 us -> 173 us  [the longest x2 42.7 us: attn_bwd(): pl.pallas_call(kept(n, attn_bwd_kernel), grid_spec=pltpu.PrefetchScalarGr...]
    dot_general x6 -> x0, matrix products: 24.8 us -> none  [tn(): lax.dot_general(a, b, (((0,), (0,)), ((), ())), preferred_element_type=F32)]
    slice x10 -> x2, local copies, waits for them, and re-layouts: 14.5 us -> 0.03 us  [the longest x1 0.01 us: per_device(): wvo[:, 2 * D:]]
  transfers between devices with their start and end apart: 4 -> 49, of which waited for: 4 -> 24; matrix products, arithmetic and copies ran while one was open for 9% -> 14% of each run, Pallas kernels for 3% -> 16%
where the time goes in v2:
time: 374 us; the launch traced here: 368 us
  Pallas kernels  173 us (46%)
  waiting for transfers between devices  68 us (18%)
  starting transfers between devices  48.9 us (13%)
  other arithmetic  45.7 us (12%)
  local copies, waits for them, and re-layouts  29.5 us (8%)
    ppermute x49, waiting for transfers between devices, swap(): lax.ppermute(value, axis, [(i, i ^ stride) for i in range(self.size[axis])])  68 us
    ppermute x49, starting transfers between devices, swap(): lax.ppermute(value, axis, [(i, i ^ stride) for i in range(self.size[axis])])  48.9 us
    pallas_call x2, Pallas kernels, attn_bwd(): pl.pallas_call(kept(n, attn_bwd_kernel), grid_spec=pltpu.PrefetchScalarGr...  42.7 us
    pallas_call x2, Pallas kernels, attn_fwd(): pl.pallas_call(kept(n, attn_fwd_kernel), grid_spec=pltpu.PrefetchScalarGr...  35.7 us
    pallas_call x2, Pallas kernels, ffn_bwd(): pl.pallas_call(kept(n, ffn_bwd_kernel), grid_spec=pltpu.PrefetchScalarGri...  32.5 us
    pallas_call x2, Pallas kernels, ffn_fwd(): pl.pallas_call(kept(n, ffn_fwd_kernel), grid_spec=pltpu.PrefetchScalarGri...  30.4 us
    convert_element_type x20, other arithmetic, add(): return (mine.astype(F32) + got.astype(F32)).astype(mine.dtype)  14.6 us
    concatenate x20, other arithmetic, join(): jnp.concatenate([jnp.where(low, value, got), jnp.where(low, got, value)],...  12.4 us
  transfers between devices with their start and end apart: 49, of which 24 were waited for; matrix products, arithmetic and copies ran while one was open for 14% of the time, Pallas kernels for 16%

profile of v2, /device:TPU:0, one launch (start us, length us, event | category | flops | bytes accessed | tf_op | source)
XLA Modules:
  0.0 368.1 jit_solution(18321728976384389362)
XLA Ops:
  3.0 4.1 %collective-permute-start.8 = (bf16[1,1,1,1,1,24,1664]{6,5,4,3,2,1,0:T(8,128)(2,1)S(1)}, bf16[1,1,1,1,1,24,1664]{6,5,4,3,2,1,0:T(8,128)(2,1)S(1)}, u32[]{:S(2)}, u32[]{:S(2)}) collective-permute-start(bf16[1,1,1,1,1,24,1664]{6,5,4,3,2,1,0:T(8,128)(2,1)S(1)} %maximum_bitcast_fusion), channel_id=1, source_target_pairs={{0,16},{2,18},{4,20},{6,22},{8,24},{10,26},{12,28},{14,30},{16,0},... | collective-permute-start | bytes 239624 | tf_op jit(solution)/shard_map/ppermute | solution.py:549
  17.6 4.6 %collective-permute-done.1 = bf16[2,1,1,1,1,24,1536]{6,5,4,3,2,1,0:T(8,128)(2,1)S(1)} collective-permute-done((bf16[2,1,1,1,1,24,1536]{6,5,4,3,2,1,0:T(8,128)(2,1)S(1)}, bf16[2,1,1,1,1,24,1536]{6,5,4,3,2,1,0:T(8,128)(2,1)S(1)}, u32[]{:S(2)}, u32[]{:S(2)}) %collective-permute-start.1) | collective-permute-done | bytes 147488 | tf_op jit(solution)/shard_map/ppermute | solution.py:549
  29.3 4.8 %collective-permute-done.5 = bf16[1,1,1,1,1,24,3072]{6,5,4,3,2,1,0:T(8,128)(2,1)S(1)} collective-permute-done((bf16[1,1,1,1,1,24,3072]{6,5,4,3,2,1,0:T(8,128)(2,1)S(1)}, bf16[1,1,1,1,1,24,3072]{6,5,4,3,2,1,0:T(8,128)(2,1)S(1)}, u32[]{:S(2)}, u32[]{:S(2)}) %collective-permute-start.5) | collective-permute-done | bytes 147488 | tf_op jit(solution)/shard_map/ppermute | solution.py:549
  40.1 3.1 collective-permute-done.6
  43.4 3.0 collective-permute-done.14
  46.5 4.0 %collective-permute-done.3 = bf16[2,2,2,1,1,24,1536]{6,5,4,3,2,1,0:T(8,128)(2,1)S(1)} collective-permute-done((bf16[2,2,2,1,1,24,1536]{6,5,4,3,2,1,0:T(8,128)(2,1)S(1)}, bf16[2,2,2,1,1,24,1536]{6,5,4,3,2,1,0:T(8,128)(2,1)S(1)}, u32[]{:S(2)}, u32[]{:S(2)}) %collective-permute-start.3) | collective-permute-done | bytes 589856 | tf_op jit(solution)/shard_map/ppermute | solution.py:549
  54.0 12.6 %collective-permute-done.7 = bf16[2,2,1,1,1,24,3072]{6,5,4,3,2,1,0:T(8,128)(2,1)S(1)} collective-permute-done((bf16[2,2,1,1,1,24,3072]{6,5,4,3,2,1,0:T(8,128)(2,1)S(1)}, bf16[2,2,1,1,1,24,3072]{6,5,4,3,2,1,0:T(8,128)(2,1)S(1)}, u32[]{:S(2)}, u32[]{:S(2)}) %collective-permute-start.7) | collective-permute-done | bytes 589856 | tf_op jit(solution)/shard_map/ppermute | solution.py:549
  78.9 17.8 %attn_fwd.2 = (bf16[1056,768]{1,0:T(8,128)(2,1)}, bf16[528,768]{1,0:T(8,128)(2,1)}, bf16[528,768]{1,0:T(8,128)(2,1)}, bf16[528,768]{1,0:T(8,128)(2,1)}, bf16[105...) custom-call(s32[1]{0:T(128)} %get-tuple-element.284.refs_0_, ...), custom_call_target="tpu_custom_call" | custom-call | flops 6643777536 | bytes 20000000 | tf_op jit(solution)/shard_map/attn_fwd/pallas_call | solution.py:174
  117.1 15.2 %ffn_fwd.2 = (bf16[1056,768]{1,0:T(8,128)(2,1)}, bf16[1056,3072]{1,0:T(8,128)(2,1)}, bf16[528,3072]{1,0:T(8,128)(2,1)}, bf16[1024,768]{1,0:T(8,128)(2,1)}, f32[1...) custom-call(s32[1]{0:T(128)} %get-tuple-element.284.refs_0_, f32[528,768]{1,0:T(8,128)} %get-tuple-element.118.refs_1_.refs_8_, ...), custom_call_target="tpu_custom_call" | custom-call | flops 9965666304 | bytes 20000000 | tf_op jit(solution)/shard_map/ffn_fwd/pallas_call | solution.py:253
  133.8 17.9 %attn_fwd.3 = (bf16[1056,768]{1,0:T(8,128)(2,1)}, bf16[528,768]{1,0:T(8,128)(2,1)}, bf16[528,768]{1,0:T(8,128)(2,1)}, bf16[528,768]{1,0:T(8,128)(2,1)}, bf16[105...) custom-call(s32[1]{0:T(128)} %get-tuple-element.285.refs_0_, ...), custom_call_target="tpu_custom_call", output_to_operand_aliasing={{0}: (1, {}), {4}: (2, {})} | custom-call | flops 6643777536 | bytes 20000000 | tf_op jit(solution)/shard_map/attn_fwd/pallas_call | solution.py:174
  151.7 15.2 %ffn_fwd.3 = (bf16[1056,768]{1,0:T(8,128)(2,1)}, bf16[1056,3072]{1,0:T(8,128)(2,1)}, bf16[528,3072]{1,0:T(8,128)(2,1)}, bf16[1024,768]{1,0:T(8,128)(2,1)}, f32[1...) custom-call(s32[1]{0:T(128)} %get-tuple-element.285.refs_0_, ...), custom_call_target="tpu_custom_call", output_to_operand_aliasing={{0}: (1, {}), {1}: (2, {}), {3}: (3, {})} | custom-call | flops 9965666304 | bytes 20000000 | tf_op jit(solution)/shard_map/ffn_fwd/pallas_call | solution.py:253
  167.5 16.3 %ffn_bwd.2 = (bf16[1056,768]{1,0:T(8,128)(2,1)}, bf16[1056,3072]{1,0:T(8,128)(2,1)}, f32[528,768]{1,0:T(8,128)}, bf16[1056,768]{1,0:T(8,128)(2,1)}, f32[1,3072]{1,0:T(1,128)}, /*index=5*/f32[8,768]{1,0:T(8,128)}) custom-call(s32[1]{0:T(128)} %get-tuple-element.285.refs_0_, bf16[1024,768]{1,0:T(8,128)(2,1)} %refs_4_.1, f32[16,768]{1,0:T(8,128)} %broadcast_1_refs_2_.2.refs_2_, ...), custom_call_target="tpu_custom_call" | custom-call | flops 9965666304 | bytes 20000000 | tf_op jit(solution)/shard_map/ffn_bwd/pallas_call | solution.py:327
  183.8 21.6 %attn_bwd.2 = (bf16[1056,768]{1,0:T(8,128)(2,1)}, bf16[1056,768]{1,0:T(8,128)(2,1)}, bf16[1056,768]{1,0:T(8,128)(2,1)}, f32[1,768]{1,0:T(1,128)}, f32[1,768]{1,0...) custom-call(s32[1]{0:T(128)} %get-tuple-element.285.refs_0_, f32[528,768]{1,0:T(8,128)} %get-tuple-element.133.refs_1_, ...), custom_call_target="tpu_custom_call" | custom-call | flops 12872318976 | bytes 20000000 | tf_op jit(solution)/shard_map/attn_bwd/pallas_call | solution.py:412
  206.8 16.2 %ffn_bwd.3 = (bf16[1056,768]{1,0:T(8,128)(2,1)}, bf16[1056,3072]{1,0:T(8,128)(2,1)}, f32[528,768]{1,0:T(8,128)}, bf16[1056,768]{1,0:T(8,128)(2,1)}, f32[1,3072]{1,0:T(1,128)}, /*index=5*/f32[8,768]{1,0:T(8,128)}) custom-call(s32[1]{0:T(128)} %get-tuple-element.284.refs_0_, ...), custom_call_target="tpu_custom_call", output_to_operand_aliasing={{0}: (1, {}), {1}: (2, {}), {3}: (3, {})} | custom-call | flops 9965666304 | bytes 20000000 | tf_op jit(solution)/shard_map/ffn_bwd/pallas_call | solution.py:327
  223.0 10.1 %wgrad_outer.1 = (bf16[3072,384]{1,0:T(8,128)(2,1)}, bf16[3072,384]{1,0:T(8,128)(2,1)}) custom-call(s32[1]{0:T(128)} %bitcast.13.core_ref, bf16[1056,3072]{1,0:T(8,128)(2,1)} %get-tuple-element.154.g_ref, bf16[1056,768]{1,0:T(8,128)(2,1)} %get-tuple-element.155.d_ref), custom_call_target="tpu_custom_call" | custom-call | flops 9965666304 | bytes 15000000 | tf_op jit(solution)/shard_map/wgrad_outer/pallas_call | solution.py:482
  233.2 10.2 %wgrad_inner.1 = (bf16[768,1536]{1,0:T(8,128)(2,1)}, bf16[768,1536]{1,0:T(8,128)(2,1)}) custom-call(s32[1]{0:T(128)} %bitcast.13.core_ref, bf16[1056,768]{1,0:T(8,128)(2,1)} %get-tuple-element.158.h_ref, bf16[1056,3072]{1,0:T(8,128)(2,1)} %get-tuple-element.159.da_ref.db_ref, bf16[1056,3072]{1,0:T(8,128)(2,1)} %get-tuple-element.159.da_ref.db_ref), custom_call_target="tpu_custom_call" | custom-call | flops 9965666304 | bytes 15000000 | tf_op jit(solution)/shard_map/wgrad_inner/pallas_call | solution.py:453
  244.1 3.0 add_convert_fusion
  254.8 21.1 %attn_bwd.3 = (bf16[1056,768]{1,0:T(8,128)(2,1)}, bf16[1056,768]{1,0:T(8,128)(2,1)}, bf16[1056,768]{1,0:T(8,128)(2,1)}, f32[1,768]{1,0:T(1,128)}, f32[1,768]{1,0...) custom-call(s32[1]{0:T(128)} %get-tuple-element.284.refs_0_, ...), custom_call_target="tpu_custom_call", output_to_operand_aliasing={{0}: (1, {}), {1}: (2, {}), {2}: (3, {}), {5}: (4, {})} | custom-call | flops 12872318976 | bytes 20000000 | tf_op jit(solution)/shard_map/attn_bwd/pallas_call | solution.py:412
  285.5 11.2 %wgrad_attn.1 = (bf16[768,768]{1,0:T(8,128)(2,1)}, bf16[768,768]{1,0:T(8,128)(2,1)}, bf16[768,768]{1,0:T(8,128)(2,1)}, bf16[768,768]{1,0:T(8,128)(2,1)}) custom-call(s32[1]{0:T(128)} %bitcast.13.core_ref, bf16[1056,768]{1,0:T(8,128)(2,1)} %get-tuple-element.175.hb_ref, bf16[1056,768]{1,0:T(8,128)(2,1)} %get-tuple-element.138.refs_10_.refs_14_.o_ref, ...), custom_call_target="tpu_custom_call" | custom-call | flops 9965666304 | bytes 15000000 | tf_op jit(solution)/shard_map/wgrad_attn/pallas_call | solution.py:514
  311.9 5.9 %collective-permute-done.30 = bf16[2,1,1,2,1,24,1536]{6,5,4,3,2,1,0:T(8,128)(2,1)S(1)} collective-permute-done((bf16[2,1,1,2,1,24,1536]{6,5,4,3,2,1,0:T(8,128)(2,1)}, bf16[2,1,1,2,1,24,1536]{6,5,4,3,2,1,0:T(8,128)(2,1)S(1)}, u32[]{:S(2)}, u32[]{:S(2)}) %collective-permute-start.30) | collective-permute-done | bytes 294944 | tf_op jit(solution)/shard_map/ppermute | solution.py:549
  317.8 4.3 %collective-permute-done.31 = bf16[2,1,1,2,1,96,384]{6,5,4,3,2,1,0:T(8,128)(2,1)S(1)} collective-permute-done((bf16[2,1,1,2,1,96,384]{6,5,4,3,2,1,0:T(8,128)(2,1)}, bf16[2,1,1,2,1,96,384]{6,5,4,3,2,1,0:T(8,128)(2,1)S(1)}, u32[]{:S(2)}, u32[]{:S(2)}) %collective-permute-start.31) | collective-permute-done | bytes 294944 | tf_op jit(solution)/shard_map/ppermute | solution.py:549
  329.3 3.3 collective-permute-start.43
  332.9 8.8 %collective-permute-done.43 = bf16[1,1,1,2,1,24,1536]{6,5,4,3,2,1,0:T(8,128)(2,1)S(1)} collective-permute-done((bf16[1,1,1,2,1,24,1536]{6,5,4,3,2,1,0:T(8,128)(2,1)S(1)}, bf16[1,1,1,2,1,24,1536]{6,5,4,3,2,1,0:T(8,128)(2,1)S(1)}, u32[]{:S(2)}, u32[]{:S(2)}) %collective-permute-start.43) | collective-permute-done | bytes 147488 | tf_op jit(solution)/shard_map/ppermute | solution.py:549
  355.1 3.0 collective-permute-start.41
  (273 shorter events, 127.5 us)
Async XLA Ops:
  3.0 13.9 %collective-permute-start.8 = (bf16[1,1,1,1,1,24,1664]{6,5,4,3,2,1,0:T(8,128)(2,1)S(1)}, bf16[1,1,1,1,1,24,1664]{6,5,4,3,2,1,0:T(8,128)(2,1)S(1)}, u32[]{:S(2)}, u32[]{:S(2)}) collective-permute-start(bf16[1,1,1,1,1,24,1664]{6,5,4,3,2,1,0:T(8,128)(2,1)S(1)} %maximum_bitcast_fusion), channel_id=1, source_target_pairs={{0,16},{2,18},{4,20},{6,22},{8,24},{10,26},{12,28},{14,30},{16,0},... | collective-permute-start | bytes 239624 | tf_op jit(solution)/shard_map/ppermute | solution.py:549
  22.2 15.1 %collective-permute-start.2 = (bf16[2,2,1,1,1,24,1536]{6,5,4,3,2,1,0:T(8,128)(2,1)S(1)}, bf16[2,2,1,1,1,24,1536]{6,5,4,3,2,1,0:T(8,128)(2,1)S(1)}, u32[]{:S(2)}, u32[]{:S(2)}) collective-permute-start(bf16[2,2,1,1,1,24,1536]{6,5,4,3,2,1,0:T(8,128)(2,1)S(1)} %pad_maximum_fusion.15), channel_id=1, source_target_pairs={{0,4},{2,6},{4,0},{6,2},{8,12},{10,14},{12,8},{14,10},{16,20},{18,... | collective-permute-start | bytes 884744 | tf_op jit(solution)/shard_map/ppermute | solution.py:549
  26.5 12.3 %collective-permute-start.10 = (bf16[2,2,1,1,1,24,1664]{6,5,4,3,2,1,0:T(8,128)(2,1)S(1)}, bf16[2,2,1,1,1,24,1664]{6,5,4,3,2,1,0:T(8,128)(2,1)S(1)}, u32[]{:S(2)}, u32[]{:S(2)}) collective-permute-start(bf16[2,2,1,1,1,24,1664]{6,5,4,3,2,1,0:T(8,128)(2,1)S(1)} %pad_maximum_fusion.14), channel_id=1, source_target_pairs={{0,1},{1,0},{2,3},{3,2},{4,5},{5,4},{6,7},{7,6},{8,9},{9,8},{10,11... | collective-permute-start | bytes 958472 | tf_op jit(solution)/shard_map/ppermute | solution.py:549
  37.5 13.1 %collective-permute-start.3 = (bf16[2,2,2,1,1,24,1536]{6,5,4,3,2,1,0:T(8,128)(2,1)S(1)}, bf16[2,2,2,1,1,24,1536]{6,5,4,3,2,1,0:T(8,128)(2,1)S(1)}, u32[]{:S(2)}, u32[]{:S(2)}) collective-permute-start(bf16[2,2,2,1,1,24,1536]{6,5,4,3,2,1,0:T(8,128)(2,1)S(1)} %pad_maximum_fusion.11), channel_id=1, source_target_pairs={{0,1},{1,0},{2,3},{3,2},{4,5},{5,4},{6,7},{7,6},{8,9},{9,8},{10,11... | collective-permute-start | bytes 1769480 | tf_op jit(solution)/shard_map/ppermute | solution.py:549
  38.9 14.3 %collective-permute-start.11 = (bf16[2,2,1,1,2,24,1664]{6,5,4,3,2,1,0:T(8,128)(2,1)S(1)}, bf16[2,2,1,1,2,24,1664]{6,5,4,3,2,1,0:T(8,128)(2,1)S(1)}, u32[]{:S(2)}, u32[]{:S(2)}) collective-permute-start(bf16[2,2,1,1,2,24,1664]{6,5,4,3,2,1,0:T(8,128)(2,1)S(1)} %pad_maximum_fusion.10), channel_id=1, source_target_pairs={{0,4},{2,6},{4,0},{6,2},{8,12},{10,14},{12,8},{14,10},{16,20},{18,... | collective-permute-start | bytes 1916936 | tf_op jit(solution)/shard_map/ppermute | solution.py:549
  50.8 20.9 %collective-permute-start.4 = (bf16[2,2,2,1,2,24,1536]{6,5,4,3,2,1,0:T(8,128)(2,1)S(1)}, bf16[2,2,2,1,2,24,1536]{6,5,4,3,2,1,0:T(8,128)(2,1)S(1)}, u32[]{:S(2)}, u32[]{:S(2)}) collective-permute-start(bf16[2,2,2,1,2,24,1536]{6,5,4,3,2,1,0:T(8,128)(2,1)S(1)} %pad_maximum_fusion.7), channel_id=1, source_target_pairs={{0,2},{2,0},{4,6},{6,4},{8,10},{10,8},{12,14},{14,12},{16,18},{18,... | collective-permute-start | bytes 3538952 | tf_op jit(solution)/shard_map/ppermute | solution.py:549
  50.8 15.7 %collective-permute-start.7 = (bf16[2,2,1,1,1,24,3072]{6,5,4,3,2,1,0:T(8,128)(2,1)S(1)}, bf16[2,2,1,1,1,24,3072]{6,5,4,3,2,1,0:T(8,128)(2,1)S(1)}, u32[]{:S(2)}, u32[]{:S(2)}) collective-permute-start(bf16[2,2,1,1,1,24,3072]{6,5,4,3,2,1,0:T(8,128)(2,1)S(1)} %pad_maximum_fusion.12), channel_id=1, source_target_pairs={{0,4},{2,6},{4,0},{6,2},{8,12},{10,14},{12,8},{14,10},{16,20},{18,... | collective-permute-start | bytes 1769480 | tf_op jit(solution)/shard_map/ppermute | solution.py:549
  53.5 20.0 %collective-permute-start.12 = (bf16[2,2,2,1,2,24,1664]{6,5,4,3,2,1,0:T(8,128)(2,1)S(1)}, bf16[2,2,2,1,2,24,1664]{6,5,4,3,2,1,0:T(8,128)(2,1)S(1)}, u32[]{:S(2)}, u32[]{:S(2)}) collective-permute-start(bf16[2,2,2,1,2,24,1664]{6,5,4,3,2,1,0:T(8,128)(2,1)S(1)} %pad_maximum_fusion.6), channel_id=1, source_target_pairs={{0,2},{2,0},{4,6},{6,4},{8,10},{10,8},{12,14},{14,12},{16,18},{18,... | collective-permute-start | bytes 3833864 | tf_op jit(solution)/shard_map/ppermute | solution.py:549
  53.6 15.9 %collective-permute-start.15 = (bf16[2,2,1,1,1,96,768]{6,5,4,3,2,1,0:T(8,128)(2,1)S(1)}, bf16[2,2,1,1,1,96,768]{6,5,4,3,2,1,0:T(8,128)(2,1)S(1)}, u32[]{:S(2)}, u32[]{:S(2)}) collective-permute-start(bf16[2,2,1,1,1,96,768]{6,5,4,3,2,1,0:T(8,128)(2,1)S(1)} %pad_maximum_fusion.13), channel_id=1, source_target_pairs={{0,1},{1,0},{2,3},{3,2},{4,5},{5,4},{6,7},{7,6},{8,9},{9,8},{10,11... | collective-permute-start | bytes 1769480 | tf_op jit(solution)/shard_map/ppermute | solution.py:549
  66.8 29.9 %collective-permute-start.16 = (bf16[2,2,2,1,1,24,3072]{6,5,4,3,2,1,0:T(8,128)(2,1)S(1)}, bf16[2,2,2,1,1,24,3072]{6,5,4,3,2,1,0:T(8,128)(2,1)S(1)}, u32[]{:S(2)}, u32[]{:S(2)}) collective-permute-start(bf16[2,2,2,1,1,24,3072]{6,5,4,3,2,1,0:T(8,128)(2,1)S(1)} %pad_maximum_fusion.8), channel_id=1, source_target_pairs={{0,1},{1,0},{2,3},{3,2},{4,5},{5,4},{6,7},{7,6},{8,9},{9,8},{10,11... | collective-permute-start | bytes 3538952 | tf_op jit(solution)/shard_map/ppermute | solution.py:549
  71.5 29.3 %collective-permute-start.18 = (bf16[2,2,1,1,2,96,768]{6,5,4,3,2,1,0:T(8,128)(2,1)}, bf16[2,2,1,1,2,96,768]{6,5,4,3,2,1,0:T(8,128)(2,1)}, u32[]{:S(2)}, u32[]{:S(2)}) collective-permute-start(bf16[2,2,1,1,2,96,768]{6,5,4,3,2,1,0:T(8,128)(2,1)} %pad_maximum_fusion.9), channel_id=1, source_target_pairs={{0,4},{2,6},{4,0},{6,2},{8,12},{10,14},{12,8},{14,10},{16,20},{18,... | collective-permute-start | bytes 3538952 | tf_op jit(solution)/shard_map/ppermute | solution.py:549
  233.1 10.9 %collective-permute-start.21 = (bf16[3072,384]{1,0:T(8,128)(2,1)}, bf16[3072,384]{1,0:T(8,128)(2,1)}, u32[]{:S(2)}, u32[]{:S(2)}) collective-permute-start(bf16[3072,384]{1,0:T(8,128)(2,1)} %get-tuple-element.157), channel_id=1, source_target_pairs={{0,2},{2,0},{4,6},{6,4},{8,10},{10,8},{12,14},{14,12},{16,18},{18,... | collective-permute-start | bytes 7077896 | tf_op jit(solution)/shard_map/ppermute | solution.py:549
  247.2 31.7 %collective-permute-start.23 = (bf16[2,2,1,2,2,96,384]{6,5,4,3,2,1,0:T(8,128)(2,1)S(1)}, bf16[2,2,1,2,2,96,384]{6,5,4,3,2,1,0:T(8,128)(2,1)}, u32[]{:S(2)}, u32[]{:S(2)}) collective-permute-start(bf16[2,2,1,2,2,96,384]{6,5,4,3,2,1,0:T(8,128)(2,1)S(1)} %constant_dynamic-slice_fusion.27), channel_id=1, source_target_pairs={{0,4},{2,6},{4,0},{6,2},{8,12},{10,14},{12,8},{14,10},{16,20},{18,... | collective-permute-start | bytes 3538952 | tf_op jit(solution)/shard_map/ppermute | solution.py:549
  253.5 28.3 %collective-permute-start.22 = (bf16[2,2,2,2,1,24,1536]{6,5,4,3,2,1,0:T(8,128)(2,1)}, bf16[2,2,2,2,1,24,1536]{6,5,4,3,2,1,0:T(8,128)(2,1)}, u32[]{:S(2)}, u32[]{:S(2)}) collective-permute-start(bf16[2,2,2,2,1,24,1536]{6,5,4,3,2,1,0:T(8,128)(2,1)} %constant_dynamic-slice_fusion.28), channel_id=1, source_target_pairs={{0,1},{1,0},{2,3},{3,2},{4,5},{5,4},{6,7},{7,6},{8,9},{9,8},{10,11... | collective-permute-start | bytes 3538952 | tf_op jit(solution)/shard_map/ppermute | solution.py:549
  283.5 14.7 %collective-permute-start.27 = (bf16[2,2,1,2,1,96,384]{6,5,4,3,2,1,0:T(8,128)(2,1)S(1)}, bf16[2,2,1,2,1,96,384]{6,5,4,3,2,1,0:T(8,128)(2,1)}, u32[]{:S(2)}, u32[]{:S(2)}) collective-permute-start(bf16[2,2,1,2,1,96,384]{6,5,4,3,2,1,0:T(8,128)(2,1)S(1)} %constant_dynamic-slice_fusion.25), channel_id=1, source_target_pairs={{0,1},{1,0},{2,3},{3,2},{4,5},{5,4},{6,7},{7,6},{8,9},{9,8},{10,11... | collective-permute-start | bytes 1769480 | tf_op jit(solution)/shard_map/ppermute | solution.py:549
  285.1 15.1 %collective-permute-start.26 = (bf16[2,2,1,2,1,24,1536]{6,5,4,3,2,1,0:T(8,128)(2,1)S(1)}, bf16[2,2,1,2,1,24,1536]{6,5,4,3,2,1,0:T(8,128)(2,1)}, u32[]{:S(2)}, u32[]{:S(2)}) collective-permute-start(bf16[2,2,1,2,1,24,1536]{6,5,4,3,2,1,0:T(8,128)(2,1)S(1)} %constant_dynamic-slice_fusion.26), channel_id=1, source_target_pairs={{0,4},{2,6},{4,0},{6,2},{8,12},{10,14},{12,8},{14,10},{16,20},{18,... | collective-permute-start | bytes 1769480 | tf_op jit(solution)/shard_map/ppermute | solution.py:549
  304.6 17.5 %collective-permute-start.28 = (bf16[2,2,2,2,1,24,768]{6,5,4,3,2,1,0:T(8,128)(2,1)}, bf16[2,2,2,2,1,24,768]{6,5,4,3,2,1,0:T(8,128)(2,1)}, u32[]{:S(2)}, u32[]{:S(2)}) collective-permute-start(bf16[2,2,2,2,1,24,768]{6,5,4,3,2,1,0:T(8,128)(2,1)} %constant_dynamic-slice_fusion.24), channel_id=1, source_target_pairs={{0,1},{1,0},{2,3},{3,2},{4,5},{5,4},{6,7},{7,6},{8,9},{9,8},{10,11... | collective-permute-start | bytes 1769480 | tf_op jit(solution)/shard_map/ppermute | solution.py:549
  306.3 15.8 %collective-permute-start.29 = (bf16[2,2,1,2,2,24,768]{6,5,4,3,2,1,0:T(8,128)(2,1)S(1)}, bf16[2,2,1,2,2,24,768]{6,5,4,3,2,1,0:T(8,128)(2,1)}, u32[]{:S(2)}, u32[]{:S(2)}) collective-permute-start(bf16[2,2,1,2,2,24,768]{6,5,4,3,2,1,0:T(8,128)(2,1)S(1)} %constant_dynamic-slice_fusion.23), channel_id=1, source_target_pairs={{0,4},{2,6},{4,0},{6,2},{8,12},{10,14},{12,8},{14,10},{16,20},{18,... | collective-permute-start | bytes 1769480 | tf_op jit(solution)/shard_map/ppermute | solution.py:549
  308.3 13.8 %collective-permute-start.31 = (bf16[2,1,1,2,1,96,384]{6,5,4,3,2,1,0:T(8,128)(2,1)}, bf16[2,1,1,2,1,96,384]{6,5,4,3,2,1,0:T(8,128)(2,1)S(1)}, u32[]{:S(2)}, u32[]{:S(2)}) collective-permute-start(bf16[2,1,1,2,1,96,384]{6,5,4,3,2,1,0:T(8,128)(2,1)} %constant_dynamic-slice_fusion.21), channel_id=1, source_target_pairs={{0,8},{2,10},{4,12},{6,14},{8,0},{10,2},{12,4},{14,6},{16,24},{18,... | collective-permute-start | bytes 884744 | tf_op jit(solution)/shard_map/ppermute | solution.py:549
  325.5 19.7 %collective-permute-start.33 = (bf16[2,2,1,2,1,24,768]{6,5,4,3,2,1,0:T(8,128)(2,1)S(1)}, bf16[2,2,1,2,1,24,768]{6,5,4,3,2,1,0:T(8,128)(2,1)S(1)}, u32[]{:S(2)}, u32[]{:S(2)}) collective-permute-start(bf16[2,2,1,2,1,24,768]{6,5,4,3,2,1,0:T(8,128)(2,1)S(1)} %constant_dynamic-slice_fusion.19), channel_id=1, source_target_pairs={{0,4},{2,6},{4,0},{6,2},{8,12},{10,14},{12,8},{14,10},{16,20},{18,... | collective-permute-start | bytes 884744 | tf_op jit(solution)/shard_map/ppermute | solution.py:549
  327.2 18.0 %collective-permute-start.34 = (bf16[2,2,1,2,1,24,768]{6,5,4,3,2,1,0:T(8,128)(2,1)S(1)}, bf16[2,2,1,2,1,24,768]{6,5,4,3,2,1,0:T(8,128)(2,1)S(1)}, u32[]{:S(2)}, u32[]{:S(2)}) collective-permute-start(bf16[2,2,1,2,1,24,768]{6,5,4,3,2,1,0:T(8,128)(2,1)S(1)} %constant_dynamic-slice_fusion.18), channel_id=1, source_target_pairs={{0,1},{1,0},{2,3},{3,2},{4,5},{5,4},{6,7},{7,6},{8,9},{9,8},{10,11... | collective-permute-start | bytes 884744 | tf_op jit(solution)/shard_map/ppermute | solution.py:549
  327.5 17.6 %collective-permute-start.35 = (f32[2,2,2,1,1,1,288]{6,4,3,2,1,0,5:T(1,128)S(1)}, f32[2,2,2,1,1,1,288]{6,4,3,2,1,0,5:T(1,128)S(1)}, u32[]{:S(2)}, u32[]{:S(2)}) collective-permute-start(f32[2,2,2,1,1,1,288]{6,4,3,2,1,0,5:T(1,128)S(1)} %constant_dynamic-slice_fusion.17), channel_id=1, source_target_pairs={{0,1},{1,0},{2,3},{3,2},{4,5},{5,4},{6,7},{7,6},{8,9},{9,8},{10,11... | collective-permute-start | bytes 27656 | tf_op jit(solution)/shard_map/ppermute | solution.py:549
  329.3 12.3 %collective-permute-start.43 = (bf16[1,1,1,2,1,24,1536]{6,5,4,3,2,1,0:T(8,128)(2,1)S(1)}, bf16[1,1,1,2,1,24,1536]{6,5,4,3,2,1,0:T(8,128)(2,1)S(1)}, u32[]{:S(2)}, u32[]{:S(2)}) collective-permute-start(bf16[1,1,1,2,1,24,1536]{6,5,4,3,2,1,0:T(8,128)(2,1)S(1)} %constant_dynamic-slice_fusion.8), channel_id=1, source_target_pairs={{0,16},{2,18},{4,20},{6,22},{8,24},{10,26},{12,28},{14,30},{16,0},... | collective-permute-start | bytes 442376 | tf_op jit(solution)/shard_map/ppermute | solution.py:549
  332.8 10.9 %collective-permute-start.45 = (bf16[1,1,1,2,1,96,384]{6,5,4,3,2,1,0:T(8,128)(2,1)S(1)}, bf16[1,1,1,2,1,96,384]{6,5,4,3,2,1,0:T(8,128)(2,1)S(1)}, u32[]{:S(2)}, u32[]{:S(2)}) collective-permute-start(bf16[1,1,1,2,1,96,384]{6,5,4,3,2,1,0:T(8,128)(2,1)S(1)} %constant_dynamic-slice_fusion.6), channel_id=1, source_target_pairs={{0,16},{2,18},{4,20},{6,22},{8,24},{10,26},{12,28},{14,30},{16,0},... | collective-permute-start | bytes 442376 | tf_op jit(solution)/shard_map/ppermute | solution.py:549
  (50 other events, 334.3 us)

commit v3 on v2

--- a/solution.py
+++ b/solution.py
@@ -28,6 +28,7 @@
 F32 = jnp.float32
 BF16 = jnp.bfloat16
 VMEM_LIMIT = 60 * 1024 * 1024
+MID_LIMIT = 63 * 1024 * 1024
 
 
 def nt(a, b):
@@ -206,149 +207,9 @@
     )(count, *prev, tok, mem, wqk, wqk, wvo, wvo, vecs, vecs)
 
 
-def ffn_fwd_kernel(
-    count_ref, xhat_ref, wi_ref, bi_ref, wo_ref, vec_ref,
-    h1b_ref, g_ref, gp_ref, mixed_ref, write_ref, xhat2_ref, rstd2_ref,
-    acc_s,
-):
-    step = pl.program_id(0)
-
-    @pl.when(step == 0)
-    def _():
-        h1b_ref[...] = (xhat_ref[...] * vec_ref[3:4, :] + vec_ref[4:5, :]).astype(BF16)
-
-    f1 = nn(h1b_ref[...], wi_ref[...]) + bi_ref[...]
-    cdf = 0.5 * (1.0 + lax.erf(f1 * math.sqrt(0.5)))
-    pdf = jnp.exp(-0.5 * f1 * f1) * (1.0 / math.sqrt(2.0 * math.pi))
-    g = (f1 * cdf).astype(BF16)
-    g_ref[...] = g
-    gp_ref[...] = (cdf + f1 * pdf).astype(BF16)
-    part = nn(g, wo_ref[...])
-
-    @pl.when(step == 0)
-    def _():
-        acc_s[...] = part
-
-    @pl.when(step > 0)
-    def _():
-        acc_s[...] = acc_s[...] + part
-
-    @pl.when(step == NF - 1)
-    def _():
-        h1 = xhat_ref[...] * vec_ref[3:4, :] + vec_ref[4:5, :]
-        r = h1 + (acc_s[...] + vec_ref[5:6, :])
-        c = r - row_mean(r)
-        rstd = lax.rsqrt(row_mean(c * c) + EPS)
-        xhat = c * rstd
-        xhat2_ref[...] = xhat
-        rstd2_ref[...] = jnp.broadcast_to(rstd, (R, 128))
-        y = xhat * vec_ref[6:7, :] + vec_ref[7:8, :]
-        live = row_ids(SEG, D) < count_ref[0]
-        mixed_ref[...] = jnp.where(live, y[0:SEG, :], 0.0).astype(BF16)
-        write_ref[...] = jnp.where(row_ids(MPAD, D) < MEM, y[SEG:R, :], 0.0)
-
-
-def ffn_fwd(slot, slots, prev, count, xhat, wi, bi, wo, vecs):
-    n = len(prev)
-    return pl.pallas_call(
-        kept(n, ffn_fwd_kernel),
-        grid_spec=pltpu.PrefetchScalarGridSpec(
-            num_scalar_prefetch=1,
-            grid=(NF,),
-            in_specs=[any_spec()] * n + [const((R, D)), cols(D, BF), cols(1, BF), rows(BF, D), const((8, D))],
-            out_specs=[
-                slot_const(slot), slot_cols(slot, BF), cols(R, BF),
-                pl.BlockSpec((SEG, D), lambda j, *_: (slot, 0)), const((MPAD, D)),
-                const((R, D)), const((R, 128)),
-            ],
-            scratch_shapes=[pltpu.VMEM((R, D), F32)],
-        ),
-        out_shape=[
-            sds((slots * R, D), BF16), sds((slots * R, FF), BF16), sds((R, FF), BF16),
-            sds((slots * SEG, D), BF16),
-            sds((MPAD, D), F32), sds((R, D), F32), sds((R, 128), F32),
-        ],
-        input_output_aliases={1: 0, 2: 1, 3: 3} if n else {},
-        compiler_params=params(),
-        cost_estimate=cost(2 * R * 2 * D * FF * 2, 20_000_000),
-        name="ffn_fwd",
-    )(count, *prev, xhat, wi, bi, wo, vecs)
-
-
 def norm_pull(grad, gain, xhat, rstd):
     gx = grad * gain
     return rstd * (gx - row_mean(gx) - xhat * row_mean(gx * xhat))
-
-
-def ffn_bwd_kernel(
-    count_ref, cot_ref, gw_ref, xhat2_ref, rstd2_ref, xhat_ref, rstd_ref, wi_ref, wo_ref,
-    gp_ref, vec_ref,
-    df2_ref, df1_ref, dr1_ref, dr1b_ref, dbi_ref, dvec_ref,
-    acc_s,
-):
-    step = pl.program_id(0)
-
-    @pl.when(step == 0)
-    def _():
-        live = row_ids(SEG, D) < count_ref[0]
-        acc_s[0:SEG, :] = jnp.where(live, cot_ref[...].astype(F32), 0.0)
-        acc_s[SEG:R, :] = gw_ref[...]
-        dy = acc_s[...]
-        xhat2 = xhat2_ref[...]
-        dvec_ref[6:7, :] = col_sum(dy * xhat2)
-        dvec_ref[7:8, :] = col_sum(dy)
-        dr2 = norm_pull(dy, vec_ref[6:7, :], xhat2, rstd2_ref[:, 0:1])
-        df2 = dr2.astype(BF16)
-        df2_ref[...] = df2
-        dvec_ref[5:6, :] = col_sum(df2.astype(F32))
-        acc_s[...] = dr2
-
-    df1 = (nt(df2_ref[...], wo_ref[...]) * gp_ref[...].astype(F32)).astype(BF16)
-    df1_ref[...] = df1
-    dbi_ref[...] = col_sum(df1.astype(F32))
-    acc_s[...] = acc_s[...] + nt(df1, wi_ref[...])
-
-    @pl.when(step == NF - 1)
-    def _():
-        dh1 = acc_s[...]
-        xhat = xhat_ref[...]
-        dvec_ref[3:4, :] = col_sum(dh1 * xhat)
-        dvec_ref[4:5, :] = col_sum(dh1)
-        dr1 = norm_pull(dh1, vec_ref[3:4, :], xhat, rstd_ref[:, 0:1])
-        dr1_ref[...] = dr1
-        dr1b = dr1.astype(BF16)
-        dr1b_ref[...] = dr1b
-        dvec_ref[2:3, :] = col_sum(dr1b.astype(F32))
-        dvec_ref[0:2, :] = jnp.zeros((2, D), F32)
-
-
-def ffn_bwd(slot, slots, prev, count, cot, gw, xhat2, rstd2, xhat, rstd, wi, wo, gp, vecs):
-    n = len(prev)
-    return pl.pallas_call(
-        kept(n, ffn_bwd_kernel),
-        grid_spec=pltpu.PrefetchScalarGridSpec(
-            num_scalar_prefetch=1,
-            grid=(NF,),
-            in_specs=[any_spec()] * n + [
-                pl.BlockSpec((SEG, D), lambda j, *_: (slot, 0)), const((MPAD, D)), const((R, D)), const((R, 128)),
-                const((R, D)), const((R, 128)), cols(D, BF), rows(BF, D), cols(R, BF),
-                const((8, D)),
-            ],
-            out_specs=[
-                slot_const(slot), slot_cols(slot, BF), const((R, D)), slot_const(slot),
-                cols(1, BF), const((8, D)),
-            ],
-            scratch_shapes=[pltpu.VMEM((R, D), F32)],
-        ),
-        out_shape=[
-            sds((slots * R, D), BF16), sds((slots * R, FF), BF16), sds((R, D), F32),
-            sds((slots * R, D), BF16), sds((1, FF), F32), sds((8, D), F32),
-        ],
-        input_output_aliases={1: 0, 2: 1, 3: 3} if n else {},
-        compiler_params=params(),
-        cost_estimate=cost(2 * R * 2 * D * FF * 2, 20_000_000),
-        name="ffn_bwd",
-    )(count, *prev, cot, gw, xhat2, rstd2, xhat, rstd, wi, wo, gp, vecs)
 
 
 def attn_bwd_kernel(
@@ -443,6 +304,299 @@
     )(count, *prev, dr1, dr1b, wqk, wqk, wvo, wvo, q, k, v, o, linv, e)
 
 
+MID_BF = 512
+
+
+def mid_kernel(
+    info_ref, xhat0_ref, rstd0_ref, init_ref, vec_ref, bi_ref,
+    wqk_hbm, wvo_hbm, wi_hbm, wu_hbm, tok_hbm, cot_hbm, hb_in, o_in,
+    mixed_hbm, hb_hbm, o_hbm, h1b_hbm, g_hbm, df2_hbm, df1_hbm, da_hbm,
+    dq_hbm, dk_hbm, dv_hbm, gtok_hbm, dr1_hbm, gmem_ref, dvec_ref, dbi_ref,
+    wqk_s, wvo_s, wi_s, wu_s, gp_s, g_s, xhat_s, xhat2_s, rstd_s, rstd2_s, h1b_s,
+    hb_s, q_s, k_s, v_s, o_s, linv_s, e_s, h_s, acc_s, df2_s, da_s, tok_s, cot_s, mixed_s, mem_s,
+    sems,
+):
+    used = [0]
+
+    def copy(src, dst):
+        used[0] += 1
+        return pltpu.make_async_copy(src, dst, sems.at[used[0] - 1])
+
+    half = FF // 2
+    in_wi = [
+        copy(wi_hbm.at[:, half * i : half * i + half], wi_s.at[:, half * i : half * i + half])
+        for i in range(2)
+    ]
+    in_wu = [
+        copy(wu_hbm.at[half * i : half * i + half], wu_s.at[half * i : half * i + half])
+        for i in range(2)
+    ]
+    in_tok = copy(tok_hbm.at[SEG : 2 * SEG], tok_s)
+    in_wqk = copy(wqk_hbm, wqk_s)
+    in_wvo = copy(wvo_hbm.at[:, 0 : 2 * D], wvo_s)
+    in_cot1 = copy(cot_hbm.at[SEG : 2 * SEG], cot_s)
+    for c in (in_wi[0], in_wu[0], in_wi[1], in_wu[1], in_tok, in_wqk, in_wvo, in_cot1):
+        c.start()
+    xhat_s[0] = xhat0_ref[...]
+    rstd_s[0] = rstd0_ref[...]
+    k_s[R:KEYS, :] = jnp.zeros((KEYS - R, D), BF16)
+    v_s[R:KEYS, :] = jnp.zeros((KEYS - R, D), BF16)
+    first = lax.broadcasted_iota(jnp.int32, (1, 128), 1) < HEAD_DIM
+    one = jnp.ones((KEYS, 128), BF16)
+
+    def row(i):
+        return vec_ref[i : i + 1, :]
+
+    def lanes(start, size):
+        return pl.ds(pl.multiple_of(start, size), size)
+
+    def feed_forward(seg):
+        h1 = xhat_s[seg] * row(3) + row(4)
+        h1b_s[...] = h1.astype(BF16)
+        acc_s[...] = h1 + row(5)
+
+        def chunk(j, carry):
+            at = lanes(j * MID_BF, MID_BF)
+            f1 = nn(h1b_s[...], wi_s[:, at]) + bi_ref[:, at]
+            cdf = 0.5 * (1.0 + lax.erf(f1 * math.sqrt(0.5)))
+            pdf = jnp.exp(-0.5 * f1 * f1) * (1.0 / math.sqrt(2.0 * math.pi))
+            g = (f1 * cdf).astype(BF16)
+            g_s[:, at] = g
+            gp_s[seg, :, at] = (cdf + f1 * pdf).astype(BF16)
+            acc_s[...] = acc_s[...] + nn(g, wu_s[at, :])
+            return carry
+
+        n = half // MID_BF
+        if seg == 0:
+            in_wi[0].wait()
+            in_wu[0].wait()
+        lax.fori_loop(0, n, chunk, 0)
+        if seg == 0:
+            in_wi[1].wait()
+            in_wu[1].wait()
+        lax.fori_loop(n, 2 * n, chunk, 0)
+        r = acc_s[...]
+        c = r - row_mean(r)
+        rstd = lax.rsqrt(row_mean(c * c) + EPS)
+        xhat = c * rstd
+        xhat2_s[seg] = xhat
+        rstd2_s[seg] = jnp.broadcast_to(rstd, (R, 128))
+        y = xhat * row(6) + row(7)
+        live = row_ids(SEG, D) < info_ref[seg]
+        mixed_s[...] = jnp.where(live, y[0:SEG, :], 0.0).astype(BF16)
+        if seg == 0:
+            write = jnp.where(row_ids(MPAD, D) < MEM, y[SEG:R, :], 0.0)
+            mem_s[...] = jnp.where(info_ref[2] > 0, init_ref[...], write)
+
+    def feed_forward_back(seg, grad_write):
+        live = row_ids(SEG, D) < info_ref[seg]
+        acc_s[0:SEG, :] = jnp.where(live, cot_s[...].astype(F32), 0.0)
+        acc_s[SEG:R, :] = grad_write
+        dy = acc_s[...]
+        xhat2 = xhat2_s[seg]
+        sums = [col_sum(dy * xhat2), col_sum(dy)]
+        dr2 = norm_pull(dy, row(6), xhat2, rstd2_s[seg, :, 0:1])
+        df2 = dr2.astype(BF16)
+        df2_s[...] = df2
+        sums.insert(0, col_sum(df2.astype(F32)))
+        acc_s[...] = dr2
+
+        def chunk(j, carry):
+            at = lanes(j * MID_BF, MID_BF)
+            df1 = (nt(df2_s[...], wu_s[at, :]) * gp_s[seg, :, at].astype(F32)).astype(BF16)
+            gp_s[seg, :, at] = df1
+            total = col_sum(df1.astype(F32))
+            dbi_ref[:, at] = total if seg == 1 else dbi_ref[:, at] + total
+            acc_s[...] = acc_s[...] + nt(df1, wi_s[:, at])
+            return carry
+
+        lax.fori_loop(0, FF // MID_BF, chunk, 0)
+        dh1 = acc_s[...]
+        xhat = xhat_s[seg]
+        sums = [col_sum(dh1 * xhat), col_sum(dh1)] + sums
+        dr1 = norm_pull(dh1, row(3), xhat, rstd_s[seg, :, 0:1])
+        acc_s[...] = dr1
+        da = dr1.astype(BF16)
+        da_s[...] = da
+        sums = [col_sum(da.astype(F32))] + sums
+        for i, total in enumerate(sums):
+            at = slice(2 + i, 3 + i)
+            dvec_ref[at, :] = total if seg == 1 else dvec_ref[at, :] + total
+
+    feed_forward(0)
+    outs = {}
+
+    def send(name, src, dst):
+        outs[name] = copy(src, dst)
+        outs[name].start()
+
+    def done(*names):
+        for name in names:
+            outs.pop(name).wait()
+
+    send("h1b0", h1b_s, h1b_hbm.at[0:R])
+    send("g0", g_s, g_hbm.at[0:R])
+    send("mixed0", mixed_s, mixed_hbm.at[0:SEG])
+
+    in_tok.wait()
+    live = row_ids(SEG, D) < info_ref[1]
+    h_s[0:SEG, :] = jnp.where(live, tok_s[...].astype(F32), 0.0)
+    h_s[SEG:R, :] = mem_s[...]
+    hb_s[...] = h_s[...].astype(BF16)
+    send("hb", hb_s, hb_hbm.at[R : 2 * R])
+    in_wqk.wait()
+    in_wvo.wait()
+    acc_s[...] = h_s[...] + row(2)
+    key = lax.broadcasted_iota(jnp.int32, (1, KEYS), 1)
+    bias = jnp.where(key < info_ref[1], 0.0, NEG)
+    twice = math.log(2.0) * math.sqrt(HEAD_DIM)
+    bias = jnp.where((key >= SEG) & (key < SEG + MEM), twice, bias)
+
+    def quad_forward(j, carry):
+        at = lanes(j * QUAD, QUAD)
+        hb = hb_s[...]
+        q_s[:, at] = (nn(hb, wqk_s[:, at]) + vec_ref[0:1, at]).astype(BF16)
+        k_s[0:R, at] = nn(hb, wqk_s[:, lanes(D + j * QUAD, QUAD)]).astype(BF16)
+        v_s[0:R, at] = (nn(hb, wvo_s[:, at]) + vec_ref[1:2, at]).astype(BF16)
+        for pair in range(2):
+            here = lanes(j * QUAD + 128 * pair, 128)
+            q2 = q_s[:, here]
+            k2 = k_s[:, here]
+            vx = jnp.concatenate([v_s[:, here], one], axis=1)
+            parts = []
+            for side in range(2):
+                mine = first if side == 0 else jnp.logical_not(first)
+                s = nt(jnp.where(mine, q2, jnp.zeros_like(q2)), k2) + bias
+                top = jnp.max(s, axis=-1, keepdims=True)
+                e = jnp.exp2((s - top) * EXP_SCALE).astype(BF16)
+                e_s[4 * j + 2 * pair + side] = e
+                parts.append(nn(e, vx))
+            num = jnp.where(first, parts[0][:, :128], parts[1][:, :128])
+            den = jnp.where(first, parts[0][:, 128:], parts[1][:, 128:])
+            inv = 1.0 / den
+            linv_s[:, here] = inv
+            o_s[:, here] = (num * inv).astype(BF16)
+        acc_s[...] = acc_s[...] + nn(o_s[:, at], wvo_s[at, D : 2 * D])
+        return carry
+
+    lax.fori_loop(0, NQ, quad_forward, 0)
+    send("o", o_s, o_hbm.at[R : 2 * R])
+    r = acc_s[...]
+    c = r - row_mean(r)
+    rstd = lax.rsqrt(row_mean(c * c) + EPS)
+    xhat_s[1] = c * rstd
+    rstd_s[1] = jnp.broadcast_to(rstd, (R, 128))
+
+    done("h1b0", "g0", "mixed0")
+    feed_forward(1)
+    send("h1b1", h1b_s, h1b_hbm.at[R : 2 * R])
+    send("g1", g_s, g_hbm.at[R : 2 * R])
+    send("mixed1", mixed_s, mixed_hbm.at[SEG : 2 * SEG])
+
+    in_cot1.wait()
+    feed_forward_back(1, jnp.zeros((MPAD, D), F32))
+    in_cot0 = copy(cot_hbm.at[0:SEG], cot_s)
+    in_cot0.start()
+    send("df2", df2_s, df2_hbm.at[R : 2 * R])
+    send("df1", gp_s.at[1], df1_hbm.at[R : 2 * R])
+    send("da", da_s, da_hbm.at[R : 2 * R])
+
+    scaling = 1.0 / math.sqrt(HEAD_DIM)
+    done("hb", "o")
+
+    def quad_back(j, carry):
+        at = lanes(j * QUAD, QUAD)
+        grad_o = nt(da_s[...], wvo_s[at, D : 2 * D]).astype(BF16).astype(F32) * linv_s[:, at]
+        grad_ob = grad_o.astype(BF16)
+        term = (-(grad_o * o_s[:, at].astype(F32))).astype(BF16)
+        for pair in range(2):
+            here = lanes(j * QUAD + 128 * pair, 128)
+            part = slice(128 * pair, 128 * pair + 128)
+            q2 = q_s[:, here]
+            k2 = k_s[:, here]
+            do2 = grad_ob[:, part]
+            tm2 = term[:, part]
+            vx = jnp.concatenate([v_s[:, here], one], axis=1)
+            dqs, dks, dvs = [], [], []
+            for side in range(2):
+                mine = first if side == 0 else jnp.logical_not(first)
+                zero = jnp.zeros_like(do2)
+                lhs = jnp.concatenate(
+                    [jnp.where(mine, do2, zero), jnp.where(mine, tm2, zero)], axis=1
+                )
+                e = e_s[4 * j + 2 * pair + side]
+                ds = (nt(lhs, vx) * e.astype(F32)).astype(BF16)
+                dqs.append(nn(ds, k2))
+                dks.append(tn(ds, q2))
+                dvs.append(tn(e, do2))
+            q_s[:, here] = (jnp.where(first, dqs[0], dqs[1]) * scaling).astype(BF16)
+            k_s[0:R, here] = (jnp.where(first, dks[0], dks[1])[0:R, :] * scaling).astype(BF16)
+            v_s[0:R, here] = jnp.where(first, dvs[0], dvs[1])[0:R, :].astype(BF16)
+        dq = q_s[:, at]
+        dk = k_s[0:R, at]
+        dv = v_s[0:R, at]
+        dvec_ref[0:1, at] = col_sum(dq.astype(F32))
+        dvec_ref[1:2, at] = col_sum(dv.astype(F32))
+        part = nt(dq, wqk_s[:, at]) + nt(dk, wqk_s[:, lanes(D + j * QUAD, QUAD)])
+        acc_s[...] = acc_s[...] + (part + nt(dv, wvo_s[:, at]))
+        return carry
+
+    lax.fori_loop(0, NQ, quad_back, 0)
+    send("dq", q_s, dq_hbm.at[R : 2 * R])
+    send("dk", k_s.at[0:R], dk_hbm.at[R : 2 * R])
+    send("dv", v_s.at[0:R], dv_hbm.at[R : 2 * R])
+    h_s[0:SEG, :] = jnp.where(live, acc_s[0:SEG, :], 0.0)
+    send("gtok", h_s.at[0:SEG], gtok_hbm.at[SEG : 2 * SEG])
+    grad_mem = jnp.where(row_ids(MPAD, D) < MEM, acc_s[SEG:R, :], 0.0)
+    gmem_ref[...] = grad_mem
+    in_cot0.wait()
+    done("df2", "da")
+    feed_forward_back(0, jnp.where(info_ref[2] > 0, 0.0, grad_mem))
+    send("df2", df2_s, df2_hbm.at[0:R])
+    send("df1b", gp_s.at[0], df1_hbm.at[0:R])
+    send("da", da_s, da_hbm.at[0:R])
+    send("dr1", acc_s, dr1_hbm)
+    done(*list(outs))
+
+
+def mid(info, xhat0, rstd0, init, vecs, bi, wqk, wvo, wi, wu, tok, cot, hb, o):
+    whole = pl.BlockSpec(memory_space=pltpu.VMEM)
+    smem = pl.BlockSpec(memory_space=pltpu.SMEM)
+    two = 2 * R
+    return pl.pallas_call(
+        mid_kernel,
+        in_specs=[smem] + [whole] * 5 + [any_spec()] * 8,
+        out_specs=[any_spec()] * 13 + [whole] * 3,
+        out_shape=[
+            sds((2 * SEG, D), BF16), sds((two, D), BF16), sds((two, D), BF16),
+            sds((two, D), BF16), sds((two, FF), BF16), sds((two, D), BF16),
+            sds((two, FF), BF16), sds((two, D), BF16), sds((two, D), BF16),
+            sds((two, D), BF16), sds((two, D), BF16), sds((2 * SEG, D), F32),
+            sds((R, D), F32), sds((MPAD, D), F32), sds((8, D), F32), sds((1, FF), F32),
+        ],
+        scratch_shapes=[
+            pltpu.VMEM((D, 2 * D), BF16), pltpu.VMEM((D, 2 * D), BF16),
+            pltpu.VMEM((D, FF), BF16), pltpu.VMEM((FF, D), BF16),
+            pltpu.VMEM((2, R, FF), BF16), pltpu.VMEM((R, FF), BF16),
+            pltpu.VMEM((2, R, D), F32), pltpu.VMEM((2, R, D), F32),
+            pltpu.VMEM((2, R, 128), F32), pltpu.VMEM((2, R, 128), F32),
+            pltpu.VMEM((R, D), BF16),
+            pltpu.VMEM((R, D), BF16), pltpu.VMEM((R, D), BF16), pltpu.VMEM((KEYS, D), BF16),
+            pltpu.VMEM((KEYS, D), BF16), pltpu.VMEM((R, D), BF16), pltpu.VMEM((R, D), F32),
+            pltpu.VMEM((HEADS, R, KEYS), BF16),
+            pltpu.VMEM((R, D), F32), pltpu.VMEM((R, D), F32),
+            pltpu.VMEM((R, D), BF16), pltpu.VMEM((R, D), BF16),
+            pltpu.VMEM((SEG, D), BF16), pltpu.VMEM((SEG, D), BF16), pltpu.VMEM((SEG, D), BF16),
+            pltpu.VMEM((MPAD, D), F32),
+            pltpu.SemaphoreType.DMA((32,)),
+        ],
+        input_output_aliases={12: 1, 13: 2},
+        compiler_params=pltpu.CompilerParams(vmem_limit_bytes=MID_LIMIT),
+        cost_estimate=cost(2 * R * 40 * D * D + 14 * R * KEYS * D * 4, 60_000_000),
+        name="mid",
+    )(info, xhat0, rstd0, init, vecs, bi, wqk, wvo, wi, wu, tok, cot, hb, o)
+
+
 def wgrad_inner_kernel(core_ref, h_ref, da_ref, db_ref, mine_ref, theirs_ref):
     mine_ref[...] = tn(h_ref[...], da_ref[...]).astype(BF16)
     theirs_ref[...] = tn(h_ref[...], db_ref[...]).astype(BF16)
@@ -640,56 +794,36 @@
     bi = vec_all[8 * D :].reshape(1, FF)
 
     init = jnp.pad(init_memory.astype(F32), ((0, 0), (0, MPAD - MEM), (0, 0)))
-    carry = jnp.zeros((MPAD, D), F32)
-    saved = []
-    hb = o = h1b = g = mixed = None
-    for s in range(slots):
-        count = true_count[s : s + 1]
-        memory = jnp.where(chain_start[s] > 0, init[s], carry)
-        prev = [hb, o] if s else []
-        hb, q, k, v, o, linv, e, xhat, rstd = attn_fwd(
-            s, slots, prev, count, tokens, memory, wqk, wvo, vecs
-        )
-        if s == 0:
-            wi = cube.join(wi, after(wi_got, xhat), cube.x)
-            wu = cube.join(wu, after(wu_got, xhat), cube.y)
-            wi = cube.grow(wi, cube.core).reshape(D, FF)
-            wu = cube.grow(wu, cube.core).reshape(FF, D)
-        prev = [h1b, g, mixed] if s else []
-        h1b, g, gp, mixed, carry, xhat2, rstd2 = ffn_fwd(
-            s, slots, prev, count, xhat, wi, bi, wu, vecs
-        )
-        saved.append((q, k, v, linv, e, xhat, rstd, gp, xhat2, rstd2))
-    back = jnp.zeros((MPAD, D), F32)
-    df2 = df1 = da = dq = dk = dv = grad_tokens = None
-    grad_init, vec_parts = [None] * slots, []
-    for s in reversed(range(slots)):
-        count = true_count[s : s + 1]
-        q, k, v, linv, e, xhat, rstd, gp, xhat2, rstd2 = saved[s]
-        prev = [df2, df1, da] if df2 is not None else []
-        df2, df1, dr1, da, dbi, dvec = ffn_bwd(
-            s, slots, prev, count, cotangent, back, xhat2, rstd2, xhat, rstd, wi, wu, gp, vecs
-        )
-        if s == 0:
-            outer = wgrad_outer(core, g, df2)
-            inner = wgrad_inner(core, after(h1b, outer), df1)
-            outer = cube.spread(cube.add(outer[0], cube.swap(outer[1], cube.core)))
-            inner = cube.spread(cube.add(inner[0], cube.swap(inner[1], cube.core)))
-            inner, inner_send = cube.split(inner, cube.x)
-            outer, outer_send = cube.split(outer, cube.y)
-            dr1 = after(dr1, inner_send, outer_send)
-            inner_got = cube.swap(inner_send, cube.x)
-            outer_got = cube.swap(outer_send, cube.y)
-        prev = [dq, dk, dv, grad_tokens] if dq is not None else []
-        dq, dk, dv, dqb, dvb, grad_tokens, gmem = attn_bwd(
-            s, slots, prev, count, dr1, da, wqk, wvo, q, k, v, o, linv, e
-        )
-        starts = chain_start[s] > 0
-        grad_init[s] = jnp.where(starts, gmem, 0.0)[:MEM]
-        back = jnp.where(starts, 0.0, gmem)
-        vec_parts.append(
-            jnp.concatenate([dqb, dvb, dvec[2:8].reshape(1, -1), dbi], axis=1)
-        )
+    count = true_count[0:1]
+    hb, q, k, v, o, linv, e, xhat, rstd = attn_fwd(
+        0, slots, [], count, tokens, init[0], wqk, wvo, vecs
+    )
+    wi = cube.join(wi, after(wi_got, xhat), cube.x)
+    wu = cube.join(wu, after(wu_got, xhat), cube.y)
+    wi = cube.grow(wi, cube.core).reshape(D, FF)
+    wu = cube.grow(wu, cube.core).reshape(FF, D)
+    info = jnp.concatenate([true_count, chain_start[1:2]])
+    (
+        mixed, hb, o, h1b, g, df2, df1, da, dq, dk, dv, grad_tokens, dr1, gmem, dvec, dbi,
+    ) = mid(info, xhat, rstd, init[1], vecs, bi, wqk, wvo, wi, wu, tokens, cotangent, hb, o)
+    grad_init = [None, jnp.where(chain_start[1] > 0, gmem, 0.0)[:MEM]]
+    outer = wgrad_outer(core, g, df2)
+    inner = wgrad_inner(core, after(h1b, outer), df1)
+    outer = cube.spread(cube.add(outer[0], cube.swap(outer[1], cube.core)))
+    inner = cube.spread(cube.add(inner[0], cube.swap(inner[1], cube.core)))
+    inner, inner_send = cube.split(inner, cube.x)
+    outer, outer_send = cube.split(outer, cube.y)
+    dr1 = after(dr1, inner_send, outer_send)
+    inner_got = cube.swap(inner_send, cube.x)
+    outer_got = cube.swap(outer_send, cube.y)
+    dq, dk, dv, dqb, dvb, grad_tokens, gmem = attn_bwd(
+        0, slots, [dq, dk, dv, grad_tokens], count, dr1, da, wqk, wvo, q, k, v, o, linv, e
+    )
+    grad_init[0] = gmem[:MEM]
+    vec_parts = [
+        jnp.concatenate([dvec.reshape(1, -1), dbi], axis=1),
+        jnp.concatenate([dqb, dvb, jnp.zeros((1, 6 * D + FF), F32)], axis=1),
+    ]
     inner = cube.add(inner, after(inner_got, dq))
     outer = cube.add(outer, after(outer_got, dq))
     inner, inner_send = cube.split(inner, cube.y)

time: 374 us -> 343 us (0.917)
  Pallas kernels: 173 us -> 141 us
  waiting for transfers between devices: 68 us -> 74.2 us
    pallas_call x2 -> x1, Pallas kernels: 42.7 us -> 21.1 us  [attn_bwd(): pl.pallas_call(kept(n, attn_bwd_kernel), grid_spec=pltpu.PrefetchScalarGr...]
    pallas_call x2 -> x1, Pallas kernels: 35.7 us -> 18.1 us  [attn_fwd(): pl.pallas_call(kept(n, attn_fwd_kernel), grid_spec=pltpu.PrefetchScalarGr...]
    pallas_call x4 -> x1, Pallas kernels: 62.9 us -> 70.5 us  [mid(): pl.pallas_call(mid_kernel, in_specs=[smem] + [whole] * 5 + [any_spec()] *...]
    ppermute x49, waiting for transfers between devices: 68 us -> 74.2 us  [swap(): lax.ppermute(value, axis, [(i, i ^ stride) for i in range(self.size[axis])])]
    unnamed x58 -> x51, local copies, waits for them, and re-layouts: 8.55 us -> 8.72 us
  transfers between devices with their start and end apart: 49 -> 49, of which waited for: 24 -> 23; matrix products, arithmetic and copies ran while one was open for 14% -> 15% of each run, Pallas kernels for 16% -> 18%
where the time goes in v3:
time: 343 us; the launch traced here: 337 us
  Pallas kernels  141 us (41%)
  waiting for transfers between devices  74.2 us (22%)
  starting transfers between devices  48.2 us (14%)
  other arithmetic  42.7 us (12%)
  local copies, waits for them, and re-layouts  28.1 us (8%)
    ppermute x49, waiting for transfers between devices, swap(): lax.ppermute(value, axis, [(i, i ^ stride) for i in range(self.size[axis])])  74.2 us
    pallas_call x1, Pallas kernels, mid(): pl.pallas_call(mid_kernel, in_specs=[smem] + [whole] * 5 + [any_spec()] *...  70.5 us
    ppermute x49, starting transfers between devices, swap(): lax.ppermute(value, axis, [(i, i ^ stride) for i in range(self.size[axis])])  48.2 us
    pallas_call x1, Pallas kernels, attn_bwd(): pl.pallas_call(kept(n, attn_bwd_kernel), grid_spec=pltpu.PrefetchScalarGr...  21.1 us
    pallas_call x1, Pallas kernels, attn_fwd(): pl.pallas_call(kept(n, attn_fwd_kernel), grid_spec=pltpu.PrefetchScalarGr...  18.1 us
    convert_element_type x20, other arithmetic, add(): return (mine.astype(F32) + got.astype(F32)).astype(mine.dtype)  14.6 us
    concatenate x20, other arithmetic, join(): jnp.concatenate([jnp.where(low, value, got), jnp.where(low, got, value)],...  12.4 us
    pallas_call x1, Pallas kernels, wgrad_attn(): pl.pallas_call(wgrad_attn_kernel, grid_spec=pltpu.PrefetchScalarGridSpec(...  11.2 us
  transfers between devices with their start and end apart: 49, of which 23 were waited for; matrix products, arithmetic and copies ran while one was open for 15% of the time, Pallas kernels for 18%

profile of v3, /device:TPU:0, one launch (start us, length us, event | category | flops | bytes accessed | tf_op | source)
XLA Modules:
  0.0 337.3 jit_solution(2275893154486825508)
XLA Ops:
  3.1 4.1 %collective-permute-start.8 = (bf16[1,1,1,1,1,24,1664]{6,5,4,3,2,1,0:T(8,128)(2,1)S(1)}, bf16[1,1,1,1,1,24,1664]{6,5,4,3,2,1,0:T(8,128)(2,1)S(1)}, u32[]{:S(2)}, u32[]{:S(2)}) collective-permute-start(bf16[1,1,1,1,1,24,1664]{6,5,4,3,2,1,0:T(8,128)(2,1)S(1)} %maximum_bitcast_fusion), channel_id=1, source_target_pairs={{0,16},{2,18},{4,20},{6,22},{8,24},{10,26},{12,28},{14,30},{16,0},... | collective-permute-start | bytes 239624 | tf_op jit(solution)/shard_map/ppermute | solution.py:703
  10.6 4.7 %collective-permute-done = bf16[1,1,1,1,1,24,1536]{6,5,4,3,2,1,0:T(8,128)(2,1)S(1)} collective-permute-done((bf16[1,1,1,1,1,24,1536]{6,5,4,3,2,1,0:T(8,128)(2,1)S(1)}, bf16[1,1,1,1,1,24,1536]{6,5,4,3,2,1,0:T(8,128)(2,1)S(1)}, u32[]{:S(2)}, u32[]{:S(2)}) %collective-permute-start) | collective-permute-done | bytes 73760 | tf_op jit(solution)/shard_map/ppermute | solution.py:703
  17.6 3.2 collective-permute-done.1
  22.5 2.5 collective-permute-start.5
  28.0 6.6 %collective-permute-done.5 = bf16[1,1,1,1,1,24,3072]{6,5,4,3,2,1,0:T(8,128)(2,1)S(1)} collective-permute-done((bf16[1,1,1,1,1,24,3072]{6,5,4,3,2,1,0:T(8,128)(2,1)S(1)}, bf16[1,1,1,1,1,24,3072]{6,5,4,3,2,1,0:T(8,128)(2,1)S(1)}, u32[]{:S(2)}, u32[]{:S(2)}) %collective-permute-start.5) | collective-permute-done | bytes 147488 | tf_op jit(solution)/shard_map/ppermute | solution.py:703
  40.4 4.4 %collective-permute-done.6 = bf16[2,1,1,1,1,24,3072]{6,5,4,3,2,1,0:T(8,128)(2,1)S(1)} collective-permute-done((bf16[2,1,1,1,1,24,3072]{6,5,4,3,2,1,0:T(8,128)(2,1)S(1)}, bf16[2,1,1,1,1,24,3072]{6,5,4,3,2,1,0:T(8,128)(2,1)S(1)}, u32[]{:S(2)}, u32[]{:S(2)}) %collective-permute-start.6) | collective-permute-done | bytes 294944 | tf_op jit(solution)/shard_map/ppermute | solution.py:703
  44.8 3.9 %collective-permute-done.14 = bf16[2,1,1,1,1,96,768]{6,5,4,3,2,1,0:T(8,128)(2,1)S(1)} collective-permute-done((bf16[2,1,1,1,1,96,768]{6,5,4,3,2,1,0:T(8,128)(2,1)S(1)}, bf16[2,1,1,1,1,96,768]{6,5,4,3,2,1,0:T(8,128)(2,1)S(1)}, u32[]{:S(2)}, u32[]{:S(2)}) %collective-permute-start.14) | collective-permute-done | bytes 294944 | tf_op jit(solution)/shard_map/ppermute | solution.py:703
  48.9 2.6 collective-permute-done.3
  54.9 12.5 %collective-permute-done.7 = bf16[2,2,1,1,1,24,3072]{6,5,4,3,2,1,0:T(8,128)(2,1)S(1)} collective-permute-done((bf16[2,2,1,1,1,24,3072]{6,5,4,3,2,1,0:T(8,128)(2,1)S(1)}, bf16[2,2,1,1,1,24,3072]{6,5,4,3,2,1,0:T(8,128)(2,1)S(1)}, u32[]{:S(2)}, u32[]{:S(2)}) %collective-permute-start.7) | collective-permute-done | bytes 589856 | tf_op jit(solution)/shard_map/ppermute | solution.py:703
  80.0 18.1 %attn_fwd.1 = (bf16[1056,768]{1,0:T(8,128)(2,1)}, bf16[528,768]{1,0:T(8,128)(2,1)}, bf16[528,768]{1,0:T(8,128)(2,1)}, bf16[528,768]{1,0:T(8,128)(2,1)}, bf16[105...) custom-call(s32[1]{0:T(128)} %bitcast.95, ...), custom_call_target="tpu_custom_call" | custom-call | flops 6643777536 | bytes 20000000 | tf_op jit(solution)/shard_map/attn_fwd/pallas_call | solution.py:175
  112.5 2.6 pad_maximum_fusion
  117.1 2.6 pad_maximum_fusion.1
  119.7 70.5 %mid.1 = (bf16[1024,768]{1,0:T(8,128)(2,1)}, bf16[1056,768]{1,0:T(8,128)(2,1)}, bf16[1056,768]{1,0:T(8,128)(2,1)}, bf16[1056,768]{1,0:T(8,128)(2,1)}, bf16[1056,...) custom-call(s32[3]{0:T(128)} %pad_add_fusion.info_ref, ...), custom_call_target="tpu_custom_call", output_to_operand_aliasing={{1}: (12, {}), {2}: (13, {})} | custom-call | flops 39447429120 | bytes 60000000 | tf_op jit(solution)/shard_map/mid/pallas_call | solution.py:566
  190.3 10.1 %wgrad_outer.1 = (bf16[3072,384]{1,0:T(8,128)(2,1)}, bf16[3072,384]{1,0:T(8,128)(2,1)}) custom-call(s32[1]{0:T(128)} %bitcast.11.core_ref, bf16[1056,3072]{1,0:T(8,128)(2,1)} %get-tuple-element.106.g_ref, bf16[1056,768]{1,0:T(8,128)(2,1)} %get-tuple-element.107.d_ref), custom_call_target="tpu_custom_call" | custom-call | flops 9965666304 | bytes 15000000 | tf_op jit(solution)/shard_map/wgrad_outer/pallas_call | solution.py:636
  200.4 10.3 %wgrad_inner.1 = (bf16[768,1536]{1,0:T(8,128)(2,1)}, bf16[768,1536]{1,0:T(8,128)(2,1)}) custom-call(s32[1]{0:T(128)} %bitcast.11.core_ref, bf16[1056,768]{1,0:T(8,128)(2,1)} %get-tuple-element.110.h_ref, bf16[1056,3072]{1,0:T(8,128)(2,1)} %get-tuple-element.111.da_ref.db_ref, bf16[1056,3072]{1,0:T(8,128)(2,1)} %get-tuple-element.111.da_ref.db_ref), custom_call_target="tpu_custom_call" | custom-call | flops 9965666304 | bytes 15000000 | tf_op jit(solution)/shard_map/wgrad_inner/pallas_call | solution.py:607
  211.9 3.0 add_convert_fusion
  222.2 21.1 %attn_bwd.1 = (bf16[1056,768]{1,0:T(8,128)(2,1)}, bf16[1056,768]{1,0:T(8,128)(2,1)}, bf16[1056,768]{1,0:T(8,128)(2,1)}, f32[1,768]{1,0:T(1,128)}, f32[1,768]{1,0...) custom-call(s32[1]{0:T(128)} %bitcast.96, ...), custom_call_target="tpu_custom_call", output_to_operand_aliasing={{0}: (1, {}), {1}: (2, {}), {2}: (3, {}), {5}: (4, {})} | custom-call | flops 12872318976 | bytes 20000000 | tf_op jit(solution)/shard_map/attn_bwd/pallas_call | solution.py:273
  253.3 11.2 %wgrad_attn.1 = (bf16[768,768]{1,0:T(8,128)(2,1)}, bf16[768,768]{1,0:T(8,128)(2,1)}, bf16[768,768]{1,0:T(8,128)(2,1)}, bf16[768,768]{1,0:T(8,128)(2,1)}) custom-call(s32[1]{0:T(128)} %bitcast.11.core_ref, bf16[1056,768]{1,0:T(8,128)(2,1)} %get-tuple-element.129.hb_ref, bf16[1056,768]{1,0:T(8,128)(2,1)} %get-tuple-element.119.refs_14_.o_ref, ...), custom_call_target="tpu_custom_call" | custom-call | flops 9965666304 | bytes 15000000 | tf_op jit(solution)/shard_map/wgrad_attn/pallas_call | solution.py:668
  280.7 5.9 %collective-permute-done.30 = bf16[2,1,1,2,1,24,1536]{6,5,4,3,2,1,0:T(8,128)(2,1)S(1)} collective-permute-done((bf16[2,1,1,2,1,24,1536]{6,5,4,3,2,1,0:T(8,128)(2,1)}, bf16[2,1,1,2,1,24,1536]{6,5,4,3,2,1,0:T(8,128)(2,1)S(1)}, u32[]{:S(2)}, u32[]{:S(2)}) %collective-permute-start.30) | collective-permute-done | bytes 294944 | tf_op jit(solution)/shard_map/ppermute | solution.py:703
  286.6 4.4 %collective-permute-done.31 = bf16[2,1,1,2,1,96,384]{6,5,4,3,2,1,0:T(8,128)(2,1)S(1)} collective-permute-done((bf16[2,1,1,2,1,96,384]{6,5,4,3,2,1,0:T(8,128)(2,1)}, bf16[2,1,1,2,1,96,384]{6,5,4,3,2,1,0:T(8,128)(2,1)S(1)}, u32[]{:S(2)}, u32[]{:S(2)}) %collective-permute-start.31) | collective-permute-done | bytes 294944 | tf_op jit(solution)/shard_map/ppermute | solution.py:703
  298.2 3.4 %collective-permute-start.43 = (bf16[1,1,1,2,1,24,1536]{6,5,4,3,2,1,0:T(8,128)(2,1)S(1)}, bf16[1,1,1,2,1,24,1536]{6,5,4,3,2,1,0:T(8,128)(2,1)S(1)}, u32[]{:S(2)}, u32[]{:S(2)}) collective-permute-start(bf16[1,1,1,2,1,24,1536]{6,5,4,3,2,1,0:T(8,128)(2,1)S(1)} %constant_dynamic-slice_fusion.8), channel_id=1, source_target_pairs={{0,16},{2,18},{4,20},{6,22},{8,24},{10,26},{12,28},{14,30},{16,0},... | collective-permute-start | bytes 442376 | tf_op jit(solution)/shard_map/ppermute | solution.py:703
  301.9 8.7 %collective-permute-done.43 = bf16[1,1,1,2,1,24,1536]{6,5,4,3,2,1,0:T(8,128)(2,1)S(1)} collective-permute-done((bf16[1,1,1,2,1,24,1536]{6,5,4,3,2,1,0:T(8,128)(2,1)S(1)}, bf16[1,1,1,2,1,24,1536]{6,5,4,3,2,1,0:T(8,128)(2,1)S(1)}, u32[]{:S(2)}, u32[]{:S(2)}) %collective-permute-start.43) | collective-permute-done | bytes 147488 | tf_op jit(solution)/shard_map/ppermute | solution.py:703
  321.1 2.4 collective-permute-done.37
  323.9 3.0 collective-permute-start.41
  (260 shorter events, 112.5 us)
Async XLA Ops:
  3.1 12.9 %collective-permute-start.8 = (bf16[1,1,1,1,1,24,1664]{6,5,4,3,2,1,0:T(8,128)(2,1)S(1)}, bf16[1,1,1,1,1,24,1664]{6,5,4,3,2,1,0:T(8,128)(2,1)S(1)}, u32[]{:S(2)}, u32[]{:S(2)}) collective-permute-start(bf16[1,1,1,1,1,24,1664]{6,5,4,3,2,1,0:T(8,128)(2,1)S(1)} %maximum_bitcast_fusion), channel_id=1, source_target_pairs={{0,16},{2,18},{4,20},{6,22},{8,24},{10,26},{12,28},{14,30},{16,0},... | collective-permute-start | bytes 239624 | tf_op jit(solution)/shard_map/ppermute | solution.py:703
  20.9 16.6 %collective-permute-start.2 = (bf16[2,2,1,1,1,24,1536]{6,5,4,3,2,1,0:T(8,128)(2,1)S(1)}, bf16[2,2,1,1,1,24,1536]{6,5,4,3,2,1,0:T(8,128)(2,1)S(1)}, u32[]{:S(2)}, u32[]{:S(2)}) collective-permute-start(bf16[2,2,1,1,1,24,1536]{6,5,4,3,2,1,0:T(8,128)(2,1)S(1)} %pad_maximum_fusion.15), channel_id=1, source_target_pairs={{0,4},{2,6},{4,0},{6,2},{8,12},{10,14},{12,8},{14,10},{16,20},{18,... | collective-permute-start | bytes 884744 | tf_op jit(solution)/shard_map/ppermute | solution.py:703
  22.5 12.1 %collective-permute-start.5 = (bf16[1,1,1,1,1,24,3072]{6,5,4,3,2,1,0:T(8,128)(2,1)S(1)}, bf16[1,1,1,1,1,24,3072]{6,5,4,3,2,1,0:T(8,128)(2,1)S(1)}, u32[]{:S(2)}, u32[]{:S(2)}) collective-permute-start(bf16[1,1,1,1,1,24,3072]{6,5,4,3,2,1,0:T(8,128)(2,1)S(1)} %reshape_reshape.6), channel_id=1, source_target_pairs={{0,16},{2,18},{4,20},{6,22},{8,24},{10,26},{12,28},{14,30},{16,0},... | collective-permute-start | bytes 442376 | tf_op jit(solution)/shard_map/ppermute | solution.py:703
  25.1 14.1 %collective-permute-start.10 = (bf16[2,2,1,1,1,24,1664]{6,5,4,3,2,1,0:T(8,128)(2,1)S(1)}, bf16[2,2,1,1,1,24,1664]{6,5,4,3,2,1,0:T(8,128)(2,1)S(1)}, u32[]{:S(2)}, u32[]{:S(2)}) collective-permute-start(bf16[2,2,1,1,1,24,1664]{6,5,4,3,2,1,0:T(8,128)(2,1)S(1)} %pad_maximum_fusion.14), channel_id=1, source_target_pairs={{0,1},{1,0},{2,3},{3,2},{4,5},{5,4},{6,7},{7,6},{8,9},{9,8},{10,11... | collective-permute-start | bytes 958472 | tf_op jit(solution)/shard_map/ppermute | solution.py:703
  36.9 11.9 %collective-permute-start.14 = (bf16[2,1,1,1,1,96,768]{6,5,4,3,2,1,0:T(8,128)(2,1)S(1)}, bf16[2,1,1,1,1,96,768]{6,5,4,3,2,1,0:T(8,128)(2,1)S(1)}, u32[]{:S(2)}, u32[]{:S(2)}) collective-permute-start(bf16[2,1,1,1,1,96,768]{6,5,4,3,2,1,0:T(8,128)(2,1)S(1)} %pad_maximum_fusion.17), channel_id=1, source_target_pairs={{0,8},{2,10},{4,12},{6,14},{8,0},{10,2},{12,4},{14,6},{16,24},{18,... | collective-permute-start | bytes 884744 | tf_op jit(solution)/shard_map/ppermute | solution.py:703
  37.6 13.8 %collective-permute-start.3 = (bf16[2,2,2,1,1,24,1536]{6,5,4,3,2,1,0:T(8,128)(2,1)S(1)}, bf16[2,2,2,1,1,24,1536]{6,5,4,3,2,1,0:T(8,128)(2,1)S(1)}, u32[]{:S(2)}, u32[]{:S(2)}) collective-permute-start(bf16[2,2,2,1,1,24,1536]{6,5,4,3,2,1,0:T(8,128)(2,1)S(1)} %pad_maximum_fusion.11), channel_id=1, source_target_pairs={{0,1},{1,0},{2,3},{3,2},{4,5},{5,4},{6,7},{7,6},{8,9},{9,8},{10,11... | collective-permute-start | bytes 1769480 | tf_op jit(solution)/shard_map/ppermute | solution.py:703
  39.3 14.8 %collective-permute-start.11 = (bf16[2,2,1,1,2,24,1664]{6,5,4,3,2,1,0:T(8,128)(2,1)S(1)}, bf16[2,2,1,1,2,24,1664]{6,5,4,3,2,1,0:T(8,128)(2,1)S(1)}, u32[]{:S(2)}, u32[]{:S(2)}) collective-permute-start(bf16[2,2,1,1,2,24,1664]{6,5,4,3,2,1,0:T(8,128)(2,1)S(1)} %pad_maximum_fusion.10), channel_id=1, source_target_pairs={{0,4},{2,6},{4,0},{6,2},{8,12},{10,14},{12,8},{14,10},{16,20},{18,... | collective-permute-start | bytes 1916936 | tf_op jit(solution)/shard_map/ppermute | solution.py:703
  51.6 21.3 %collective-permute-start.4 = (bf16[2,2,2,1,2,24,1536]{6,5,4,3,2,1,0:T(8,128)(2,1)S(1)}, bf16[2,2,2,1,2,24,1536]{6,5,4,3,2,1,0:T(8,128)(2,1)S(1)}, u32[]{:S(2)}, u32[]{:S(2)}) collective-permute-start(bf16[2,2,2,1,2,24,1536]{6,5,4,3,2,1,0:T(8,128)(2,1)S(1)} %pad_maximum_fusion.7), channel_id=1, source_target_pairs={{0,2},{2,0},{4,6},{6,4},{8,10},{10,8},{12,14},{14,12},{16,18},{18,... | collective-permute-start | bytes 3538952 | tf_op jit(solution)/shard_map/ppermute | solution.py:703
  51.7 15.7 %collective-permute-start.7 = (bf16[2,2,1,1,1,24,3072]{6,5,4,3,2,1,0:T(8,128)(2,1)S(1)}, bf16[2,2,1,1,1,24,3072]{6,5,4,3,2,1,0:T(8,128)(2,1)S(1)}, u32[]{:S(2)}, u32[]{:S(2)}) collective-permute-start(bf16[2,2,1,1,1,24,3072]{6,5,4,3,2,1,0:T(8,128)(2,1)S(1)} %pad_maximum_fusion.12), channel_id=1, source_target_pairs={{0,4},{2,6},{4,0},{6,2},{8,12},{10,14},{12,8},{14,10},{16,20},{18,... | collective-permute-start | bytes 1769480 | tf_op jit(solution)/shard_map/ppermute | solution.py:703
  54.5 20.2 %collective-permute-start.12 = (bf16[2,2,2,1,2,24,1664]{6,5,4,3,2,1,0:T(8,128)(2,1)S(1)}, bf16[2,2,2,1,2,24,1664]{6,5,4,3,2,1,0:T(8,128)(2,1)S(1)}, u32[]{:S(2)}, u32[]{:S(2)}) collective-permute-start(bf16[2,2,2,1,2,24,1664]{6,5,4,3,2,1,0:T(8,128)(2,1)S(1)} %pad_maximum_fusion.6), channel_id=1, source_target_pairs={{0,2},{2,0},{4,6},{6,4},{8,10},{10,8},{12,14},{14,12},{16,18},{18,... | collective-permute-start | bytes 3833864 | tf_op jit(solution)/shard_map/ppermute | solution.py:703
  54.5 16.0 %collective-permute-start.15 = (bf16[2,2,1,1,1,96,768]{6,5,4,3,2,1,0:T(8,128)(2,1)S(1)}, bf16[2,2,1,1,1,96,768]{6,5,4,3,2,1,0:T(8,128)(2,1)S(1)}, u32[]{:S(2)}, u32[]{:S(2)}) collective-permute-start(bf16[2,2,1,1,1,96,768]{6,5,4,3,2,1,0:T(8,128)(2,1)S(1)} %pad_maximum_fusion.13), channel_id=1, source_target_pairs={{0,1},{1,0},{2,3},{3,2},{4,5},{5,4},{6,7},{7,6},{8,9},{9,8},{10,11... | collective-permute-start | bytes 1769480 | tf_op jit(solution)/shard_map/ppermute | solution.py:703
  67.7 30.4 %collective-permute-start.16 = (bf16[2,2,2,1,1,24,3072]{6,5,4,3,2,1,0:T(8,128)(2,1)S(1)}, bf16[2,2,2,1,1,24,3072]{6,5,4,3,2,1,0:T(8,128)(2,1)S(1)}, u32[]{:S(2)}, u32[]{:S(2)}) collective-permute-start(bf16[2,2,2,1,1,24,3072]{6,5,4,3,2,1,0:T(8,128)(2,1)S(1)} %pad_maximum_fusion.8), channel_id=1, source_target_pairs={{0,1},{1,0},{2,3},{3,2},{4,5},{5,4},{6,7},{7,6},{8,9},{9,8},{10,11... | collective-permute-start | bytes 3538952 | tf_op jit(solution)/shard_map/ppermute | solution.py:703
  72.6 29.6 %collective-permute-start.18 = (bf16[2,2,1,1,2,96,768]{6,5,4,3,2,1,0:T(8,128)(2,1)}, bf16[2,2,1,1,2,96,768]{6,5,4,3,2,1,0:T(8,128)(2,1)}, u32[]{:S(2)}, u32[]{:S(2)}) collective-permute-start(bf16[2,2,1,1,2,96,768]{6,5,4,3,2,1,0:T(8,128)(2,1)} %pad_maximum_fusion.9), channel_id=1, source_target_pairs={{0,4},{2,6},{4,0},{6,2},{8,12},{10,14},{12,8},{14,10},{16,20},{18,... | collective-permute-start | bytes 3538952 | tf_op jit(solution)/shard_map/ppermute | solution.py:703
  215.1 31.1 %collective-permute-start.23 = (bf16[2,2,1,2,2,96,384]{6,5,4,3,2,1,0:T(8,128)(2,1)S(1)}, bf16[2,2,1,2,2,96,384]{6,5,4,3,2,1,0:T(8,128)(2,1)}, u32[]{:S(2)}, u32[]{:S(2)}) collective-permute-start(bf16[2,2,1,2,2,96,384]{6,5,4,3,2,1,0:T(8,128)(2,1)S(1)} %constant_dynamic-slice_fusion.27), channel_id=1, source_target_pairs={{0,4},{2,6},{4,0},{6,2},{8,12},{10,14},{12,8},{14,10},{16,20},{18,... | collective-permute-start | bytes 3538952 | tf_op jit(solution)/shard_map/ppermute | solution.py:703
  221.6 28.0 %collective-permute-start.22 = (bf16[2,2,2,2,1,24,1536]{6,5,4,3,2,1,0:T(8,128)(2,1)}, bf16[2,2,2,2,1,24,1536]{6,5,4,3,2,1,0:T(8,128)(2,1)}, u32[]{:S(2)}, u32[]{:S(2)}) collective-permute-start(bf16[2,2,2,2,1,24,1536]{6,5,4,3,2,1,0:T(8,128)(2,1)} %constant_dynamic-slice_fusion.28), channel_id=1, source_target_pairs={{0,1},{1,0},{2,3},{3,2},{4,5},{5,4},{6,7},{7,6},{8,9},{9,8},{10,11... | collective-permute-start | bytes 3538952 | tf_op jit(solution)/shard_map/ppermute | solution.py:703
  251.3 14.5 %collective-permute-start.27 = (bf16[2,2,1,2,1,96,384]{6,5,4,3,2,1,0:T(8,128)(2,1)S(1)}, bf16[2,2,1,2,1,96,384]{6,5,4,3,2,1,0:T(8,128)(2,1)}, u32[]{:S(2)}, u32[]{:S(2)}) collective-permute-start(bf16[2,2,1,2,1,96,384]{6,5,4,3,2,1,0:T(8,128)(2,1)S(1)} %constant_dynamic-slice_fusion.25), channel_id=1, source_target_pairs={{0,1},{1,0},{2,3},{3,2},{4,5},{5,4},{6,7},{7,6},{8,9},{9,8},{10,11... | collective-permute-start | bytes 1769480 | tf_op jit(solution)/shard_map/ppermute | solution.py:703
  252.1 15.6 %collective-permute-start.26 = (bf16[2,2,1,2,1,24,1536]{6,5,4,3,2,1,0:T(8,128)(2,1)S(1)}, bf16[2,2,1,2,1,24,1536]{6,5,4,3,2,1,0:T(8,128)(2,1)}, u32[]{:S(2)}, u32[]{:S(2)}) collective-permute-start(bf16[2,2,1,2,1,24,1536]{6,5,4,3,2,1,0:T(8,128)(2,1)S(1)} %constant_dynamic-slice_fusion.26), channel_id=1, source_target_pairs={{0,4},{2,6},{4,0},{6,2},{8,12},{10,14},{12,8},{14,10},{16,20},{18,... | collective-permute-start | bytes 1769480 | tf_op jit(solution)/shard_map/ppermute | solution.py:703
  272.6 18.5 %collective-permute-start.28 = (bf16[2,2,2,2,1,24,768]{6,5,4,3,2,1,0:T(8,128)(2,1)}, bf16[2,2,2,2,1,24,768]{6,5,4,3,2,1,0:T(8,128)(2,1)}, u32[]{:S(2)}, u32[]{:S(2)}) collective-permute-start(bf16[2,2,2,2,1,24,768]{6,5,4,3,2,1,0:T(8,128)(2,1)} %constant_dynamic-slice_fusion.24), channel_id=1, source_target_pairs={{0,1},{1,0},{2,3},{3,2},{4,5},{5,4},{6,7},{7,6},{8,9},{9,8},{10,11... | collective-permute-start | bytes 1769480 | tf_op jit(solution)/shard_map/ppermute | solution.py:703
  274.3 16.7 %collective-permute-start.29 = (bf16[2,2,1,2,2,24,768]{6,5,4,3,2,1,0:T(8,128)(2,1)S(1)}, bf16[2,2,1,2,2,24,768]{6,5,4,3,2,1,0:T(8,128)(2,1)}, u32[]{:S(2)}, u32[]{:S(2)}) collective-permute-start(bf16[2,2,1,2,2,24,768]{6,5,4,3,2,1,0:T(8,128)(2,1)S(1)} %constant_dynamic-slice_fusion.23), channel_id=1, source_target_pairs={{0,4},{2,6},{4,0},{6,2},{8,12},{10,14},{12,8},{14,10},{16,20},{18,... | collective-permute-start | bytes 1769480 | tf_op jit(solution)/shard_map/ppermute | solution.py:703
  277.8 13.2 %collective-permute-start.31 = (bf16[2,1,1,2,1,96,384]{6,5,4,3,2,1,0:T(8,128)(2,1)}, bf16[2,1,1,2,1,96,384]{6,5,4,3,2,1,0:T(8,128)(2,1)S(1)}, u32[]{:S(2)}, u32[]{:S(2)}) collective-permute-start(bf16[2,1,1,2,1,96,384]{6,5,4,3,2,1,0:T(8,128)(2,1)} %constant_dynamic-slice_fusion.21), channel_id=1, source_target_pairs={{0,8},{2,10},{4,12},{6,14},{8,0},{10,2},{12,4},{14,6},{16,24},{18,... | collective-permute-start | bytes 884744 | tf_op jit(solution)/shard_map/ppermute | solution.py:703
  294.3 19.7 %collective-permute-start.33 = (bf16[2,2,1,2,1,24,768]{6,5,4,3,2,1,0:T(8,128)(2,1)S(1)}, bf16[2,2,1,2,1,24,768]{6,5,4,3,2,1,0:T(8,128)(2,1)S(1)}, u32[]{:S(2)}, u32[]{:S(2)}) collective-permute-start(bf16[2,2,1,2,1,24,768]{6,5,4,3,2,1,0:T(8,128)(2,1)S(1)} %constant_dynamic-slice_fusion.19), channel_id=1, source_target_pairs={{0,4},{2,6},{4,0},{6,2},{8,12},{10,14},{12,8},{14,10},{16,20},{18,... | collective-permute-start | bytes 884744 | tf_op jit(solution)/shard_map/ppermute | solution.py:703
  296.1 18.0 %collective-permute-start.34 = (bf16[2,2,1,2,1,24,768]{6,5,4,3,2,1,0:T(8,128)(2,1)S(1)}, bf16[2,2,1,2,1,24,768]{6,5,4,3,2,1,0:T(8,128)(2,1)S(1)}, u32[]{:S(2)}, u32[]{:S(2)}) collective-permute-start(bf16[2,2,1,2,1,24,768]{6,5,4,3,2,1,0:T(8,128)(2,1)S(1)} %constant_dynamic-slice_fusion.18), channel_id=1, source_target_pairs={{0,1},{1,0},{2,3},{3,2},{4,5},{5,4},{6,7},{7,6},{8,9},{9,8},{10,11... | collective-permute-start | bytes 884744 | tf_op jit(solution)/shard_map/ppermute | solution.py:703
  296.4 17.7 %collective-permute-start.35 = (f32[2,2,2,1,1,1,288]{6,4,3,2,1,0,5:T(1,128)S(1)}, f32[2,2,2,1,1,1,288]{6,4,3,2,1,0,5:T(1,128)S(1)}, u32[]{:S(2)}, u32[]{:S(2)}) collective-permute-start(f32[2,2,2,1,1,1,288]{6,4,3,2,1,0,5:T(1,128)S(1)} %constant_dynamic-slice_fusion.17), channel_id=1, source_target_pairs={{0,1},{1,0},{2,3},{3,2},{4,5},{5,4},{6,7},{7,6},{8,9},{9,8},{10,11... | collective-permute-start | bytes 27656 | tf_op jit(solution)/shard_map/ppermute | solution.py:703
  298.2 12.4 %collective-permute-start.43 = (bf16[1,1,1,2,1,24,1536]{6,5,4,3,2,1,0:T(8,128)(2,1)S(1)}, bf16[1,1,1,2,1,24,1536]{6,5,4,3,2,1,0:T(8,128)(2,1)S(1)}, u32[]{:S(2)}, u32[]{:S(2)}) collective-permute-start(bf16[1,1,1,2,1,24,1536]{6,5,4,3,2,1,0:T(8,128)(2,1)S(1)} %constant_dynamic-slice_fusion.8), channel_id=1, source_target_pairs={{0,16},{2,18},{4,20},{6,22},{8,24},{10,26},{12,28},{14,30},{16,0},... | collective-permute-start | bytes 442376 | tf_op jit(solution)/shard_map/ppermute | solution.py:703
  (48 other events, 280.7 us)
